TPU v7x, 256 devices: a whole 4x4x8 slice. The times are simulated.
256 devices in a mesh: section: 2 (over core), dp: 32 (over z, x), mp: 4 (over y).
Axes of the slice: x: 4, y: 4, z: 8, core: 2. Of those that a mesh axis runs over, the one named last changes fastest.
Arguments:
- features: bfloat16 [32768, 4096], P(('section', 'dp'), 'mp'), may hold values from -16 to 16
- w_in: bfloat16 [4096, 2048], P(('section', 'dp'), 'mp'), may hold values from -0.09375 to 0.09375
- w_out: bfloat16 [512, 2048], P(('section', 'dp'), 'mp'), may hold values from -0.125 to 0.125
- codebook: bfloat16 [3, 65536, 512], P(None, ('section', 'dp'), 'mp'), may hold values from -3 to 3
- codes: int32 [3, 32768], P(None, ('section', 'dp')), may hold values from 0 to 65535, as said below
- decoder_grad: bfloat16 [32768, 512], P(('section', 'dp'), 'mp'), may hold values from -16 to 16
Outputs:
- in_grad: float32 [4096, 2048], P(('section', 'dp'), 'mp')
- out_grad: float32 [512, 2048], P(('section', 'dp'), 'mp')
- code_sums: float32 [3, 65536, 512], P(None, ('section', 'dp'), 'mp')
Inputs may be any that keep to these rules, and one draw needn't show every extreme that they name: Row k of a level's codebook belongs to owner k // 1024. Within the 512 items of one device (aligned blocks of items), at each level at most 16 codes belong to one owner; at each level some owner receives exactly 16 codes from every device's items.
All inputs are finite; a program needn't handle non-finite values.
Results may differ from a plain program's by a relative error of at most 0.0026.
Values may be sent and summed in bfloat16 or wider, within the bound.
No kernel may reach another device: no remote copies, remote signals or barrier semaphores. Data moves between devices by JAX's collectives and lax.ppermute only.
A program may use at most 64 MiB of HBM per device.

v0:
```python
import jax
import jax.numpy as jnp
from jax import lax
from jax.experimental import pallas as pl
from jax.experimental.pallas import tpu as pltpu
from jax.sharding import Mesh, PartitionSpec as P

BETA = 0.25
BF = jnp.bfloat16
F32 = jnp.float32
I32 = jnp.int32
OWN = ("s", "z", "x")
VMEM = pl.BlockSpec(memory_space=pltpu.VMEM)
SMEM = pl.BlockSpec(memory_space=pltpu.SMEM)


def shift(value, axis, by):
    size = lax.axis_size(axis)
    return lax.ppermute(value, axis, [(i, (i + by) % size) for i in range(size)])


def exchange(value, axis):
    return lax.all_to_all(value, axis, split_axis=0, concat_axis=0, tiled=True)


def mm(a, b, dims=((1,), (0,))):
    return lax.dot_general(a, b, (dims, ((), ())), preferred_element_type=F32)


def encode(feats, near, other, place, in_rows, out_rows):
    items, depth = feats[0].shape
    nz, _, hid = near[0].shape
    nx = len(near)
    ny = len(feats)
    hz = nz * 2 // ny
    width = hz * nx * out_rows
    tile = items // 2

    def kernel(place_ref, *refs):
        f_refs, refs = refs[:ny], refs[ny:]
        n_refs, refs = refs[:nx], refs[nx:]
        o_refs, refs = refs[:nx], refs[nx:]
        hid_ref, slope_ref, wo_ref = refs[:3]
        lat_refs, (w_ref, wo32_ref) = refs[3:3 + ny], refs[3 + ny:]
        for k in range(nx):
            xk = place_ref[k]
            for r, ref in enumerate((n_refs[k], o_refs[k])):
                for zh in range(ny // 2):
                    p = r * (ny // 2) + zh
                    cut = ref[zh * hz:(zh + 1) * hz]
                    w_ref[p, :, xk] = cut[:, :in_rows]
                    wo32_ref[p, :, xk] = cut[:, in_rows:].astype(F32)
        for p in range(ny):
            wo_ref[p] = wo32_ref[p].reshape(width, hid).astype(BF)

        def step(t, carry):
            rows = pl.ds(t * tile, tile)
            acc = None
            for k in range(ny):
                part = mm(f_refs[k][rows, :], w_ref[place_ref[nx + k]].reshape(depth, hid))
                acc = part if acc is None else acc + part
            logistic = jax.nn.sigmoid(acc)
            hidden = (acc * logistic).astype(BF)
            hid_ref[rows, :] = hidden
            slope_ref[rows, :] = logistic * (1.0 + acc * (1.0 - logistic))
            for j in range(ny):
                lat_refs[j][rows, :] = mm(hidden, wo_ref[place_ref[nx + ny + j]], ((1,), (1,)))
            return carry

        lax.fori_loop(0, items // tile, step, 0)

    return pl.pallas_call(
        kernel,
        out_shape=[
            jax.ShapeDtypeStruct((items, hid), BF),
            jax.ShapeDtypeStruct((items, hid), F32),
            jax.ShapeDtypeStruct((ny, width, hid), BF),
        ] + [jax.ShapeDtypeStruct((items, width), F32)] * ny,
        in_specs=[SMEM] + [VMEM] * (ny + 2 * nx),
        out_specs=[VMEM] * (3 + ny),
        scratch_shapes=[
            pltpu.VMEM((ny, hz, nx, in_rows, hid), BF),
            pltpu.VMEM((ny, hz, nx, out_rows, hid), F32),
        ],
        compiler_params=pltpu.CompilerParams(vmem_limit_bytes=48 * 1024 * 1024),
        cost_estimate=pl.CostEstimate(
            flops=2 * items * hid * ny * (depth + width), bytes_accessed=12 << 20, transcendentals=items * hid),
        name="encode",
    )(place, *feats, *near, *other)


def ask(codes, w_in, w_out, nz, nx, ns, rows_own, cap):
    levels, items = codes.shape
    in_rows, hid = w_in.shape
    out_rows = w_out.shape[0]
    owners = ns * nz * nx
    slots = owners * cap
    group = slots // nz
    digit_rows = 8
    lane = 128

    def kernel(codes_ref, wi_ref, wo_ref, slot_ref, pay_ref, col_ref, found_ref):
        fill = jnp.zeros((8 - levels, lane), I32)
        for t in range(items // lane):
            block = jnp.concatenate([codes_ref[:, t * lane:(t + 1) * lane], fill], axis=0).T
            for l in range(levels):
                col_ref[l, t * lane:(t + 1) * lane, :] = block[:, l:l + 1]
        found_ref[...] = jnp.zeros_like(found_ref)

        def level(l, carry):
            code_row, code_col = codes_ref[pl.ds(l, 1), :], col_ref[l]
            own_row, own_col = code_row // rows_own, code_col // rows_own
            first = lax.broadcasted_iota(I32, (items, items), 0)
            second = lax.broadcasted_iota(I32, (items, items), 1)
            before = jnp.where(second < first, jnp.where(own_col == own_row, 1.0, 0.0), 0.0)
            rank = jnp.sum(before, axis=1, keepdims=True).astype(I32)
            slot_ref[l] = own_col * cap + rank
            section, rest = own_col // (nz * nx), own_col % (nz * nx)
            spot = (rest * ns + section) * cap + rank
            value = (code_col % rows_own + 1).astype(F32)
            lanes = lax.broadcasted_iota(I32, (items, slots), 1)
            want = jnp.sum(jnp.where(lanes == spot, value, 0.0), axis=0, keepdims=True).astype(I32)
            found_ref[pl.ds(2 * l, 1), :] = (want // 32).astype(F32)
            found_ref[pl.ds(2 * l + 1, 1), :] = (want % 32).astype(F32)
            return carry

        lax.fori_loop(0, levels, level, 0)
        rest = jnp.zeros((digit_rows, hid - group), F32)
        for z in range(nz):
            pay_ref[z, :in_rows] = wi_ref[...]
            digits = jnp.concatenate([found_ref[:, z * group:(z + 1) * group], rest], axis=1)
            pay_ref[z, in_rows:] = jnp.concatenate([wo_ref[...].astype(F32), digits], axis=0).astype(BF)

    return pl.pallas_call(
        kernel,
        out_shape=[
            jax.ShapeDtypeStruct((levels, items, 1), I32),
            jax.ShapeDtypeStruct((nz, in_rows + out_rows + digit_rows, hid), BF),
        ],
        in_specs=[VMEM] * 3,
        out_specs=[VMEM] * 2,
        scratch_shapes=[pltpu.VMEM((levels, items, 1), I32), pltpu.VMEM((digit_rows, slots), F32)],
        name="ask",
    )(codes, w_in, w_out)


def pick(asked, book, owners):
    levels, lines, lane = asked.shape
    rows_own, width = book.shape[1:]
    slots = lines * lane
    cap = slots // owners
    tile = 256

    def kernel(asked_ref, book_ref, out_ref, col_ref):
        turned = asked_ref[0].T
        for t in range(lines):
            col_ref[t * lane:(t + 1) * lane, :] = turned[:, t:t + 1]

        def step(t, carry):
            col = col_ref[pl.ds(pl.multiple_of(t * tile, tile), tile), :]
            hit = jnp.where(lax.broadcasted_iota(I32, (tile, rows_own), 1) == col, 1.0, 0.0).astype(BF)
            got = mm(hit, book_ref[0]).astype(BF)
            out_ref[pl.ds(t * (tile // cap), tile // cap)] = got.reshape(tile // cap, cap, width)
            return carry

        lax.fori_loop(0, slots // tile, step, 0)

    return pl.pallas_call(
        kernel,
        out_shape=jax.ShapeDtypeStruct((owners, levels * cap, width), BF),
        grid=(levels,),
        in_specs=[
            pl.BlockSpec((1, lines, lane), lambda l: (l, 0, 0)),
            pl.BlockSpec((1, rows_own, width), lambda l: (l, 0, 0)),
        ],
        out_specs=pl.BlockSpec((owners, cap, width), lambda l: (0, l, 0)),
        scratch_shapes=[pltpu.VMEM((slots, 1), I32)],
        name="pick",
    )(asked, book)


def collect(asked, incoming, rows_own):
    levels, lines, lane = asked.shape
    owners, _, width = incoming.shape
    slots = lines * lane
    cap = slots // owners
    tile = 256

    def kernel(asked_ref, in_ref, out_ref):
        line = jnp.concatenate([asked_ref[0, t:t + 1, :] for t in range(lines)], axis=1)
        values = in_ref[...].reshape(slots, width)

        def step(t, carry):
            rows = lax.broadcasted_iota(I32, (tile, slots), 0) + t * tile
            hit = jnp.where(rows == line, 1.0, 0.0).astype(BF)
            out_ref[0, pl.ds(pl.multiple_of(t * tile, tile), tile), :] = mm(hit, values)
            return carry

        lax.fori_loop(0, rows_own // tile, step, 0)

    return pl.pallas_call(
        kernel,
        out_shape=jax.ShapeDtypeStruct((levels, rows_own, width), F32),
        grid=(levels,),
        in_specs=[
            pl.BlockSpec((1, lines, lane), lambda l: (l, 0, 0)),
            pl.BlockSpec((owners, cap, width), lambda l: (0, l, 0)),
        ],
        out_specs=pl.BlockSpec((1, rows_own, width), lambda l: (l, 0, 0)),
        name="collect",
    )(asked, incoming)


def turn(feats, place):
    items, depth = feats[0].shape
    ny = len(feats)
    hy = ny // 2
    cols = 256

    def kernel(place_ref, *refs):
        here_ref, there_ref = refs[ny:]
        for k in range(ny):
            spot = place_ref[k]
            flat = refs[k][...].T

            @pl.when(spot < hy)
            def _():
                here_ref[spot] = flat

            @pl.when(spot >= hy)
            def _():
                there_ref[spot - hy] = flat

    out = pl.BlockSpec((hy, cols, items), lambda i: (0, i, 0))
    return pl.pallas_call(
        kernel,
        out_shape=[jax.ShapeDtypeStruct((hy, depth, items), BF)] * 2,
        grid=(depth // cols,),
        in_specs=[SMEM] + [pl.BlockSpec((items, cols), lambda i: (0, i))] * ny,
        out_specs=[out] * 2,
        cost_estimate=pl.CostEstimate(flops=0, bytes_accessed=8 << 20, transcendentals=0),
        name="turn",
    )(place, *feats)


def back(grads, hidden, slope, w_out, place):
    items, hid = hidden.shape
    ny, width = w_out.shape[:2]

    def kernel(place_ref, *refs):
        g_refs, (hid_ref, slope_ref, wo_ref, pre_ref, out_ref) = refs[:ny], refs[ny:]
        acc = None
        for k in range(ny):
            part = mm(g_refs[k][...], wo_ref[place_ref[k]])
            acc = part if acc is None else acc + part
            out_ref[place_ref[k]] = mm(g_refs[k][...], hid_ref[...], ((0,), (0,)))
        pre_ref[...] = (acc * slope_ref[...]).astype(BF)

    return pl.pallas_call(
        kernel,
        out_shape=[
            jax.ShapeDtypeStruct((items, hid), BF),
            jax.ShapeDtypeStruct((ny, width, hid), F32),
        ],
        in_specs=[SMEM] + [VMEM] * (ny + 3),
        out_specs=[VMEM] * 2,
        cost_estimate=pl.CostEstimate(flops=4 * items * hid * ny * width, bytes_accessed=4 << 20, transcendentals=0),
        name="back",
    )(place, *grads, hidden, slope, w_out)


def cut_by_x(feats_t, pre, came, out_mine, out_came, order, nz, nx, c):
    items = feats_t.shape[2]
    hid = came.shape[1]
    in_rows = came.shape[0] // (nz * nx)
    hy = feats_t.shape[0]
    ny, width = out_mine.shape[:2]
    out_rows = hy * width // (nz * nx)
    both = in_rows + out_rows
    feats_t = feats_t.reshape(-1, items)
    out_mine = out_mine.reshape(ny * width, -1)
    out_came = out_came.reshape(ny * width, -1)
    group = 2
    many, few = group * nx * in_rows, group * nx * out_rows
    ahead = hy * width // few

    def kernel(order_ref, f_ref, p_ref, came_ref, om_ref, oc_ref, own_ref, *rest):
        sends, part = rest[:-1], rest[-1]
        total = (mm(f_ref[...], p_ref[...]) + came_ref[...]).reshape(group, nx, in_rows, hid)
        outs = (om_ref[...] + oc_ref[...]).reshape(group, nx, out_rows, hid)
        for g in range(group):
            part[:, :in_rows] = total[g]
            part[:, in_rows:] = outs[g]
            own_ref[g] = part[order_ref[0]]
            for k, send in enumerate(sends):
                send[g] = part[order_ref[k + 1]].astype(BF)

    block = pl.BlockSpec((group, both, hid), lambda t: (t, 0, 0))
    return pl.pallas_call(
        kernel,
        out_shape=[jax.ShapeDtypeStruct((nz, both, hid), F32)]
        + [jax.ShapeDtypeStruct((nz, both, hid), BF)] * (nx - 1),
        grid=(nz // group,),
        in_specs=[
            SMEM,
            pl.BlockSpec((many, items), lambda t: (t, 0)),
            pl.BlockSpec((items, hid), lambda t: (0, c)),
            pl.BlockSpec((many, hid), lambda t: (t, 0)),
            pl.BlockSpec((few, hid), lambda t: (t, c)),
            pl.BlockSpec((few, hid), lambda t: (ahead + t, c)),
        ],
        out_specs=[block] * nx,
        scratch_shapes=[pltpu.VMEM((nx, both, hid), F32)],
        cost_estimate=pl.CostEstimate(
            flops=2 * nz * nx * in_rows * items * hid, bytes_accessed=8 << 20, transcendentals=0),
        name="cut_by_x",
    )(order, feats_t, pre, came, out_mine, out_came)


def shards(features, w_in, w_out, codebook, codes, decoder_grad):
    s, x, y = lax.axis_index("s"), lax.axis_index("x"), lax.axis_index("y")
    ns, nz, nx, ny = (lax.axis_size(a) for a in ("s", "z", "x", "y"))
    owners = ns * nz * nx
    items, depth = features.shape
    levels, rows_own, width = codebook.shape
    cap = 2 * items // owners
    slots = owners * cap
    hid = w_in.shape[1]
    in_rows, out_rows = w_in.shape[0], w_out.shape[0]
    items_all = items * owners
    hy = ny // ns

    slot_all, payload = ask(codes, w_in, w_out, nz, nx, ns, rows_own, cap)
    got_z = exchange(payload, "z")
    w_z, digits = got_z[:, :in_rows + out_rows], got_z[:, in_rows + out_rows:, :slots // nz]
    feats = [features, shift(features, "y", 1), shift(features, "y", 2), shift(features, "y", -1)]
    near = [w_z, shift(w_z, "x", 1), shift(w_z, "x", 2), shift(w_z, "x", -1)]
    other = [shift(block, "s", 1) for block in near]
    steps = jnp.arange(ny, dtype=I32)
    x_place = (x - steps) % nx
    y_place = (y - steps - hy * s) % ny
    y_send = (y + steps - hy * s) % ny
    x_send = (x + steps) % nx

    slot_list = [slot_all[l, :, 0] for l in range(levels)]
    slot_ids = jnp.arange(slots)
    digit_by = [
        digits, shift(digits, "x", 1), shift(digits, "x", 2), shift(digits, "x", -1)]
    none = jnp.zeros_like(digits)
    by_x = jnp.stack([
        sum(jnp.where((x - k) % nx == xa, digit_by[k], none) for k in range(nx)) for xa in range(nx)])
    far_x = shift(by_x, "s", 1)
    by_sx = jnp.stack([jnp.where(s == sa, by_x, far_x) for sa in range(ns)])
    mine = ((x * ns + s) * cap + jnp.arange(cap))[None, :] == jnp.arange(slots // nz)[:, None]
    picked = mm(by_sx.reshape(-1, slots // nz), mine.astype(BF)).reshape(ns, nx, nz, -1, cap)
    picked = jnp.transpose(picked, (3, 0, 2, 1, 4)).reshape(-1, slots).astype(jnp.int32)
    asked = (picked[0::2] * 32 + picked[1::2] - 1)[:levels].reshape(levels, -1, 128)
    rows_back = exchange(pick(asked, codebook, owners), OWN)
    words = [
        mm(
            (slot_list[l][:, None] == slot_ids[None, :]).astype(BF),
            rows_back[:, l * cap:(l + 1) * cap].reshape(slots, width),
        )
        for l in range(levels)
    ]

    hidden, slope, w_out_all, *lat = encode(
        feats, near, other, jnp.concatenate([x_place, y_place, y_send]), in_rows, out_rows
    )
    far = shift(lat[2], "y", 2)
    fwd = shift(lat[1], "y", 1)
    bwd = shift(lat[3], "y", -1)
    feats_here, feats_there = turn(feats, y_place)
    words = lax.optimization_barrier(words)
    latent = lat[0] + fwd + bwd + far

    residual = latent
    pull_sum = jnp.zeros_like(latent)
    outgoing = []
    for l in range(levels):
        placed = mm((slot_ids[:, None] == slot_list[l][None, :]).astype(BF), residual.astype(BF))
        outgoing.append(placed.astype(BF).reshape(owners, cap, width))
        residual = residual - words[l]
        pull_sum = pull_sum + residual
    latent_grad = (
        (decoder_grad.astype(F32) + 2.0 * BETA * pull_sum) / jnp.sqrt(F32(items_all))
    ).astype(BF)
    grads = [
        latent_grad,
        shift(latent_grad, "y", 1),
        shift(latent_grad, "y", 2),
        shift(latent_grad, "y", -1),
    ]
    incoming = exchange(jnp.concatenate(outgoing, axis=1), OWN)
    code_sums = collect(asked, incoming, rows_own)

    pre_grad, out_part = back(grads, hidden, slope, w_out_all, y_place)
    out_came = shift(out_part, "s", 1)
    pieces = 2
    step = hid // pieces
    there_rows = feats_there.reshape(hy * depth, items)
    sends = []
    for c in range(pieces):
        there = mm(there_rows, pre_grad[:, c * step:(c + 1) * step])
        came = shift(there, "s", 1)
        sends.append(cut_by_x(feats_here, pre_grad, came, out_part, out_came, x_send, nz, nx, c))
    in_list, out_list = [], []
    for c in range(pieces):
        own, to_1, to_2, to_3 = sends[c]
        sum_x = (
            own
            + shift(to_1, "x", 1).astype(F32)
            + shift(to_2, "x", 2).astype(F32)
            + shift(to_3, "x", -1).astype(F32)
        )
        over_z = exchange(sum_x.astype(BF), "z")
        sum_z = jnp.sum(over_z.astype(F32), axis=0)
        in_list.append(sum_z[:in_rows])
        out_list.append(sum_z[in_rows:])
    return (jnp.concatenate(in_list, axis=1), jnp.concatenate(out_list, axis=1), code_sums)


def solution(mesh):
    fine = Mesh(mesh.devices.reshape(2, 8, 4, 4), ("s", "z", "x", "y"))
    in_specs = (
        P(OWN, "y"),
        P(OWN, "y"),
        P(OWN, "y"),
        P(None, OWN, "y"),
        P(None, OWN),
        P(OWN, "y"),
    )
    out_specs = (P(OWN, "y"), P(OWN, "y"), P(None, OWN, "y"))
    return jax.shard_map(shards, mesh=fine, in_specs=in_specs, out_specs=out_specs, check_vma=False)
```

profile of v0, /device:TPU:8, one launch (start us, length us, event | category | flops | bytes accessed | tf_op | source)
XLA Modules:
  0.0 221.1 jit_solution(9284255257934130345)
XLA Ops:
  0.6 4.9 %ask.1 = (s32[3,512,1]{2,1,0:T(8,128)}, bf16[8,80,512]{2,1,0:T(8,128)(2,1)}) custom-call(s32[3,512]{1,0:T(4,128)} %codes_ref.1, bf16[64,512]{1,0:T(8,128)(2,1)} %wi_ref.1, bf16[8,512]{1,0:T(8,128)(2,1)} %wo_ref.1), custom_call_target="tpu_custom_call" | custom-call | tf_op jit(solution)/shard_map/ask/pallas_call | solution.py:134
  5.5 28.8 %all_to_all.25 = bf16[8,80,512]{2,1,0:T(8,128)(2,1)S(1)} all-to-all(bf16[8,80,512]{2,1,0:T(8,128)(2,1)} %get-tuple-element.28), channel_id=1, replica_groups=mesh['s'=2,'z'=8,'x'=4,'y'=4] {'z'}, dimensions={0} | all-to-all | bytes 1310720 | tf_op jit(solution)/shard_map/all_to_all | solution.py:23
  34.3 1.5 collective-permute-start.13
  35.8 2.7 %collective-permute-start.14 = (bf16[8,8,128]{2,1,0:T(8,128)(2,1)S(1)}, bf16[8,8,128]{2,1,0:T(8,128)(2,1)S(1)}, u32[]{:S(2)}, u32[]{:S(2)}) collective-permute-start(bf16[8,8,128]{2,1,0:T(8,128)(2,1)S(1)} %slice.69), channel_id=1, source_target_pairs={{0,8},{4,12},{8,0},{12,4},{1,9},{5,13},{9,1},{13,5},{2,10},{6,14},... | collective-permute-start | bytes 49160 | tf_op jit(solution)/shard_map/ppermute | solution.py:19
  38.5 1.4 collective-permute-start.15
  39.9 1.6 collective-permute-start
  41.5 0.9 collective-permute-start.1
  42.6 1.2 collective-permute-done.16
  44.6 0.6 copy.13
  45.2 7.3 %pick.1 = bf16[64,48,128]{2,1,0:T(8,128)(2,1)} custom-call(s32[3,8,128]{2,1,0:T(8,128)} %bitcast.53, bf16[3,1024,128]{2,1,0:T(8,128)(2,1)} %book_ref.1), custom_call_target="tpu_custom_call" | custom-call | tf_op jit(solution)/shard_map/pick/pallas_call | solution.py:168
  52.6 5.5 %all-to-all-start.1 = ((bf16[64,48,128]{2,1,0:T(8,128)(2,1)}), bf16[64,48,128]{2,1,0:T(8,128)(2,1)}, u32[]{:S(2)}, u32[]{:S(2)}) async-start(bf16[64,48,128]{2,1,0:T(8,128)(2,1)} %pick.1), calls=%async_computation.1 | async-start | bytes 1572864 | tf_op jit(solution)/shard_map/all_to_all | solution.py:23
  58.1 1.5 collective-permute-start.3
  59.5 2.7 %collective-permute-start.4 = (bf16[8,72,512]{2,1,0:T(8,128)(2,1)S(1)}, bf16[8,72,512]{2,1,0:T(8,128)(2,1)S(1)}, u32[]{:S(2)}, u32[]{:S(2)}) collective-permute-start(bf16[8,72,512]{2,1,0:T(8,128)(2,1)S(1)} %slice.68.refs_4_), channel_id=1, source_target_pairs={{0,8},{4,12},{8,0},{12,4},{1,9},{5,13},{9,1},{13,5},{2,10},{6,14},... | collective-permute-start | bytes 1769480 | tf_op jit(solution)/shard_map/ppermute | solution.py:19
  62.2 1.5 collective-permute-start.5
  63.7 2.5 %collective-permute-done.refs_1_ = bf16[512,1024]{1,0:T(8,128)(2,1)S(1)} collective-permute-done((bf16[512,1024]{1,0:T(8,128)(2,1)}, bf16[512,1024]{1,0:T(8,128)(2,1)S(1)}, u32[]{:S(2)}, u32[]{:S(2)}) %collective-permute-start) | collective-permute-done | bytes 1048608 | tf_op jit(solution)/shard_map/ppermute | solution.py:19
  66.2 0.5 collective-permute-start.2
  67.1 15.9 %collective-permute-done.3.refs_5_ = bf16[8,72,512]{2,1,0:T(8,128)(2,1)S(1)} collective-permute-done((bf16[8,72,512]{2,1,0:T(8,128)(2,1)S(1)}, bf16[8,72,512]{2,1,0:T(8,128)(2,1)S(1)}, u32[]{:S(2)}, u32[]{:S(2)}) %collective-permute-start.3) | collective-permute-done | bytes 589856 | tf_op jit(solution)/shard_map/ppermute | solution.py:19
  83.1 12.6 %collective-permute-done.4.refs_6_ = bf16[8,72,512]{2,1,0:T(8,128)(2,1)S(1)} collective-permute-done((bf16[8,72,512]{2,1,0:T(8,128)(2,1)S(1)}, bf16[8,72,512]{2,1,0:T(8,128)(2,1)S(1)}, u32[]{:S(2)}, u32[]{:S(2)}) %collective-permute-start.4) | collective-permute-done | bytes 589856 | tf_op jit(solution)/shard_map/ppermute | solution.py:19
  95.7 0.5 collective-permute-start.9
  96.3 1.4 slice_reduce_fusion
  97.7 2.3 %collective-permute-done.2.refs_3_ = bf16[512,1024]{1,0:T(8,128)(2,1)} collective-permute-done((bf16[512,1024]{1,0:T(8,128)(2,1)}, bf16[512,1024]{1,0:T(8,128)(2,1)}, u32[]{:S(2)}, u32[]{:S(2)}) %collective-permute-start.2) | collective-permute-done | bytes 1048608 | tf_op jit(solution)/shard_map/ppermute | solution.py:19
  100.0 7.4 %encode.1 = (bf16[512,512]{1,0:T(8,128)(2,1)S(1)}, f32[512,512]{1,0:T(8,128)}, bf16[4,128,512]{2,1,0:T(8,128)(2,1)S(1)}, f32[512,128]{1,0:T(8,128)S(1)}, f32[512...) custom-call(s32[12]{0:T(128)S(1)} %pad_add_fusion.place_ref, bf16[512,1024]{1,0:T(8,128)(2,1)} %refs_0_.3, ...), custom_call_target="tpu_custom_call" | custom-call | flops 2415919104 | bytes 12582912 | tf_op jit(solution)/shard_map/encode/pallas_call | solution.py:72
  107.4 0.8 copy-done
  108.2 0.8 copy-done.1
  109.1 2.0 collective-permute-start.10
  111.1 1.5 collective-permute-start.12
  112.6 1.3 fusion.37
  113.8 0.5 fusion.2
  114.4 0.5 fusion.1
  114.9 0.5 fusion
  115.4 3.1 %collective-permute-done.10 = f32[512,128]{1,0:T(8,128)S(1)} collective-permute-done((f32[512,128]{1,0:T(8,128)}, f32[512,128]{1,0:T(8,128)S(1)}, u32[]{:S(2)}, u32[]{:S(2)}) %collective-permute-start.10) | collective-permute-done | bytes 262176 | tf_op jit(solution)/shard_map/ppermute | solution.py:19
  118.5 5.9 %collective-permute-done.12 = f32[512,128]{1,0:T(8,128)S(1)} collective-permute-done((f32[512,128]{1,0:T(8,128)S(1)}, f32[512,128]{1,0:T(8,128)S(1)}, u32[]{:S(2)}, u32[]{:S(2)}) %collective-permute-start.12) | collective-permute-done | bytes 262176 | tf_op jit(solution)/shard_map/ppermute | solution.py:19
  124.6 3.2 %collective-permute-start.18 = (bf16[512,128]{1,0:T(8,128)(2,1)S(1)}, bf16[512,128]{1,0:T(8,128)(2,1)S(1)}, u32[]{:S(2)}, u32[]{:S(2)}) collective-permute-start(bf16[512,128]{1,0:T(8,128)(2,1)S(1)} %get-tuple-element.54.refs_0_), channel_id=1, source_target_pairs={{0,2},{1,3},{2,0},{3,1},{4,6},{5,7},{6,4},{7,5},{8,10},{9,11},{10,... | collective-permute-start | bytes 393224 | tf_op jit(solution)/shard_map/ppermute | solution.py:19
  127.8 2.3 %collective-permute-start.19 = (bf16[512,128]{1,0:T(8,128)(2,1)S(1)}, bf16[512,128]{1,0:T(8,128)(2,1)S(1)}, u32[]{:S(2)}, u32[]{:S(2)}) collective-permute-start(bf16[512,128]{1,0:T(8,128)(2,1)S(1)} %get-tuple-element.54.refs_0_), channel_id=1, source_target_pairs={{0,3},{1,0},{2,1},{3,2},{4,7},{5,4},{6,5},{7,6},{8,11},{9,8},{10,9... | collective-permute-start | bytes 393224 | tf_op jit(solution)/shard_map/ppermute | solution.py:19
  130.2 5.8 %turn.1 = (bf16[2,1024,512]{2,1,0:T(8,128)(2,1)}, bf16[2,1024,512]{2,1,0:T(8,128)(2,1)}) custom-call(s32[4]{0:T(128)} %copy-done.15, bf16[512,1024]{1,0:T(8,128)(2,1)} %refs_0_.3, bf16[512,1024]{1,0:T(8,128)(2,1)} %copy-done.7, bf16[512,1024]{1,0:T(8,128)(2,1)} %collective-permute-done.1.refs_2_, bf16[512,1024]{1,0:T(8,128)(2,1)} %collective-permute-done.2.refs_3_), custom_call_target="tpu_custom_call" | custom-call | bytes 8388608 | tf_op jit(solution)/shard_map/turn/pallas_call | solution.py:235
  136.0 0.6 copy-done.12
  136.7 3.8 %back.1 = (bf16[512,512]{1,0:T(8,128)(2,1)}, f32[4,128,512]{2,1,0:T(8,128)}) custom-call(s32[4]{0:T(128)} %copy-done.15, bf16[512,128]{1,0:T(8,128)(2,1)} %copy-done.10, bf16[512,128]{1,0:T(8,128)(2,1)} %copy-done.12, bf16[512,128]{1,0:T(8,128)(2,1)} %copy-done.13, bf16[512,128]{1,0:T(8,128)(2,1)} %copy-done.14, bf16[512,512]{1,0:T(8,128)(2,1)} %copy-done, ...), custom_call_target="tpu_custom_call" | custom-call | flops 536870912 | bytes 4194304 | tf_op jit(solution)/shard_map/back/pallas_call | solution.py:259
  140.5 3.0 %fusion.18 = f32[2048,256]{1,0:T(8,128)} fusion(bf16[2048,512]{1,0:T(8,128)(2,1)S(1)} %bitcast.39, bf16[512,512]{1,0:T(8,128)(2,1)} %get-tuple-element.40.p_ref), kind=kOutput, calls=%fused_computation.30 | convolution fusion | flops 536870912 | bytes 4456448 | tf_op jit(solution)/shard_map/dot_general | solution.py:27
  143.6 2.1 fusion.16
  145.6 0.5 collective-permute-start.25
  147.7 1.0 pad_maximum_fusion
  148.7 8.2 %all-to-all-start.4 = ((bf16[64,48,128]{2,1,0:T(8,128)(2,1)}), bf16[64,48,128]{2,1,0:T(8,128)(2,1)S(1)}, u32[]{:S(2)}, u32[]{:S(2)}) async-start(bf16[64,48,128]{2,1,0:T(8,128)(2,1)} %pad_maximum_fusion), calls=%async_computation.4 | async-start | bytes 1572864 | tf_op jit(solution)/shard_map/all_to_all | solution.py:23
  156.8 0.5 and_select_fusion.3.order_ref
  157.4 1.0 copy-done.5
  158.3 4.9 %cut_by_x.2 = (f32[8,72,256]{2,1,0:T(8,128)}, bf16[8,72,256]{2,1,0:T(8,128)(2,1)}, bf16[8,72,256]{2,1,0:T(8,128)(2,1)}, bf16[8,72,256]{2,1,0:T(8,128)(2,1)}) custom-call(s32[4]{0:T(128)} %and_select_fusion.3.order_ref, bf16[2048,512]{1,0:T(8,128)(2,1)} %bitcast.41, bf16[512,512]{1,0:T(8,128)(2,1)} %get-tuple-element.40.p_ref, ...), custom_call_target="tpu_custom_call" | custom-call | flops 536870912 | bytes 8388608 | tf_op jit(solution)/shard_map/cut_by_x/pallas_call | solution.py:299
  163.2 1.6 collective-permute-start.22
  164.8 2.7 %collective-permute-start.23 = (bf16[8,72,256]{2,1,0:T(8,128)(2,1)}, bf16[8,72,256]{2,1,0:T(8,128)(2,1)S(1)}, u32[]{:S(2)}, u32[]{:S(2)}) collective-permute-start(bf16[8,72,256]{2,1,0:T(8,128)(2,1)} %get-tuple-element.45), channel_id=1, source_target_pairs={{0,8},{4,12},{8,0},{12,4},{1,9},{5,13},{9,1},{13,5},{2,10},{6,14},... | collective-permute-start | bytes 884744 | tf_op jit(solution)/shard_map/ppermute | solution.py:19
  167.5 1.5 collective-permute-start.24
  169.0 4.9 %cut_by_x.3 = (f32[8,72,256]{2,1,0:T(8,128)}, bf16[8,72,256]{2,1,0:T(8,128)(2,1)}, bf16[8,72,256]{2,1,0:T(8,128)(2,1)}, bf16[8,72,256]{2,1,0:T(8,128)(2,1)}) custom-call(s32[4]{0:T(128)} %and_select_fusion.3.order_ref, bf16[2048,512]{1,0:T(8,128)(2,1)} %bitcast.42, bf16[512,512]{1,0:T(8,128)(2,1)} %get-tuple-element.40.p_ref, ...), custom_call_target="tpu_custom_call" | custom-call | flops 536870912 | bytes 8388608 | tf_op jit(solution)/shard_map/cut_by_x/pallas_call | solution.py:299
  173.9 0.6 collective-permute-start.26
  174.5 1.0 collective-permute-start.27
  175.5 3.9 %collective-permute-done.22 = bf16[8,72,256]{2,1,0:T(8,128)(2,1)S(1)} collective-permute-done((bf16[8,72,256]{2,1,0:T(8,128)(2,1)}, bf16[8,72,256]{2,1,0:T(8,128)(2,1)S(1)}, u32[]{:S(2)}, u32[]{:S(2)}) %collective-permute-start.22) | collective-permute-done | bytes 294944 | tf_op jit(solution)/shard_map/ppermute | solution.py:19
  179.3 1.3 collective-permute-start.28
  180.7 5.8 %collective-permute-done.23 = bf16[8,72,256]{2,1,0:T(8,128)(2,1)S(1)} collective-permute-done((bf16[8,72,256]{2,1,0:T(8,128)(2,1)}, bf16[8,72,256]{2,1,0:T(8,128)(2,1)S(1)}, u32[]{:S(2)}, u32[]{:S(2)}) %collective-permute-start.23) | collective-permute-done | bytes 294944 | tf_op jit(solution)/shard_map/ppermute | solution.py:19
  186.4 0.8 add_convert_fusion.1
  187.3 5.7 %all-to-all-start.2 = ((bf16[8,72,256]{2,1,0:T(8,128)(2,1)}), bf16[8,72,256]{2,1,0:T(8,128)(2,1)S(1)}, u32[]{:S(2)}, u32[]{:S(2)}) async-start(bf16[8,72,256]{2,1,0:T(8,128)(2,1)} %add_convert_fusion.1), calls=%async_computation.2 | async-start | bytes 589824 | tf_op jit(solution)/shard_map/all_to_all | solution.py:23
  192.9 5.6 %collective-permute-done.27 = bf16[8,72,256]{2,1,0:T(8,128)(2,1)S(1)} collective-permute-done((bf16[8,72,256]{2,1,0:T(8,128)(2,1)}, bf16[8,72,256]{2,1,0:T(8,128)(2,1)S(1)}, u32[]{:S(2)}, u32[]{:S(2)}) %collective-permute-start.27) | collective-permute-done | bytes 294944 | tf_op jit(solution)/shard_map/ppermute | solution.py:19
  198.5 1.8 add_convert_fusion
  200.3 5.0 %all-to-all-done.2 = bf16[8,72,256]{2,1,0:T(8,128)(2,1)S(1)} async-done(((bf16[8,72,256]{2,1,0:T(8,128)(2,1)}), bf16[8,72,256]{2,1,0:T(8,128)(2,1)S(1)}, u32[]{:S(2)}, u32[]{:S(2)}) %all-to-all-start.2) | async-done | bytes 294944 | tf_op jit(solution)/shard_map/all_to_all | solution.py:23
  205.3 3.4 %all-to-all-start.3 = ((bf16[8,72,256]{2,1,0:T(8,128)(2,1)}), bf16[8,72,256]{2,1,0:T(8,128)(2,1)S(1)}, u32[]{:S(2)}, u32[]{:S(2)}) async-start(bf16[8,72,256]{2,1,0:T(8,128)(2,1)} %add_convert_fusion), calls=%async_computation.3 | async-start | bytes 589824 | tf_op jit(solution)/shard_map/all_to_all | solution.py:23
  208.8 5.4 %collect.1 = f32[3,1024,128]{2,1,0:T(8,128)} custom-call(s32[3,8,128]{2,1,0:T(8,128)} %bitcast.54, bf16[64,48,128]{2,1,0:T(8,128)(2,1)} %copy-done.6), custom_call_target="tpu_custom_call" | custom-call | tf_op jit(solution)/shard_map/collect/pallas_call | solution.py:201
  214.3 5.4 %all-to-all-done.3 = bf16[8,72,256]{2,1,0:T(8,128)(2,1)S(1)} async-done(((bf16[8,72,256]{2,1,0:T(8,128)(2,1)}), bf16[8,72,256]{2,1,0:T(8,128)(2,1)S(1)}, u32[]{:S(2)}, u32[]{:S(2)}) %all-to-all-start.3) | async-done | bytes 294944 | tf_op jit(solution)/shard_map/all_to_all | solution.py:23
  219.8 0.6 pad_maximum_fusion.3
  220.4 0.7 pad_maximum_fusion.1
  (83 shorter events, 3.5 us)
Async XLA Ops:
  34.3 8.2 %collective-permute-start.13 = (bf16[8,8,128]{2,1,0:T(8,128)(2,1)S(1)}, bf16[8,8,128]{2,1,0:T(8,128)(2,1)S(1)}, u32[]{:S(2)}, u32[]{:S(2)}) collective-permute-start(bf16[8,8,128]{2,1,0:T(8,128)(2,1)S(1)} %slice.69), channel_id=1, source_target_pairs={{0,4},{4,8},{8,12},{12,0},{1,5},{5,9},{9,13},{13,1},{2,6},{6,10},{... | collective-permute-start | bytes 49160 | tf_op jit(solution)/shard_map/ppermute | solution.py:19
  35.8 6.7 %collective-permute-start.14 = (bf16[8,8,128]{2,1,0:T(8,128)(2,1)S(1)}, bf16[8,8,128]{2,1,0:T(8,128)(2,1)S(1)}, u32[]{:S(2)}, u32[]{:S(2)}) collective-permute-start(bf16[8,8,128]{2,1,0:T(8,128)(2,1)S(1)} %slice.69), channel_id=1, source_target_pairs={{0,8},{4,12},{8,0},{12,4},{1,9},{5,13},{9,1},{13,5},{2,10},{6,14},... | collective-permute-start | bytes 49160 | tf_op jit(solution)/shard_map/ppermute | solution.py:19
  38.5 4.0 %collective-permute-start.15 = (bf16[8,8,128]{2,1,0:T(8,128)(2,1)S(1)}, bf16[8,8,128]{2,1,0:T(8,128)(2,1)S(1)}, u32[]{:S(2)}, u32[]{:S(2)}) collective-permute-start(bf16[8,8,128]{2,1,0:T(8,128)(2,1)S(1)} %slice.69), channel_id=1, source_target_pairs={{0,12},{4,0},{8,4},{12,8},{1,13},{5,1},{9,5},{13,9},{2,14},{6,2},{... | collective-permute-start | bytes 49160 | tf_op jit(solution)/shard_map/ppermute | solution.py:19
  39.9 26.2 %collective-permute-start = (bf16[512,1024]{1,0:T(8,128)(2,1)}, bf16[512,1024]{1,0:T(8,128)(2,1)S(1)}, u32[]{:S(2)}, u32[]{:S(2)}) collective-permute-start(bf16[512,1024]{1,0:T(8,128)(2,1)} %refs_0_.3), channel_id=1, source_target_pairs={{0,1},{1,2},{2,3},{3,0},{4,5},{5,6},{6,7},{7,4},{8,9},{9,10},{10,1... | collective-permute-start | bytes 3145736 | tf_op jit(solution)/shard_map/ppermute | solution.py:19
  41.5 25.6 %collective-permute-start.1 = (bf16[512,1024]{1,0:T(8,128)(2,1)}, bf16[512,1024]{1,0:T(8,128)(2,1)}, u32[]{:S(2)}, u32[]{:S(2)}) collective-permute-start(bf16[512,1024]{1,0:T(8,128)(2,1)} %refs_0_.3), channel_id=1, source_target_pairs={{0,2},{1,3},{2,0},{3,1},{4,6},{5,7},{6,4},{7,5},{8,10},{9,11},{10,... | collective-permute-start | bytes 3145736 | tf_op jit(solution)/shard_map/ppermute | solution.py:19
  42.5 1.3 collective-permute-start.16
  52.6 60.0 %all-to-all-start.1 = ((bf16[64,48,128]{2,1,0:T(8,128)(2,1)}), bf16[64,48,128]{2,1,0:T(8,128)(2,1)}, u32[]{:S(2)}, u32[]{:S(2)}) async-start(bf16[64,48,128]{2,1,0:T(8,128)(2,1)} %pick.1), calls=%async_computation.1 | async-start | bytes 1572864 | tf_op jit(solution)/shard_map/all_to_all | solution.py:23
  58.1 25.0 %collective-permute-start.3 = (bf16[8,72,512]{2,1,0:T(8,128)(2,1)S(1)}, bf16[8,72,512]{2,1,0:T(8,128)(2,1)S(1)}, u32[]{:S(2)}, u32[]{:S(2)}) collective-permute-start(bf16[8,72,512]{2,1,0:T(8,128)(2,1)S(1)} %slice.68.refs_4_), channel_id=1, source_target_pairs={{0,4},{4,8},{8,12},{12,0},{1,5},{5,9},{9,13},{13,1},{2,6},{6,10},{... | collective-permute-start | bytes 1769480 | tf_op jit(solution)/shard_map/ppermute | solution.py:19
  59.5 36.1 %collective-permute-start.4 = (bf16[8,72,512]{2,1,0:T(8,128)(2,1)S(1)}, bf16[8,72,512]{2,1,0:T(8,128)(2,1)S(1)}, u32[]{:S(2)}, u32[]{:S(2)}) collective-permute-start(bf16[8,72,512]{2,1,0:T(8,128)(2,1)S(1)} %slice.68.refs_4_), channel_id=1, source_target_pairs={{0,8},{4,12},{8,0},{12,4},{1,9},{5,13},{9,1},{13,5},{2,10},{6,14},... | collective-permute-start | bytes 1769480 | tf_op jit(solution)/shard_map/ppermute | solution.py:19
  62.2 33.4 %collective-permute-start.5 = (bf16[8,72,512]{2,1,0:T(8,128)(2,1)S(1)}, bf16[8,72,512]{2,1,0:T(8,128)(2,1)S(1)}, u32[]{:S(2)}, u32[]{:S(2)}) collective-permute-start(bf16[8,72,512]{2,1,0:T(8,128)(2,1)S(1)} %slice.68.refs_4_), channel_id=1, source_target_pairs={{0,12},{4,0},{8,4},{12,8},{1,13},{5,1},{9,5},{13,9},{2,14},{6,2},{... | collective-permute-start | bytes 1769480 | tf_op jit(solution)/shard_map/ppermute | solution.py:19
  66.2 1.0 copy-start.7
  66.2 33.8 %collective-permute-start.2 = (bf16[512,1024]{1,0:T(8,128)(2,1)}, bf16[512,1024]{1,0:T(8,128)(2,1)}, u32[]{:S(2)}, u32[]{:S(2)}) collective-permute-start(bf16[512,1024]{1,0:T(8,128)(2,1)} %refs_0_.3), channel_id=1, source_target_pairs={{0,3},{1,0},{2,1},{3,2},{4,7},{5,4},{6,5},{7,6},{8,11},{9,8},{10,9... | collective-permute-start | bytes 3145736 | tf_op jit(solution)/shard_map/ppermute | solution.py:19
  67.1 32.8 %collective-permute-start.6 = (bf16[8,72,512]{2,1,0:T(8,128)(2,1)S(1)}, bf16[8,72,512]{2,1,0:T(8,128)(2,1)S(1)}, u32[]{:S(2)}, u32[]{:S(2)}) collective-permute-start(bf16[8,72,512]{2,1,0:T(8,128)(2,1)S(1)} %slice.68.refs_4_), channel_id=1, source_target_pairs={{0,128},{128,0},{1,129},{129,1},{2,130},{130,2},{3,131},{131,3},{4... | collective-permute-start | bytes 1769480 | tf_op jit(solution)/shard_map/ppermute | solution.py:19
  83.1 16.9 %collective-permute-start.7 = (bf16[8,72,512]{2,1,0:T(8,128)(2,1)S(1)}, bf16[8,72,512]{2,1,0:T(8,128)(2,1)}, u32[]{:S(2)}, u32[]{:S(2)}) collective-permute-start(bf16[8,72,512]{2,1,0:T(8,128)(2,1)S(1)} %collective-permute-done.3.refs_5_), channel_id=1, source_target_pairs={{0,128},{128,0},{1,129},{129,1},{2,130},{130,2},{3,131},{131,3},{4... | collective-permute-start | bytes 1769480 | tf_op jit(solution)/shard_map/ppermute | solution.py:19
  95.7 4.3 %collective-permute-start.8 = (bf16[8,72,512]{2,1,0:T(8,128)(2,1)S(1)}, bf16[8,72,512]{2,1,0:T(8,128)(2,1)}, u32[]{:S(2)}, u32[]{:S(2)}) collective-permute-start(bf16[8,72,512]{2,1,0:T(8,128)(2,1)S(1)} %collective-permute-done.4.refs_6_), channel_id=1, source_target_pairs={{0,128},{128,0},{1,129},{129,1},{2,130},{130,2},{3,131},{131,3},{4... | collective-permute-start | bytes 1769480 | tf_op jit(solution)/shard_map/ppermute | solution.py:19
  95.7 4.3 %collective-permute-start.9 = (bf16[8,72,512]{2,1,0:T(8,128)(2,1)S(1)}, bf16[8,72,512]{2,1,0:T(8,128)(2,1)}, u32[]{:S(2)}, u32[]{:S(2)}) collective-permute-start(bf16[8,72,512]{2,1,0:T(8,128)(2,1)S(1)} %collective-permute-done.5.refs_7_), channel_id=1, source_target_pairs={{0,128},{128,0},{1,129},{129,1},{2,130},{130,2},{3,131},{131,3},{4... | collective-permute-start | bytes 1769480 | tf_op jit(solution)/shard_map/ppermute | solution.py:19
  96.2 11.2 %copy-start.15 = (s32[4]{0:T(128)}, s32[4]{0:T(128)S(1)}, u32[]{:S(2)}) copy-start(s32[4]{0:T(128)S(1)} %get-tuple-element.65.place_ref) | copy-start | bytes 52
  107.4 0.8 copy-start
  108.2 0.8 copy-start.1
  109.1 9.4 %collective-permute-start.10 = (f32[512,128]{1,0:T(8,128)}, f32[512,128]{1,0:T(8,128)S(1)}, u32[]{:S(2)}, u32[]{:S(2)}) collective-permute-start(f32[512,128]{1,0:T(8,128)} %get-tuple-element.30), channel_id=1, source_target_pairs={{0,1},{1,2},{2,3},{3,0},{4,5},{5,6},{6,7},{7,4},{8,9},{9,10},{10,1... | collective-permute-start | bytes 786440 | tf_op jit(solution)/shard_map/ppermute | solution.py:19
  111.1 7.4 %collective-permute-start.11 = (f32[512,128]{1,0:T(8,128)}, f32[512,128]{1,0:T(8,128)S(1)}, u32[]{:S(2)}, u32[]{:S(2)}) collective-permute-start(f32[512,128]{1,0:T(8,128)} %get-tuple-element.31), channel_id=1, source_target_pairs={{0,3},{1,0},{2,1},{3,2},{4,7},{5,4},{6,5},{7,6},{8,11},{9,8},{10,9... | collective-permute-start | bytes 786440 | tf_op jit(solution)/shard_map/ppermute | solution.py:19
  111.1 13.2 %copy-start.11 = (bf16[512,128]{1,0:T(8,128)(2,1)S(1)}, bf16[512,128]{1,0:T(8,128)(2,1)}, u32[]{:S(2)}) copy-start(bf16[512,128]{1,0:T(8,128)(2,1)} %param.11) | copy-start | bytes 393220
  111.1 13.2 %collective-permute-start.12 = (f32[512,128]{1,0:T(8,128)S(1)}, f32[512,128]{1,0:T(8,128)S(1)}, u32[]{:S(2)}, u32[]{:S(2)}) collective-permute-start(f32[512,128]{1,0:T(8,128)S(1)} %get-tuple-element.32), channel_id=1, source_target_pairs={{0,2},{1,3},{2,0},{3,1},{4,6},{5,7},{6,4},{7,5},{8,10},{9,11},{10,... | collective-permute-start | bytes 786440 | tf_op jit(solution)/shard_map/ppermute | solution.py:19
  124.5 11.4 %copy-start.10 = (bf16[512,128]{1,0:T(8,128)(2,1)}, bf16[512,128]{1,0:T(8,128)(2,1)S(1)}, u32[]{:S(2)}) copy-start(bf16[512,128]{1,0:T(8,128)(2,1)S(1)} %get-tuple-element.54.refs_0_) | copy-start | bytes 393220
  124.5 11.4 %collective-permute-start.17 = (bf16[512,128]{1,0:T(8,128)(2,1)S(1)}, bf16[512,128]{1,0:T(8,128)(2,1)S(1)}, u32[]{:S(2)}, u32[]{:S(2)}) collective-permute-start(bf16[512,128]{1,0:T(8,128)(2,1)S(1)} %get-tuple-element.54.refs_0_), channel_id=1, source_target_pairs={{0,1},{1,2},{2,3},{3,0},{4,5},{5,6},{6,7},{7,4},{8,9},{9,10},{10,1... | collective-permute-start | bytes 393224 | tf_op jit(solution)/shard_map/ppermute | solution.py:19
  124.6 11.4 %collective-permute-start.18 = (bf16[512,128]{1,0:T(8,128)(2,1)S(1)}, bf16[512,128]{1,0:T(8,128)(2,1)S(1)}, u32[]{:S(2)}, u32[]{:S(2)}) collective-permute-start(bf16[512,128]{1,0:T(8,128)(2,1)S(1)} %get-tuple-element.54.refs_0_), channel_id=1, source_target_pairs={{0,2},{1,3},{2,0},{3,1},{4,6},{5,7},{6,4},{7,5},{8,10},{9,11},{10,... | collective-permute-start | bytes 393224 | tf_op jit(solution)/shard_map/ppermute | solution.py:19
  127.8 8.2 %collective-permute-start.19 = (bf16[512,128]{1,0:T(8,128)(2,1)S(1)}, bf16[512,128]{1,0:T(8,128)(2,1)S(1)}, u32[]{:S(2)}, u32[]{:S(2)}) collective-permute-start(bf16[512,128]{1,0:T(8,128)(2,1)S(1)} %get-tuple-element.54.refs_0_), channel_id=1, source_target_pairs={{0,3},{1,0},{2,1},{3,2},{4,7},{5,4},{6,5},{7,6},{8,11},{9,8},{10,9... | collective-permute-start | bytes 393224 | tf_op jit(solution)/shard_map/ppermute | solution.py:19
  135.9 4.6 %copy-start.2 = (bf16[2,1024,512]{2,1,0:T(8,128)(2,1)S(1)}, bf16[2,1024,512]{2,1,0:T(8,128)(2,1)}, u32[]{:S(2)}) copy-start(bf16[2,1024,512]{2,1,0:T(8,128)(2,1)} %get-tuple-element.41) | copy-start | bytes 6291460
  135.9 0.7 copy-start.12
  136.0 0.7 copy-start.13
  136.0 0.7 copy-start.14
  140.5 3.1 %copy-start.3 = (bf16[512,512]{1,0:T(8,128)(2,1)S(1)}, bf16[512,512]{1,0:T(8,128)(2,1)}, u32[]{:S(2)}) copy-start(bf16[512,512]{1,0:T(8,128)(2,1)} %get-tuple-element.40.p_ref) | copy-start | bytes 1572868
  143.6 13.8 %collective-permute-start.20 = (f32[2048,256]{1,0:T(8,128)}, f32[2048,256]{1,0:T(8,128)}, u32[]{:S(2)}, u32[]{:S(2)}) collective-permute-start(f32[2048,256]{1,0:T(8,128)} %fusion.18), channel_id=1, source_target_pairs={{0,128},{128,0},{1,129},{129,1},{2,130},{130,2},{3,131},{131,3},{4... | collective-permute-start | bytes 6291464 | tf_op jit(solution)/shard_map/ppermute | solution.py:19
  145.6 1.9 copy-start.4
  145.6 23.3 %collective-permute-start.25 = (f32[2048,256]{1,0:T(8,128)}, f32[2048,256]{1,0:T(8,128)}, u32[]{:S(2)}, u32[]{:S(2)}) collective-permute-start(f32[2048,256]{1,0:T(8,128)} %fusion.16), channel_id=1, source_target_pairs={{0,128},{128,0},{1,129},{129,1},{2,130},{130,2},{3,131},{131,3},{4... | collective-permute-start | bytes 6291464 | tf_op jit(solution)/shard_map/ppermute | solution.py:19
  147.6 9.8 %collective-permute-start.21 = (f32[4,128,512]{2,1,0:T(8,128)S(1)}, f32[4,128,512]{2,1,0:T(8,128)S(1)}, u32[]{:S(2)}, u32[]{:S(2)}) collective-permute-start(f32[4,128,512]{2,1,0:T(8,128)S(1)} %copy-done.4), channel_id=1, source_target_pairs={{0,128},{128,0},{1,129},{129,1},{2,130},{130,2},{3,131},{131,3},{4... | collective-permute-start | bytes 3145736 | tf_op jit(solution)/shard_map/ppermute | solution.py:19
  148.7 38.6 %all-to-all-start.4 = ((bf16[64,48,128]{2,1,0:T(8,128)(2,1)}), bf16[64,48,128]{2,1,0:T(8,128)(2,1)S(1)}, u32[]{:S(2)}, u32[]{:S(2)}) async-start(bf16[64,48,128]{2,1,0:T(8,128)(2,1)} %pad_maximum_fusion), calls=%async_computation.4 | async-start | bytes 1572864 | tf_op jit(solution)/shard_map/all_to_all | solution.py:23
  157.4 1.0 copy-start.5
  163.2 16.1 %collective-permute-start.22 = (bf16[8,72,256]{2,1,0:T(8,128)(2,1)}, bf16[8,72,256]{2,1,0:T(8,128)(2,1)S(1)}, u32[]{:S(2)}, u32[]{:S(2)}) collective-permute-start(bf16[8,72,256]{2,1,0:T(8,128)(2,1)} %get-tuple-element.44), channel_id=1, source_target_pairs={{0,4},{4,8},{8,12},{12,0},{1,5},{5,9},{9,13},{13,1},{2,6},{6,10},{... | collective-permute-start | bytes 884744 | tf_op jit(solution)/shard_map/ppermute | solution.py:19
  164.8 21.6 %collective-permute-start.23 = (bf16[8,72,256]{2,1,0:T(8,128)(2,1)}, bf16[8,72,256]{2,1,0:T(8,128)(2,1)S(1)}, u32[]{:S(2)}, u32[]{:S(2)}) collective-permute-start(bf16[8,72,256]{2,1,0:T(8,128)(2,1)} %get-tuple-element.45), channel_id=1, source_target_pairs={{0,8},{4,12},{8,0},{12,4},{1,9},{5,13},{9,1},{13,5},{2,10},{6,14},... | collective-permute-start | bytes 884744 | tf_op jit(solution)/shard_map/ppermute | solution.py:19
  167.5 18.9 %copy-start.9 = (f32[8,72,256]{2,1,0:T(8,128)S(1)}, f32[8,72,256]{2,1,0:T(8,128)}, u32[]{:S(2)}) copy-start(f32[8,72,256]{2,1,0:T(8,128)} %get-tuple-element.43) | copy-start | bytes 1769476
  167.5 18.9 %collective-permute-start.24 = (bf16[8,72,256]{2,1,0:T(8,128)(2,1)}, bf16[8,72,256]{2,1,0:T(8,128)(2,1)S(1)}, u32[]{:S(2)}, u32[]{:S(2)}) collective-permute-start(bf16[8,72,256]{2,1,0:T(8,128)(2,1)} %get-tuple-element.46), channel_id=1, source_target_pairs={{0,12},{4,0},{8,4},{12,8},{1,13},{5,1},{9,5},{13,9},{2,14},{6,2},{... | collective-permute-start | bytes 884744 | tf_op jit(solution)/shard_map/ppermute | solution.py:19
  173.9 24.6 %copy-start.8 = (f32[8,72,256]{2,1,0:T(8,128)S(1)}, f32[8,72,256]{2,1,0:T(8,128)}, u32[]{:S(2)}) copy-start(f32[8,72,256]{2,1,0:T(8,128)} %get-tuple-element.47) | copy-start | bytes 1769476
  173.9 19.0 %collective-permute-start.26 = (bf16[8,72,256]{2,1,0:T(8,128)(2,1)}, bf16[8,72,256]{2,1,0:T(8,128)(2,1)S(1)}, u32[]{:S(2)}, u32[]{:S(2)}) collective-permute-start(bf16[8,72,256]{2,1,0:T(8,128)(2,1)} %get-tuple-element.48), channel_id=1, source_target_pairs={{0,4},{4,8},{8,12},{12,0},{1,5},{5,9},{9,13},{13,1},{2,6},{6,10},{... | collective-permute-start | bytes 884744 | tf_op jit(solution)/shard_map/ppermute | solution.py:19
  174.5 24.0 %collective-permute-start.27 = (bf16[8,72,256]{2,1,0:T(8,128)(2,1)}, bf16[8,72,256]{2,1,0:T(8,128)(2,1)S(1)}, u32[]{:S(2)}, u32[]{:S(2)}) collective-permute-start(bf16[8,72,256]{2,1,0:T(8,128)(2,1)} %get-tuple-element.49), channel_id=1, source_target_pairs={{0,8},{4,12},{8,0},{12,4},{1,9},{5,13},{9,1},{13,5},{2,10},{6,14},... | collective-permute-start | bytes 884744 | tf_op jit(solution)/shard_map/ppermute | solution.py:19
  179.3 19.2 %collective-permute-start.28 = (bf16[8,72,256]{2,1,0:T(8,128)(2,1)}, bf16[8,72,256]{2,1,0:T(8,128)(2,1)}, u32[]{:S(2)}, u32[]{:S(2)}) collective-permute-start(bf16[8,72,256]{2,1,0:T(8,128)(2,1)} %get-tuple-element.50), channel_id=1, source_target_pairs={{0,12},{4,0},{8,4},{12,8},{1,13},{5,1},{9,5},{13,9},{2,14},{6,2},{... | collective-permute-start | bytes 884744 | tf_op jit(solution)/shard_map/ppermute | solution.py:19
  187.3 21.5 %copy-start.6 = (bf16[64,48,128]{2,1,0:T(8,128)(2,1)}, bf16[64,48,128]{2,1,0:T(8,128)(2,1)S(1)}, u32[]{:S(2)}) copy-start(bf16[64,48,128]{2,1,0:T(8,128)(2,1)S(1)} %all-to-all-done.4.in_ref) | copy-start | bytes 2359300
  187.3 18.1 %all-to-all-start.2 = ((bf16[8,72,256]{2,1,0:T(8,128)(2,1)}), bf16[8,72,256]{2,1,0:T(8,128)(2,1)S(1)}, u32[]{:S(2)}, u32[]{:S(2)}) async-start(bf16[8,72,256]{2,1,0:T(8,128)(2,1)} %add_convert_fusion.1), calls=%async_computation.2 | async-start | bytes 589824 | tf_op jit(solution)/shard_map/all_to_all | solution.py:23
  205.3 14.4 %all-to-all-start.3 = ((bf16[8,72,256]{2,1,0:T(8,128)(2,1)}), bf16[8,72,256]{2,1,0:T(8,128)(2,1)S(1)}, u32[]{:S(2)}, u32[]{:S(2)}) async-start(bf16[8,72,256]{2,1,0:T(8,128)(2,1)} %add_convert_fusion), calls=%async_computation.3 | async-start | bytes 589824 | tf_op jit(solution)/shard_map/all_to_all | solution.py:23
where the time goes:
time: 223 us; the launch traced here: 221 us
  waiting for transfers between devices  69.2 us (31%)
  starting transfers between devices  56.1 us (25%)
  Pallas kernels  44.4 us (20%)
  blocking collectives  28.8 us (13%)
  matrix products  8.28 us (4%)
  local copies, waits for them, and re-layouts  7.59 us (3%)
  other arithmetic  5.78 us (3%)
    ppermute x29, waiting for transfers between devices, shift(): lax.ppermute(value, axis, [(i, (i + by) % size) for i in range(size)])  58.7 us
    ppermute x29, starting transfers between devices, shift(): lax.ppermute(value, axis, [(i, (i + by) % size) for i in range(size)])  33.4 us
    all_to_all x1, blocking collectives, exchange(): return lax.all_to_all(value, axis, split_axis=0, concat_axis=0, tiled=True)  28.8 us
    all_to_all x4, starting transfers between devices, exchange(): return lax.all_to_all(value, axis, split_axis=0, concat_axis=0, tiled=True)  22.7 us
    all_to_all x4, waiting for transfers between devices, exchange(): return lax.all_to_all(value, axis, split_axis=0, concat_axis=0, tiled=True)  10.5 us
    pallas_call x2, Pallas kernels, cut_by_x(): pl.pallas_call(kernel, out_shape=[jax.ShapeDtypeStruct((nz, both, hid), F...  9.78 us
    dot_general x9, matrix products, mm(): return lax.dot_general(a, b, (dims, ((), ())), preferred_element_type=F32)  8.28 us
    pallas_call x1, Pallas kernels, encode(): pl.pallas_call(kernel, out_shape=[jax.ShapeDtypeStruct((items, hid), BF),...  7.42 us
  transfers between devices with their start and end apart: 33, of which 12 were waited for; matrix products, arithmetic and copies ran while one was open for 6% of the time, Pallas kernels for 16%

commit v1 on v0

--- a/solution.py
+++ b/solution.py
@@ -27,10 +27,17 @@
     return lax.dot_general(a, b, (dims, ((), ())), preferred_element_type=F32)
 
 
-def encode(feats, near, other, place, in_rows, out_rows):
+def split(value, size):
+    if size & (size - 1) == 0:
+        return lax.shift_right_logical(value, jnp.full_like(value, size.bit_length() - 1)), value & (size - 1)
+    return value // size, value % size
+
+
+def encode(feats, near, other, spans, place, in_rows, out_rows):
     items, depth = feats[0].shape
     nz, _, hid = near[0].shape
-    nx = len(near)
+    many = len(near)
+    nx = 1 + max(k for k, _, _ in spans)
     ny = len(feats)
     hz = nz * 2 // ny
     width = hz * nx * out_rows
@@ -38,16 +45,16 @@
 
     def kernel(place_ref, *refs):
         f_refs, refs = refs[:ny], refs[ny:]
-        n_refs, refs = refs[:nx], refs[nx:]
-        o_refs, refs = refs[:nx], refs[nx:]
+        n_refs, refs = refs[:many], refs[many:]
+        o_refs, refs = refs[:many], refs[many:]
         hid_ref, slope_ref, wo_ref = refs[:3]
         lat_refs, (w_ref, wo32_ref) = refs[3:3 + ny], refs[3 + ny:]
-        for k in range(nx):
+        for (k, low, high), *pair in zip(spans, n_refs, o_refs):
             xk = place_ref[k]
-            for r, ref in enumerate((n_refs[k], o_refs[k])):
-                for zh in range(ny // 2):
+            for r, ref in enumerate(pair):
+                for zh in range(low, high):
                     p = r * (ny // 2) + zh
-                    cut = ref[zh * hz:(zh + 1) * hz]
+                    cut = ref[(zh - low) * hz:(zh - low + 1) * hz]
                     w_ref[p, :, xk] = cut[:, :in_rows]
                     wo32_ref[p, :, xk] = cut[:, in_rows:].astype(F32)
         for p in range(ny):
@@ -76,7 +83,7 @@
             jax.ShapeDtypeStruct((items, hid), F32),
             jax.ShapeDtypeStruct((ny, width, hid), BF),
         ] + [jax.ShapeDtypeStruct((items, width), F32)] * ny,
-        in_specs=[SMEM] + [VMEM] * (ny + 2 * nx),
+        in_specs=[SMEM] + [VMEM] * (ny + 2 * many),
         out_specs=[VMEM] * (3 + ny),
         scratch_shapes=[
             pltpu.VMEM((ny, hz, nx, in_rows, hid), BF),
@@ -109,19 +116,21 @@
 
         def level(l, carry):
             code_row, code_col = codes_ref[pl.ds(l, 1), :], col_ref[l]
-            own_row, own_col = code_row // rows_own, code_col // rows_own
+            own_row, _ = split(code_row, rows_own)
+            own_col, row_col = split(code_col, rows_own)
             first = lax.broadcasted_iota(I32, (items, items), 0)
             second = lax.broadcasted_iota(I32, (items, items), 1)
             before = jnp.where(second < first, jnp.where(own_col == own_row, 1.0, 0.0), 0.0)
             rank = jnp.sum(before, axis=1, keepdims=True).astype(I32)
             slot_ref[l] = own_col * cap + rank
-            section, rest = own_col // (nz * nx), own_col % (nz * nx)
+            section, rest = split(own_col, nz * nx)
             spot = (rest * ns + section) * cap + rank
-            value = (code_col % rows_own + 1).astype(F32)
+            value = (row_col + 1).astype(F32)
             lanes = lax.broadcasted_iota(I32, (items, slots), 1)
             want = jnp.sum(jnp.where(lanes == spot, value, 0.0), axis=0, keepdims=True).astype(I32)
-            found_ref[pl.ds(2 * l, 1), :] = (want // 32).astype(F32)
-            found_ref[pl.ds(2 * l + 1, 1), :] = (want % 32).astype(F32)
+            high, low = split(want, 32)
+            found_ref[pl.ds(2 * l, 1), :] = high.astype(F32)
+            found_ref[pl.ds(2 * l + 1, 1), :] = low.astype(F32)
             return carry
 
         lax.fori_loop(0, levels, level, 0)
@@ -286,7 +295,7 @@
 
     def kernel(order_ref, f_ref, p_ref, came_ref, om_ref, oc_ref, own_ref, *rest):
         sends, part = rest[:-1], rest[-1]
-        total = (mm(f_ref[...], p_ref[...]) + came_ref[...]).reshape(group, nx, in_rows, hid)
+        total = (mm(f_ref[...], p_ref[...]) + came_ref[...].astype(F32)).reshape(group, nx, in_rows, hid)
         outs = (om_ref[...] + oc_ref[...]).reshape(group, nx, out_rows, hid)
         for g in range(group):
             part[:, :in_rows] = total[g]
@@ -315,6 +324,26 @@
             flops=2 * nz * nx * in_rows * items * hid, bytes_accessed=8 << 20, transcendentals=0),
         name="cut_by_x",
     )(order, feats_t, pre, came, out_mine, out_came)
+
+
+def finish(parts, in_rows):
+    _, both, step = parts[0].shape
+    hid = step * len(parts)
+
+    def kernel(*refs):
+        in_ref, out_ref = refs[-2:]
+        for c, ref in enumerate(refs[:-2]):
+            total = jnp.sum(ref[...].astype(F32), axis=0)
+            in_ref[:, c * step:(c + 1) * step] = total[:in_rows]
+            out_ref[:, c * step:(c + 1) * step] = total[in_rows:]
+
+    return pl.pallas_call(
+        kernel,
+        out_shape=[jax.ShapeDtypeStruct((in_rows, hid), F32), jax.ShapeDtypeStruct((both - in_rows, hid), F32)],
+        in_specs=[VMEM] * len(parts),
+        out_specs=[VMEM] * 2,
+        name="finish",
+    )(*parts)
 
 
 def shards(features, w_in, w_out, codebook, codes, decoder_grad):
@@ -334,7 +363,10 @@
     got_z = exchange(payload, "z")
     w_z, digits = got_z[:, :in_rows + out_rows], got_z[:, in_rows + out_rows:, :slots // nz]
     feats = [features, shift(features, "y", 1), shift(features, "y", 2), shift(features, "y", -1)]
-    near = [w_z, shift(w_z, "x", 1), shift(w_z, "x", 2), shift(w_z, "x", -1)]
+    hz = nz // 2
+    from_left, from_right = shift(w_z, "x", 1), shift(w_z, "x", -1)
+    near = [w_z, from_left, from_right, shift(from_left[:hz], "x", 1), shift(from_right[hz:], "x", -1)]
+    spans = [(0, 0, 2), (1, 0, 2), (3, 0, 2), (2, 0, 1), (2, 1, 2)]
     other = [shift(block, "s", 1) for block in near]
     steps = jnp.arange(ny, dtype=I32)
     x_place = (x - steps) % nx
@@ -355,7 +387,8 @@
     picked = mm(by_sx.reshape(-1, slots // nz), mine.astype(BF)).reshape(ns, nx, nz, -1, cap)
     picked = jnp.transpose(picked, (3, 0, 2, 1, 4)).reshape(-1, slots).astype(jnp.int32)
     asked = (picked[0::2] * 32 + picked[1::2] - 1)[:levels].reshape(levels, -1, 128)
-    rows_back = exchange(pick(asked, codebook, owners), OWN)
+    chosen = pick(asked, codebook, owners)
+    rows_back = exchange(chosen, OWN)
     words = [
         mm(
             (slot_list[l][:, None] == slot_ids[None, :]).astype(BF),
@@ -365,7 +398,7 @@
     ]
 
     hidden, slope, w_out_all, *lat = encode(
-        feats, near, other, jnp.concatenate([x_place, y_place, y_send]), in_rows, out_rows
+        feats, near, other, spans, jnp.concatenate([x_place, y_place, y_send]), in_rows, out_rows
     )
     far = shift(lat[2], "y", 2)
     fwd = shift(lat[1], "y", 1)
@@ -385,12 +418,7 @@
     latent_grad = (
         (decoder_grad.astype(F32) + 2.0 * BETA * pull_sum) / jnp.sqrt(F32(items_all))
     ).astype(BF)
-    grads = [
-        latent_grad,
-        shift(latent_grad, "y", 1),
-        shift(latent_grad, "y", 2),
-        shift(latent_grad, "y", -1),
-    ]
+    grads = [latent_grad, shift(latent_grad, "y", 1), shift(latent_grad, "y", 2), shift(latent_grad, "y", -1)]
     incoming = exchange(jnp.concatenate(outgoing, axis=1), OWN)
     code_sums = collect(asked, incoming, rows_own)
 
@@ -401,10 +429,10 @@
     there_rows = feats_there.reshape(hy * depth, items)
     sends = []
     for c in range(pieces):
-        there = mm(there_rows, pre_grad[:, c * step:(c + 1) * step])
+        there = mm(there_rows, pre_grad[:, c * step:(c + 1) * step]).astype(BF)
         came = shift(there, "s", 1)
         sends.append(cut_by_x(feats_here, pre_grad, came, out_part, out_came, x_send, nz, nx, c))
-    in_list, out_list = [], []
+    over_z = []
     for c in range(pieces):
         own, to_1, to_2, to_3 = sends[c]
         sum_x = (
@@ -413,11 +441,9 @@
             + shift(to_2, "x", 2).astype(F32)
             + shift(to_3, "x", -1).astype(F32)
         )
-        over_z = exchange(sum_x.astype(BF), "z")
-        sum_z = jnp.sum(over_z.astype(F32), axis=0)
-        in_list.append(sum_z[:in_rows])
-        out_list.append(sum_z[in_rows:])
-    return (jnp.concatenate(in_list, axis=1), jnp.concatenate(out_list, axis=1), code_sums)
+        over_z.append(exchange(sum_x.astype(BF), "z"))
+    in_grad, out_grad = finish(over_z, in_rows)
+    return (in_grad, out_grad, code_sums)
 
 
 def solution(mesh):

time: 223 us -> 219 us (0.982)
  waiting for transfers between devices: 69.2 us -> 61.9 us
  starting transfers between devices: 56.1 us -> 58.8 us
    ppermute x29 -> x31, waiting for transfers between devices: 58.7 us -> 49.4 us  [shift(): lax.ppermute(value, axis, [(i, (i + by) % size) for i in range(size)])]
    ppermute x29 -> x31, starting transfers between devices: 33.4 us -> 36 us  [shift(): lax.ppermute(value, axis, [(i, (i + by) % size) for i in range(size)])]
    unnamed x33 -> x39, local copies, waits for them, and re-layouts: 4.42 us -> 5.65 us
  transfers between devices with their start and end apart: 33 -> 35, of which waited for: 12 -> 12; matrix products, arithmetic and copies ran while one was open for 6% -> 7% of each run, Pallas kernels for 16% -> 18%
where the time goes in v1:
time: 219 us; the launch traced here: 217 us
  waiting for transfers between devices  61.9 us (28%)
  starting transfers between devices  58.8 us (27%)
  Pallas kernels  45.1 us (21%)
  blocking collectives  28.8 us (13%)
  local copies, waits for them, and re-layouts  9.56 us (4%)
  matrix products  7.28 us (3%)
  other arithmetic  4.51 us (2%)
    ppermute x31, waiting for transfers between devices, shift(): lax.ppermute(value, axis, [(i, (i + by) % size) for i in range(size)])  49.4 us
    ppermute x31, starting transfers between devices, shift(): lax.ppermute(value, axis, [(i, (i + by) % size) for i in range(size)])  36 us
    all_to_all x1, blocking collectives, exchange(): return lax.all_to_all(value, axis, split_axis=0, concat_axis=0, tiled=True)  28.8 us
    all_to_all x4, starting transfers between devices, exchange(): return lax.all_to_all(value, axis, split_axis=0, concat_axis=0, tiled=True)  22.8 us
    all_to_all x4, waiting for transfers between devices, exchange(): return lax.all_to_all(value, axis, split_axis=0, concat_axis=0, tiled=True)  12.4 us
    pallas_call x2, Pallas kernels, cut_by_x(): pl.pallas_call(kernel, out_shape=[jax.ShapeDtypeStruct((nz, both, hid), F...  9.29 us
    pallas_call x1, Pallas kernels, pick(): pl.pallas_call(kernel, out_shape=jax.ShapeDtypeStruct((owners, levels * c...  7.35 us
    pallas_call x1, Pallas kernels, encode(): pl.pallas_call(kernel, out_shape=[jax.ShapeDtypeStruct((items, hid), BF),...  7.32 us
  transfers between devices with their start and end apart: 35, of which 12 were waited for; matrix products, arithmetic and copies ran while one was open for 7% of the time, Pallas kernels for 18%

profile of v1, /device:TPU:8, one launch (start us, length us, event | category | flops | bytes accessed | tf_op | source)
XLA Modules:
  0.0 216.9 jit_solution(730942168563104151)
XLA Ops:
  0.6 4.3 %ask.1 = (s32[3,512,1]{2,1,0:T(8,128)}, bf16[8,80,512]{2,1,0:T(8,128)(2,1)}) custom-call(s32[3,512]{1,0:T(4,128)} %codes_ref.1, bf16[64,512]{1,0:T(8,128)(2,1)} %wi_ref.1, bf16[8,512]{1,0:T(8,128)(2,1)} %wo_ref.1), custom_call_target="tpu_custom_call" | custom-call | tf_op jit(solution)/shard_map/ask/pallas_call | solution.py:143
  4.9 28.8 %all_to_all.25 = bf16[8,80,512]{2,1,0:T(8,128)(2,1)S(1)} all-to-all(bf16[8,80,512]{2,1,0:T(8,128)(2,1)} %get-tuple-element.30), channel_id=1, replica_groups=mesh['s'=2,'z'=8,'x'=4,'y'=4] {'z'}, dimensions={0} | all-to-all | bytes 1310720 | tf_op jit(solution)/shard_map/all_to_all | solution.py:23
  33.7 3.0 %collective-permute-start.16 = (bf16[8,8,128]{2,1,0:T(8,128)(2,1)S(1)}, bf16[8,8,128]{2,1,0:T(8,128)(2,1)S(1)}, u32[]{:S(2)}, u32[]{:S(2)}) collective-permute-start(bf16[8,8,128]{2,1,0:T(8,128)(2,1)S(1)} %slice.63), channel_id=1, source_target_pairs={{0,8},{4,12},{8,0},{12,4},{1,9},{5,13},{9,1},{13,5},{2,10},{6,14},... | collective-permute-start | bytes 49160 | tf_op jit(solution)/shard_map/ppermute | solution.py:19
  36.7 0.6 collective-permute-start.15
  37.3 2.6 %collective-permute-start.17 = (bf16[8,8,128]{2,1,0:T(8,128)(2,1)S(1)}, bf16[8,8,128]{2,1,0:T(8,128)(2,1)S(1)}, u32[]{:S(2)}, u32[]{:S(2)}) collective-permute-start(bf16[8,8,128]{2,1,0:T(8,128)(2,1)S(1)} %slice.63), channel_id=1, source_target_pairs={{0,12},{4,0},{8,4},{12,8},{1,13},{5,1},{9,5},{13,9},{2,14},{6,2},{... | collective-permute-start | bytes 49160 | tf_op jit(solution)/shard_map/ppermute | solution.py:19
  40.4 2.6 %collective-permute-start.1 = (bf16[512,1024]{1,0:T(8,128)(2,1)}, bf16[512,1024]{1,0:T(8,128)(2,1)}, u32[]{:S(2)}, u32[]{:S(2)}) collective-permute-start(bf16[512,1024]{1,0:T(8,128)(2,1)} %refs_0_.3), channel_id=1, source_target_pairs={{0,2},{1,3},{2,0},{3,1},{4,6},{5,7},{6,4},{7,5},{8,10},{9,11},{10,... | collective-permute-start | bytes 3145736 | tf_op jit(solution)/shard_map/ppermute | solution.py:19
  43.0 1.9 collective-permute-start
  45.1 1.2 collective-permute-done.18
  47.1 0.6 copy.13
  47.7 7.3 %pick.1 = bf16[64,48,128]{2,1,0:T(8,128)(2,1)} custom-call(s32[3,8,128]{2,1,0:T(8,128)} %bitcast.51, bf16[3,1024,128]{2,1,0:T(8,128)(2,1)} %book_ref.1), custom_call_target="tpu_custom_call" | custom-call | tf_op jit(solution)/shard_map/pick/pallas_call | solution.py:177
  55.0 5.5 %all-to-all-start.1 = ((bf16[64,48,128]{2,1,0:T(8,128)(2,1)}), bf16[64,48,128]{2,1,0:T(8,128)(2,1)}, u32[]{:S(2)}, u32[]{:S(2)}) async-start(bf16[64,48,128]{2,1,0:T(8,128)(2,1)} %pick.1), calls=%async_computation.1 | async-start | bytes 1572864 | tf_op jit(solution)/shard_map/all_to_all | solution.py:23
  60.5 2.7 %collective-permute-start.4 = (bf16[8,72,512]{2,1,0:T(8,128)(2,1)S(1)}, bf16[8,72,512]{2,1,0:T(8,128)(2,1)S(1)}, u32[]{:S(2)}, u32[]{:S(2)}) collective-permute-start(bf16[8,72,512]{2,1,0:T(8,128)(2,1)S(1)} %slice.60.refs_4_), channel_id=1, source_target_pairs={{0,12},{4,0},{8,4},{12,8},{1,13},{5,1},{9,5},{13,9},{2,14},{6,2},{... | collective-permute-start | bytes 1769480 | tf_op jit(solution)/shard_map/ppermute | solution.py:19
  63.2 20.6 %collective-permute-done.4.refs_6_ = bf16[8,72,512]{2,1,0:T(8,128)(2,1)S(1)} collective-permute-done((bf16[8,72,512]{2,1,0:T(8,128)(2,1)S(1)}, bf16[8,72,512]{2,1,0:T(8,128)(2,1)S(1)}, u32[]{:S(2)}, u32[]{:S(2)}) %collective-permute-start.4) | collective-permute-done | bytes 589856 | tf_op jit(solution)/shard_map/ppermute | solution.py:19
  83.8 3.3 %collective-permute-start.6 = (bf16[4,72,512]{2,1,0:T(8,128)(2,1)S(1)}, bf16[4,72,512]{2,1,0:T(8,128)(2,1)S(1)}, u32[]{:S(2)}, u32[]{:S(2)}) collective-permute-start(bf16[4,72,512]{2,1,0:T(8,128)(2,1)S(1)} %slice.62), channel_id=1, source_target_pairs={{0,12},{4,0},{8,4},{12,8},{1,13},{5,1},{9,5},{13,9},{2,14},{6,2},{... | collective-permute-start | bytes 884744 | tf_op jit(solution)/shard_map/ppermute | solution.py:19
  87.1 0.7 slice.61
  87.9 0.5 collective-permute-start.9
  88.7 4.5 %collective-permute-done.6.refs_8_ = bf16[4,72,512]{2,1,0:T(8,128)(2,1)S(1)} collective-permute-done((bf16[4,72,512]{2,1,0:T(8,128)(2,1)S(1)}, bf16[4,72,512]{2,1,0:T(8,128)(2,1)S(1)}, u32[]{:S(2)}, u32[]{:S(2)}) %collective-permute-start.6) | collective-permute-done | bytes 294944 | tf_op jit(solution)/shard_map/ppermute | solution.py:19
  93.3 4.4 %collective-permute-done.5.refs_7_ = bf16[4,72,512]{2,1,0:T(8,128)(2,1)S(1)} collective-permute-done((bf16[4,72,512]{2,1,0:T(8,128)(2,1)}, bf16[4,72,512]{2,1,0:T(8,128)(2,1)S(1)}, u32[]{:S(2)}, u32[]{:S(2)}) %collective-permute-start.5) | collective-permute-done | bytes 294944 | tf_op jit(solution)/shard_map/ppermute | solution.py:19
  97.7 1.4 slice_reduce_fusion
  99.1 5.8 %turn.1 = (bf16[2,1024,512]{2,1,0:T(8,128)(2,1)}, bf16[2,1024,512]{2,1,0:T(8,128)(2,1)}) custom-call(s32[4]{0:T(128)} %copy-done.17, bf16[512,1024]{1,0:T(8,128)(2,1)} %refs_0_.3, bf16[512,1024]{1,0:T(8,128)(2,1)} %collective-permute-done.refs_1_, bf16[512,1024]{1,0:T(8,128)(2,1)} %collective-permute-done.1.refs_2_, ...), custom_call_target="tpu_custom_call" | custom-call | bytes 8388608 | tf_op jit(solution)/shard_map/turn/pallas_call | solution.py:244
  105.0 7.3 %encode.1 = (bf16[512,512]{1,0:T(8,128)(2,1)S(1)}, f32[512,512]{1,0:T(8,128)}, bf16[4,128,512]{2,1,0:T(8,128)(2,1)S(1)}, f32[512,128]{1,0:T(8,128)S(1)}, f32[512...) custom-call(s32[12]{0:T(128)S(1)} %pad_add_fusion.place_ref, bf16[512,1024]{1,0:T(8,128)(2,1)} %refs_0_.3, ...), custom_call_target="tpu_custom_call" | custom-call | flops 2415919104 | bytes 12582912 | tf_op jit(solution)/shard_map/encode/pallas_call | solution.py:79
  112.3 0.8 copy-done
  113.1 0.8 copy-done.1
  113.9 2.0 collective-permute-start.13
  115.9 1.3 collective-permute-start.14
  117.2 1.3 fusion.35
  118.5 0.5 fusion.2
  119.0 0.5 fusion.1
  119.5 0.5 fusion
  120.0 3.2 %collective-permute-done.12 = f32[512,128]{1,0:T(8,128)S(1)} collective-permute-done((f32[512,128]{1,0:T(8,128)}, f32[512,128]{1,0:T(8,128)S(1)}, u32[]{:S(2)}, u32[]{:S(2)}) %collective-permute-start.12) | collective-permute-done | bytes 262176 | tf_op jit(solution)/shard_map/ppermute | solution.py:19
  123.3 6.2 %collective-permute-done.14 = f32[512,128]{1,0:T(8,128)S(1)} collective-permute-done((f32[512,128]{1,0:T(8,128)}, f32[512,128]{1,0:T(8,128)S(1)}, u32[]{:S(2)}, u32[]{:S(2)}) %collective-permute-start.14) | collective-permute-done | bytes 262176 | tf_op jit(solution)/shard_map/ppermute | solution.py:19
  131.0 1.0 collective-permute-start.21
  132.0 1.4 collective-permute-start.20
  133.4 2.5 %collective-permute-start.19 = (bf16[512,128]{1,0:T(8,128)(2,1)S(1)}, bf16[512,128]{1,0:T(8,128)(2,1)S(1)}, u32[]{:S(2)}, u32[]{:S(2)}) collective-permute-start(bf16[512,128]{1,0:T(8,128)(2,1)S(1)} %get-tuple-element.58.refs_0_), channel_id=1, source_target_pairs={{0,1},{1,2},{2,3},{3,0},{4,5},{5,6},{6,7},{7,4},{8,9},{9,10},{10,1... | collective-permute-start | bytes 393224 | tf_op jit(solution)/shard_map/ppermute | solution.py:19
  135.9 0.9 pad_maximum_fusion
  136.9 7.5 %all-to-all-start.4 = ((bf16[64,48,128]{2,1,0:T(8,128)(2,1)}), bf16[64,48,128]{2,1,0:T(8,128)(2,1)S(1)}, u32[]{:S(2)}, u32[]{:S(2)}) async-start(bf16[64,48,128]{2,1,0:T(8,128)(2,1)} %pad_maximum_fusion), calls=%async_computation.4 | async-start | bytes 1572864 | tf_op jit(solution)/shard_map/all_to_all | solution.py:23
  144.5 0.6 copy-done.14
  145.2 3.8 %back.1 = (bf16[512,512]{1,0:T(8,128)(2,1)}, f32[4,128,512]{2,1,0:T(8,128)}) custom-call(s32[4]{0:T(128)} %copy-done.17, bf16[512,128]{1,0:T(8,128)(2,1)} %copy-done.12, bf16[512,128]{1,0:T(8,128)(2,1)} %copy-done.16, bf16[512,128]{1,0:T(8,128)(2,1)} %copy-done.15, bf16[512,128]{1,0:T(8,128)(2,1)} %copy-done.14, bf16[512,512]{1,0:T(8,128)(2,1)} %copy-done, ...), custom_call_target="tpu_custom_call" | custom-call | flops 536870912 | bytes 4194304 | tf_op jit(solution)/shard_map/back/pallas_call | solution.py:268
  149.1 2.4 %convolution_convert_fusion = bf16[2048,256]{1,0:T(8,128)(2,1)S(1)} fusion(bf16[2048,512]{1,0:T(8,128)(2,1)} %bitcast.53, bf16[512,512]{1,0:T(8,128)(2,1)} %get-tuple-element.42.p_ref), kind=kOutput, calls=%fused_computation | convolution fusion | flops 537395200 | bytes 3407872 | tf_op jit(solution)/shard_map/dot_general | solution.py:27
  151.6 0.5 collective-permute-start.23
  152.1 1.7 convolution_convert_fusion.1
  153.9 0.5 and_select_fusion.3.order_ref
  154.4 1.3 collective-permute-done.23
  155.8 1.0 copy-done.3
  156.8 4.6 %cut_by_x.3 = (f32[8,72,256]{2,1,0:T(8,128)}, bf16[8,72,256]{2,1,0:T(8,128)(2,1)}, bf16[8,72,256]{2,1,0:T(8,128)(2,1)}, bf16[8,72,256]{2,1,0:T(8,128)(2,1)}) custom-call(s32[4]{0:T(128)} %and_select_fusion.3.order_ref, bf16[2048,512]{1,0:T(8,128)(2,1)} %bitcast.39, bf16[512,512]{1,0:T(8,128)(2,1)} %get-tuple-element.42.p_ref, bf16[2048,256]{1,0:T(8,128)(2,1)} %copy-done.9, ...), custom_call_target="tpu_custom_call" | custom-call | flops 536870912 | bytes 8388608 | tf_op jit(solution)/shard_map/cut_by_x/pallas_call | solution.py:308
  161.4 1.4 collective-permute-start.28
  162.8 2.7 %collective-permute-start.29 = (bf16[8,72,256]{2,1,0:T(8,128)(2,1)}, bf16[8,72,256]{2,1,0:T(8,128)(2,1)}, u32[]{:S(2)}, u32[]{:S(2)}) collective-permute-start(bf16[8,72,256]{2,1,0:T(8,128)(2,1)} %get-tuple-element.51), channel_id=1, source_target_pairs={{0,8},{4,12},{8,0},{12,4},{1,9},{5,13},{9,1},{13,5},{2,10},{6,14},... | collective-permute-start | bytes 884744 | tf_op jit(solution)/shard_map/ppermute | solution.py:19
  165.5 1.5 collective-permute-start.30
  167.0 1.0 copy-done.8
  167.9 4.6 %cut_by_x.2 = (f32[8,72,256]{2,1,0:T(8,128)}, bf16[8,72,256]{2,1,0:T(8,128)(2,1)}, bf16[8,72,256]{2,1,0:T(8,128)(2,1)}, bf16[8,72,256]{2,1,0:T(8,128)(2,1)}) custom-call(s32[4]{0:T(128)} %and_select_fusion.3.order_ref, bf16[2048,512]{1,0:T(8,128)(2,1)} %bitcast.40, bf16[512,512]{1,0:T(8,128)(2,1)} %get-tuple-element.42.p_ref, bf16[2048,256]{1,0:T(8,128)(2,1)} %copy-done.8, ...), custom_call_target="tpu_custom_call" | custom-call | flops 536870912 | bytes 8388608 | tf_op jit(solution)/shard_map/cut_by_x/pallas_call | solution.py:308
  172.6 0.6 collective-permute-start.24
  173.2 0.9 collective-permute-start.25
  174.1 1.9 collective-permute-start.26
  176.0 4.0 %collective-permute-done.29 = bf16[8,72,256]{2,1,0:T(8,128)(2,1)} collective-permute-done((bf16[8,72,256]{2,1,0:T(8,128)(2,1)}, bf16[8,72,256]{2,1,0:T(8,128)(2,1)}, u32[]{:S(2)}, u32[]{:S(2)}) %collective-permute-start.29) | collective-permute-done | bytes 294944 | tf_op jit(solution)/shard_map/ppermute | solution.py:19
  180.3 1.9 add_convert_fusion
  182.2 6.4 %all-to-all-start.3 = ((bf16[8,72,256]{2,1,0:T(8,128)(2,1)}), bf16[8,72,256]{2,1,0:T(8,128)(2,1)S(1)}, u32[]{:S(2)}, u32[]{:S(2)}) async-start(bf16[8,72,256]{2,1,0:T(8,128)(2,1)} %add_convert_fusion), calls=%async_computation.3 | async-start | bytes 589824 | tf_op jit(solution)/shard_map/all_to_all | solution.py:23
  188.6 3.6 %collective-permute-done.25 = bf16[8,72,256]{2,1,0:T(8,128)(2,1)S(1)} collective-permute-done((bf16[8,72,256]{2,1,0:T(8,128)(2,1)}, bf16[8,72,256]{2,1,0:T(8,128)(2,1)S(1)}, u32[]{:S(2)}, u32[]{:S(2)}) %collective-permute-start.25) | collective-permute-done | bytes 294944 | tf_op jit(solution)/shard_map/ppermute | solution.py:19
  192.2 0.9 add_convert_fusion.1
  193.1 7.1 %all-to-all-done.3.refs_1_ = bf16[8,72,256]{2,1,0:T(8,128)(2,1)S(1)} async-done(((bf16[8,72,256]{2,1,0:T(8,128)(2,1)}), bf16[8,72,256]{2,1,0:T(8,128)(2,1)S(1)}, u32[]{:S(2)}, u32[]{:S(2)}) %all-to-all-start.3) | async-done | bytes 294944 | tf_op jit(solution)/shard_map/all_to_all | solution.py:23
  200.2 3.4 %all-to-all-start.2 = ((bf16[8,72,256]{2,1,0:T(8,128)(2,1)}), bf16[8,72,256]{2,1,0:T(8,128)(2,1)S(1)}, u32[]{:S(2)}, u32[]{:S(2)}) async-start(bf16[8,72,256]{2,1,0:T(8,128)(2,1)} %add_convert_fusion.1), calls=%async_computation.2 | async-start | bytes 589824 | tf_op jit(solution)/shard_map/all_to_all | solution.py:23
  203.6 5.4 %collect.1 = f32[3,1024,128]{2,1,0:T(8,128)} custom-call(s32[3,8,128]{2,1,0:T(8,128)} %bitcast.52, bf16[64,48,128]{2,1,0:T(8,128)(2,1)} %copy-done.4), custom_call_target="tpu_custom_call" | custom-call | tf_op jit(solution)/shard_map/collect/pallas_call | solution.py:210
  209.1 5.3 %all-to-all-done.2.refs_0_ = bf16[8,72,256]{2,1,0:T(8,128)(2,1)S(1)} async-done(((bf16[8,72,256]{2,1,0:T(8,128)(2,1)}), bf16[8,72,256]{2,1,0:T(8,128)(2,1)S(1)}, u32[]{:S(2)}, u32[]{:S(2)}) %all-to-all-start.2) | async-done | bytes 294944 | tf_op jit(solution)/shard_map/all_to_all | solution.py:23
  214.4 0.7 copy-done.7
  215.1 1.8 finish.1
  (88 shorter events, 4.0 us)
Async XLA Ops:
  33.7 9.3 %collective-permute-start.16 = (bf16[8,8,128]{2,1,0:T(8,128)(2,1)S(1)}, bf16[8,8,128]{2,1,0:T(8,128)(2,1)S(1)}, u32[]{:S(2)}, u32[]{:S(2)}) collective-permute-start(bf16[8,8,128]{2,1,0:T(8,128)(2,1)S(1)} %slice.63), channel_id=1, source_target_pairs={{0,8},{4,12},{8,0},{12,4},{1,9},{5,13},{9,1},{13,5},{2,10},{6,14},... | collective-permute-start | bytes 49160 | tf_op jit(solution)/shard_map/ppermute | solution.py:19
  36.7 8.2 %collective-permute-start.15 = (bf16[8,8,128]{2,1,0:T(8,128)(2,1)S(1)}, bf16[8,8,128]{2,1,0:T(8,128)(2,1)S(1)}, u32[]{:S(2)}, u32[]{:S(2)}) collective-permute-start(bf16[8,8,128]{2,1,0:T(8,128)(2,1)S(1)} %slice.63), channel_id=1, source_target_pairs={{0,4},{4,8},{8,12},{12,0},{1,5},{5,9},{9,13},{13,1},{2,6},{6,10},{... | collective-permute-start | bytes 49160 | tf_op jit(solution)/shard_map/ppermute | solution.py:19
  37.3 7.6 %collective-permute-start.17 = (bf16[8,8,128]{2,1,0:T(8,128)(2,1)S(1)}, bf16[8,8,128]{2,1,0:T(8,128)(2,1)S(1)}, u32[]{:S(2)}, u32[]{:S(2)}) collective-permute-start(bf16[8,8,128]{2,1,0:T(8,128)(2,1)S(1)} %slice.63), channel_id=1, source_target_pairs={{0,12},{4,0},{8,4},{12,8},{1,13},{5,1},{9,5},{13,9},{2,14},{6,2},{... | collective-permute-start | bytes 49160 | tf_op jit(solution)/shard_map/ppermute | solution.py:19
  40.0 47.9 %collective-permute-start.2 = (bf16[512,1024]{1,0:T(8,128)(2,1)}, bf16[512,1024]{1,0:T(8,128)(2,1)}, u32[]{:S(2)}, u32[]{:S(2)}) collective-permute-start(bf16[512,1024]{1,0:T(8,128)(2,1)} %refs_0_.3), channel_id=1, source_target_pairs={{0,3},{1,0},{2,1},{3,2},{4,7},{5,4},{6,5},{7,6},{8,11},{9,8},{10,9... | collective-permute-start | bytes 3145736 | tf_op jit(solution)/shard_map/ppermute | solution.py:19
  40.4 47.5 %collective-permute-start.1 = (bf16[512,1024]{1,0:T(8,128)(2,1)}, bf16[512,1024]{1,0:T(8,128)(2,1)}, u32[]{:S(2)}, u32[]{:S(2)}) collective-permute-start(bf16[512,1024]{1,0:T(8,128)(2,1)} %refs_0_.3), channel_id=1, source_target_pairs={{0,2},{1,3},{2,0},{3,1},{4,6},{5,7},{6,4},{7,5},{8,10},{9,11},{10,... | collective-permute-start | bytes 3145736 | tf_op jit(solution)/shard_map/ppermute | solution.py:19
  43.0 45.4 %collective-permute-start = (bf16[512,1024]{1,0:T(8,128)(2,1)}, bf16[512,1024]{1,0:T(8,128)(2,1)}, u32[]{:S(2)}, u32[]{:S(2)}) collective-permute-start(bf16[512,1024]{1,0:T(8,128)(2,1)} %refs_0_.3), channel_id=1, source_target_pairs={{0,1},{1,2},{2,3},{3,0},{4,5},{5,6},{6,7},{7,4},{8,9},{9,10},{10,1... | collective-permute-start | bytes 3145736 | tf_op jit(solution)/shard_map/ppermute | solution.py:19
  45.0 1.3 collective-permute-start.18
  55.0 62.2 %all-to-all-start.1 = ((bf16[64,48,128]{2,1,0:T(8,128)(2,1)}), bf16[64,48,128]{2,1,0:T(8,128)(2,1)}, u32[]{:S(2)}, u32[]{:S(2)}) async-start(bf16[64,48,128]{2,1,0:T(8,128)(2,1)} %pick.1), calls=%async_computation.1 | async-start | bytes 1572864 | tf_op jit(solution)/shard_map/all_to_all | solution.py:23
  60.5 23.3 %collective-permute-start.4 = (bf16[8,72,512]{2,1,0:T(8,128)(2,1)S(1)}, bf16[8,72,512]{2,1,0:T(8,128)(2,1)S(1)}, u32[]{:S(2)}, u32[]{:S(2)}) collective-permute-start(bf16[8,72,512]{2,1,0:T(8,128)(2,1)S(1)} %slice.60.refs_4_), channel_id=1, source_target_pairs={{0,12},{4,0},{8,4},{12,8},{1,13},{5,1},{9,5},{13,9},{2,14},{6,2},{... | collective-permute-start | bytes 1769480 | tf_op jit(solution)/shard_map/ppermute | solution.py:19
  63.2 23.9 %collective-permute-start.3 = (bf16[8,72,512]{2,1,0:T(8,128)(2,1)S(1)}, bf16[8,72,512]{2,1,0:T(8,128)(2,1)S(1)}, u32[]{:S(2)}, u32[]{:S(2)}) collective-permute-start(bf16[8,72,512]{2,1,0:T(8,128)(2,1)S(1)} %slice.60.refs_4_), channel_id=1, source_target_pairs={{0,4},{4,8},{8,12},{12,0},{1,5},{5,9},{9,13},{13,1},{2,6},{6,10},{... | collective-permute-start | bytes 1769480 | tf_op jit(solution)/shard_map/ppermute | solution.py:19
  83.8 9.4 %collective-permute-start.6 = (bf16[4,72,512]{2,1,0:T(8,128)(2,1)S(1)}, bf16[4,72,512]{2,1,0:T(8,128)(2,1)S(1)}, u32[]{:S(2)}, u32[]{:S(2)}) collective-permute-start(bf16[4,72,512]{2,1,0:T(8,128)(2,1)S(1)} %slice.62), channel_id=1, source_target_pairs={{0,12},{4,0},{8,4},{12,8},{1,13},{5,1},{9,5},{13,9},{2,14},{6,2},{... | collective-permute-start | bytes 884744 | tf_op jit(solution)/shard_map/ppermute | solution.py:19
  87.9 9.7 %collective-permute-start.5 = (bf16[4,72,512]{2,1,0:T(8,128)(2,1)}, bf16[4,72,512]{2,1,0:T(8,128)(2,1)S(1)}, u32[]{:S(2)}, u32[]{:S(2)}) collective-permute-start(bf16[4,72,512]{2,1,0:T(8,128)(2,1)} %slice.61), channel_id=1, source_target_pairs={{0,4},{4,8},{8,12},{12,0},{1,5},{5,9},{9,13},{13,1},{2,6},{6,10},{... | collective-permute-start | bytes 884744 | tf_op jit(solution)/shard_map/ppermute | solution.py:19
  87.9 17.0 %collective-permute-start.7 = (bf16[8,72,512]{2,1,0:T(8,128)(2,1)S(1)}, bf16[8,72,512]{2,1,0:T(8,128)(2,1)S(1)}, u32[]{:S(2)}, u32[]{:S(2)}) collective-permute-start(bf16[8,72,512]{2,1,0:T(8,128)(2,1)S(1)} %slice.60.refs_4_), channel_id=1, source_target_pairs={{0,128},{128,0},{1,129},{129,1},{2,130},{130,2},{3,131},{131,3},{4... | collective-permute-start | bytes 1769480 | tf_op jit(solution)/shard_map/ppermute | solution.py:19
  87.9 17.1 %collective-permute-start.9 = (bf16[8,72,512]{2,1,0:T(8,128)(2,1)S(1)}, bf16[8,72,512]{2,1,0:T(8,128)(2,1)}, u32[]{:S(2)}, u32[]{:S(2)}) collective-permute-start(bf16[8,72,512]{2,1,0:T(8,128)(2,1)S(1)} %collective-permute-done.4.refs_6_), channel_id=1, source_target_pairs={{0,128},{128,0},{1,129},{129,1},{2,130},{130,2},{3,131},{131,3},{4... | collective-permute-start | bytes 1769480 | tf_op jit(solution)/shard_map/ppermute | solution.py:19
  88.4 16.6 %collective-permute-start.8 = (bf16[8,72,512]{2,1,0:T(8,128)(2,1)S(1)}, bf16[8,72,512]{2,1,0:T(8,128)(2,1)}, u32[]{:S(2)}, u32[]{:S(2)}) collective-permute-start(bf16[8,72,512]{2,1,0:T(8,128)(2,1)S(1)} %collective-permute-done.3.refs_5_), channel_id=1, source_target_pairs={{0,128},{128,0},{1,129},{129,1},{2,130},{130,2},{3,131},{131,3},{4... | collective-permute-start | bytes 1769480 | tf_op jit(solution)/shard_map/ppermute | solution.py:19
  88.7 10.4 %copy-start.17 = (s32[4]{0:T(128)}, s32[4]{0:T(128)S(1)}, u32[]{:S(2)}) copy-start(s32[4]{0:T(128)S(1)} %get-tuple-element.69.place_ref) | copy-start | bytes 52
  93.3 11.7 %collective-permute-start.11 = (bf16[4,72,512]{2,1,0:T(8,128)(2,1)S(1)}, bf16[4,72,512]{2,1,0:T(8,128)(2,1)S(1)}, u32[]{:S(2)}, u32[]{:S(2)}) collective-permute-start(bf16[4,72,512]{2,1,0:T(8,128)(2,1)S(1)} %collective-permute-done.6.refs_8_), channel_id=1, source_target_pairs={{0,128},{128,0},{1,129},{129,1},{2,130},{130,2},{3,131},{131,3},{4... | collective-permute-start | bytes 884744 | tf_op jit(solution)/shard_map/ppermute | solution.py:19
  97.6 7.3 %collective-permute-start.10 = (bf16[4,72,512]{2,1,0:T(8,128)(2,1)S(1)}, bf16[4,72,512]{2,1,0:T(8,128)(2,1)}, u32[]{:S(2)}, u32[]{:S(2)}) collective-permute-start(bf16[4,72,512]{2,1,0:T(8,128)(2,1)S(1)} %collective-permute-done.5.refs_7_), channel_id=1, source_target_pairs={{0,128},{128,0},{1,129},{129,1},{2,130},{130,2},{3,131},{131,3},{4... | collective-permute-start | bytes 884744 | tf_op jit(solution)/shard_map/ppermute | solution.py:19
  112.3 0.8 copy-start
  113.1 0.8 copy-start.1
  113.9 9.4 %collective-permute-start.12 = (f32[512,128]{1,0:T(8,128)}, f32[512,128]{1,0:T(8,128)S(1)}, u32[]{:S(2)}, u32[]{:S(2)}) collective-permute-start(f32[512,128]{1,0:T(8,128)} %get-tuple-element.32), channel_id=1, source_target_pairs={{0,1},{1,2},{2,3},{3,0},{4,5},{5,6},{6,7},{7,4},{8,9},{9,10},{10,1... | collective-permute-start | bytes 786440 | tf_op jit(solution)/shard_map/ppermute | solution.py:19
  113.9 9.4 %collective-permute-start.13 = (f32[512,128]{1,0:T(8,128)}, f32[512,128]{1,0:T(8,128)S(1)}, u32[]{:S(2)}, u32[]{:S(2)}) collective-permute-start(f32[512,128]{1,0:T(8,128)} %get-tuple-element.33), channel_id=1, source_target_pairs={{0,3},{1,0},{2,1},{3,2},{4,7},{5,4},{6,5},{7,6},{8,11},{9,8},{10,9... | collective-permute-start | bytes 786440 | tf_op jit(solution)/shard_map/ppermute | solution.py:19
  115.9 13.6 %copy-start.13 = (bf16[512,128]{1,0:T(8,128)(2,1)S(1)}, bf16[512,128]{1,0:T(8,128)(2,1)}, u32[]{:S(2)}) copy-start(bf16[512,128]{1,0:T(8,128)(2,1)} %param.11) | copy-start | bytes 393220
  115.9 13.6 %collective-permute-start.14 = (f32[512,128]{1,0:T(8,128)}, f32[512,128]{1,0:T(8,128)S(1)}, u32[]{:S(2)}, u32[]{:S(2)}) collective-permute-start(f32[512,128]{1,0:T(8,128)} %get-tuple-element.34), channel_id=1, source_target_pairs={{0,2},{1,3},{2,0},{3,1},{4,6},{5,7},{6,4},{7,5},{8,10},{9,11},{10,... | collective-permute-start | bytes 786440 | tf_op jit(solution)/shard_map/ppermute | solution.py:19
  129.6 7.3 %copy-start.12 = (bf16[512,128]{1,0:T(8,128)(2,1)}, bf16[512,128]{1,0:T(8,128)(2,1)S(1)}, u32[]{:S(2)}) copy-start(bf16[512,128]{1,0:T(8,128)(2,1)S(1)} %get-tuple-element.58.refs_0_) | copy-start | bytes 393220
  131.0 13.4 %collective-permute-start.21 = (bf16[512,128]{1,0:T(8,128)(2,1)S(1)}, bf16[512,128]{1,0:T(8,128)(2,1)S(1)}, u32[]{:S(2)}, u32[]{:S(2)}) collective-permute-start(bf16[512,128]{1,0:T(8,128)(2,1)S(1)} %get-tuple-element.58.refs_0_), channel_id=1, source_target_pairs={{0,3},{1,0},{2,1},{3,2},{4,7},{5,4},{6,5},{7,6},{8,11},{9,8},{10,9... | collective-permute-start | bytes 393224 | tf_op jit(solution)/shard_map/ppermute | solution.py:19
  132.0 12.4 %collective-permute-start.20 = (bf16[512,128]{1,0:T(8,128)(2,1)S(1)}, bf16[512,128]{1,0:T(8,128)(2,1)S(1)}, u32[]{:S(2)}, u32[]{:S(2)}) collective-permute-start(bf16[512,128]{1,0:T(8,128)(2,1)S(1)} %get-tuple-element.58.refs_0_), channel_id=1, source_target_pairs={{0,2},{1,3},{2,0},{3,1},{4,6},{5,7},{6,4},{7,5},{8,10},{9,11},{10,... | collective-permute-start | bytes 393224 | tf_op jit(solution)/shard_map/ppermute | solution.py:19
  133.4 11.1 %collective-permute-start.19 = (bf16[512,128]{1,0:T(8,128)(2,1)S(1)}, bf16[512,128]{1,0:T(8,128)(2,1)S(1)}, u32[]{:S(2)}, u32[]{:S(2)}) collective-permute-start(bf16[512,128]{1,0:T(8,128)(2,1)S(1)} %get-tuple-element.58.refs_0_), channel_id=1, source_target_pairs={{0,1},{1,2},{2,3},{3,0},{4,5},{5,6},{6,7},{7,4},{8,9},{9,10},{10,1... | collective-permute-start | bytes 393224 | tf_op jit(solution)/shard_map/ppermute | solution.py:19
  136.9 45.3 %all-to-all-start.4 = ((bf16[64,48,128]{2,1,0:T(8,128)(2,1)}), bf16[64,48,128]{2,1,0:T(8,128)(2,1)S(1)}, u32[]{:S(2)}, u32[]{:S(2)}) async-start(bf16[64,48,128]{2,1,0:T(8,128)(2,1)} %pad_maximum_fusion), calls=%async_computation.4 | async-start | bytes 1572864 | tf_op jit(solution)/shard_map/all_to_all | solution.py:23
  144.4 0.7 copy-start.14
  144.4 0.7 copy-start.15
  144.5 0.8 copy-start.16
  149.1 2.6 %copy-start.2 = (f32[4,128,512]{2,1,0:T(8,128)S(1)}, f32[4,128,512]{2,1,0:T(8,128)}, u32[]{:S(2)}) copy-start(f32[4,128,512]{2,1,0:T(8,128)} %get-tuple-element.44) | copy-start | bytes 3145732
  149.1 3.1 %copy-start.5 = (bf16[512,512]{1,0:T(8,128)(2,1)S(1)}, bf16[512,512]{1,0:T(8,128)(2,1)}, u32[]{:S(2)}) copy-start(bf16[512,512]{1,0:T(8,128)(2,1)} %get-tuple-element.42.p_ref) | copy-start | bytes 1572868
  149.1 3.1 %copy-start.18 = (bf16[2,1024,512]{2,1,0:T(8,128)(2,1)S(1)}, bf16[2,1024,512]{2,1,0:T(8,128)(2,1)}, u32[]{:S(2)}) copy-start(bf16[2,1024,512]{2,1,0:T(8,128)(2,1)} %get-tuple-element.43) | copy-start | bytes 6291460
  151.5 2.9 %collective-permute-start.27 = (bf16[2048,256]{1,0:T(8,128)(2,1)S(1)}, bf16[2048,256]{1,0:T(8,128)(2,1)S(1)}, u32[]{:S(2)}, u32[]{:S(2)}) collective-permute-start(bf16[2048,256]{1,0:T(8,128)(2,1)S(1)} %convolution_convert_fusion), channel_id=1, source_target_pairs={{0,128},{128,0},{1,129},{129,1},{2,130},{130,2},{3,131},{131,3},{4... | collective-permute-start | bytes 3145736 | tf_op jit(solution)/shard_map/ppermute | solution.py:19
  151.6 4.1 %collective-permute-start.23 = (f32[4,128,512]{2,1,0:T(8,128)S(1)}, f32[4,128,512]{2,1,0:T(8,128)S(1)}, u32[]{:S(2)}, u32[]{:S(2)}) collective-permute-start(f32[4,128,512]{2,1,0:T(8,128)S(1)} %copy-done.2), channel_id=1, source_target_pairs={{0,128},{128,0},{1,129},{129,1},{2,130},{130,2},{3,131},{131,3},{4... | collective-permute-start | bytes 3145736 | tf_op jit(solution)/shard_map/ppermute | solution.py:19
  153.8 13.2 %collective-permute-start.22 = (bf16[2048,256]{1,0:T(8,128)(2,1)}, bf16[2048,256]{1,0:T(8,128)(2,1)S(1)}, u32[]{:S(2)}, u32[]{:S(2)}) collective-permute-start(bf16[2048,256]{1,0:T(8,128)(2,1)} %convolution_convert_fusion.1), channel_id=1, source_target_pairs={{0,128},{128,0},{1,129},{129,1},{2,130},{130,2},{3,131},{131,3},{4... | collective-permute-start | bytes 3145736 | tf_op jit(solution)/shard_map/ppermute | solution.py:19
  154.4 1.3 copy-start.9
  155.8 1.0 copy-start.3
  161.4 12.7 %collective-permute-start.28 = (bf16[8,72,256]{2,1,0:T(8,128)(2,1)}, bf16[8,72,256]{2,1,0:T(8,128)(2,1)S(1)}, u32[]{:S(2)}, u32[]{:S(2)}) collective-permute-start(bf16[8,72,256]{2,1,0:T(8,128)(2,1)} %get-tuple-element.50), channel_id=1, source_target_pairs={{0,4},{4,8},{8,12},{12,0},{1,5},{5,9},{9,13},{13,1},{2,6},{6,10},{... | collective-permute-start | bytes 884744 | tf_op jit(solution)/shard_map/ppermute | solution.py:19
  162.8 17.2 %collective-permute-start.29 = (bf16[8,72,256]{2,1,0:T(8,128)(2,1)}, bf16[8,72,256]{2,1,0:T(8,128)(2,1)}, u32[]{:S(2)}, u32[]{:S(2)}) collective-permute-start(bf16[8,72,256]{2,1,0:T(8,128)(2,1)} %get-tuple-element.51), channel_id=1, source_target_pairs={{0,8},{4,12},{8,0},{12,4},{1,9},{5,13},{9,1},{13,5},{2,10},{6,14},... | collective-permute-start | bytes 884744 | tf_op jit(solution)/shard_map/ppermute | solution.py:19
  165.5 14.8 %copy-start.11 = (f32[8,72,256]{2,1,0:T(8,128)S(1)}, f32[8,72,256]{2,1,0:T(8,128)}, u32[]{:S(2)}) copy-start(f32[8,72,256]{2,1,0:T(8,128)} %get-tuple-element.49) | copy-start | bytes 1769476
  165.5 14.8 %collective-permute-start.30 = (bf16[8,72,256]{2,1,0:T(8,128)(2,1)}, bf16[8,72,256]{2,1,0:T(8,128)(2,1)}, u32[]{:S(2)}, u32[]{:S(2)}) collective-permute-start(bf16[8,72,256]{2,1,0:T(8,128)(2,1)} %get-tuple-element.52), channel_id=1, source_target_pairs={{0,12},{4,0},{8,4},{12,8},{1,13},{5,1},{9,5},{13,9},{2,14},{6,2},{... | collective-permute-start | bytes 884744 | tf_op jit(solution)/shard_map/ppermute | solution.py:19
  167.0 1.0 copy-start.8
  172.6 19.6 %copy-start.10 = (f32[8,72,256]{2,1,0:T(8,128)S(1)}, f32[8,72,256]{2,1,0:T(8,128)}, u32[]{:S(2)}) copy-start(f32[8,72,256]{2,1,0:T(8,128)} %get-tuple-element.45) | copy-start | bytes 1769476
  172.6 16.0 %collective-permute-start.24 = (bf16[8,72,256]{2,1,0:T(8,128)(2,1)}, bf16[8,72,256]{2,1,0:T(8,128)(2,1)S(1)}, u32[]{:S(2)}, u32[]{:S(2)}) collective-permute-start(bf16[8,72,256]{2,1,0:T(8,128)(2,1)} %get-tuple-element.46), channel_id=1, source_target_pairs={{0,4},{4,8},{8,12},{12,0},{1,5},{5,9},{9,13},{13,1},{2,6},{6,10},{... | collective-permute-start | bytes 884744 | tf_op jit(solution)/shard_map/ppermute | solution.py:19
  173.2 19.0 %collective-permute-start.25 = (bf16[8,72,256]{2,1,0:T(8,128)(2,1)}, bf16[8,72,256]{2,1,0:T(8,128)(2,1)S(1)}, u32[]{:S(2)}, u32[]{:S(2)}) collective-permute-start(bf16[8,72,256]{2,1,0:T(8,128)(2,1)} %get-tuple-element.47), channel_id=1, source_target_pairs={{0,8},{4,12},{8,0},{12,4},{1,9},{5,13},{9,1},{13,5},{2,10},{6,14},... | collective-permute-start | bytes 884744 | tf_op jit(solution)/shard_map/ppermute | solution.py:19
  174.1 18.0 %collective-permute-start.26 = (bf16[8,72,256]{2,1,0:T(8,128)(2,1)}, bf16[8,72,256]{2,1,0:T(8,128)(2,1)S(1)}, u32[]{:S(2)}, u32[]{:S(2)}) collective-permute-start(bf16[8,72,256]{2,1,0:T(8,128)(2,1)} %get-tuple-element.48), channel_id=1, source_target_pairs={{0,12},{4,0},{8,4},{12,8},{1,13},{5,1},{9,5},{13,9},{2,14},{6,2},{... | collective-permute-start | bytes 884744 | tf_op jit(solution)/shard_map/ppermute | solution.py:19
  182.2 21.4 %copy-start.4 = (bf16[64,48,128]{2,1,0:T(8,128)(2,1)}, bf16[64,48,128]{2,1,0:T(8,128)(2,1)S(1)}, u32[]{:S(2)}) copy-start(bf16[64,48,128]{2,1,0:T(8,128)(2,1)S(1)} %all-to-all-done.4.in_ref) | copy-start | bytes 2359300
  182.2 18.0 %all-to-all-start.3 = ((bf16[8,72,256]{2,1,0:T(8,128)(2,1)}), bf16[8,72,256]{2,1,0:T(8,128)(2,1)S(1)}, u32[]{:S(2)}, u32[]{:S(2)}) async-start(bf16[8,72,256]{2,1,0:T(8,128)(2,1)} %add_convert_fusion), calls=%async_computation.3 | async-start | bytes 589824 | tf_op jit(solution)/shard_map/all_to_all | solution.py:23
  200.2 14.2 %copy-start.6 = (bf16[8,72,256]{2,1,0:T(8,128)(2,1)}, bf16[8,72,256]{2,1,0:T(8,128)(2,1)S(1)}, u32[]{:S(2)}) copy-start(bf16[8,72,256]{2,1,0:T(8,128)(2,1)S(1)} %all-to-all-done.3.refs_1_) | copy-start | bytes 884740
  200.2 14.2 %all-to-all-start.2 = ((bf16[8,72,256]{2,1,0:T(8,128)(2,1)}), bf16[8,72,256]{2,1,0:T(8,128)(2,1)S(1)}, u32[]{:S(2)}, u32[]{:S(2)}) async-start(bf16[8,72,256]{2,1,0:T(8,128)(2,1)} %add_convert_fusion.1), calls=%async_computation.2 | async-start | bytes 589824 | tf_op jit(solution)/shard_map/all_to_all | solution.py:23
  214.4 0.7 copy-start.7

commit v2 on v1

--- a/solution.py
+++ b/solution.py
@@ -252,30 +252,40 @@
     )(place, *feats)
 
 
-def back(grads, hidden, slope, w_out, place):
+def back(grads, hidden, slope, w_out, feats_there, place, step):
     items, hid = hidden.shape
     ny, width = w_out.shape[:2]
+    rows = feats_there.shape[0]
 
     def kernel(place_ref, *refs):
-        g_refs, (hid_ref, slope_ref, wo_ref, pre_ref, out_ref) = refs[:ny], refs[ny:]
+        g_refs, (hid_ref, slope_ref, wo_ref, f_ref, pre_ref, out_ref, there_ref) = refs[:ny], refs[ny:]
         acc = None
         for k in range(ny):
             part = mm(g_refs[k][...], wo_ref[place_ref[k]])
             acc = part if acc is None else acc + part
+        pre_ref[...] = (acc * slope_ref[...]).astype(BF)
+
+        def product(t, carry):
+            cut = pl.ds(pl.multiple_of(t * 512, 512), 512)
+            there_ref[cut, :] = mm(f_ref[cut, :], pre_ref[:, :step]).astype(BF)
+            return carry
+
+        lax.fori_loop(0, rows // 512, product, 0)
+        for k in range(ny):
             out_ref[place_ref[k]] = mm(g_refs[k][...], hid_ref[...], ((0,), (0,)))
-        pre_ref[...] = (acc * slope_ref[...]).astype(BF)
 
     return pl.pallas_call(
         kernel,
         out_shape=[
             jax.ShapeDtypeStruct((items, hid), BF),
             jax.ShapeDtypeStruct((ny, width, hid), F32),
-        ],
-        in_specs=[SMEM] + [VMEM] * (ny + 3),
-        out_specs=[VMEM] * 2,
-        cost_estimate=pl.CostEstimate(flops=4 * items * hid * ny * width, bytes_accessed=4 << 20, transcendentals=0),
+            jax.ShapeDtypeStruct((rows, step), BF),
+        ],
+        in_specs=[SMEM] + [VMEM] * (ny + 4),
+        out_specs=[VMEM] * 3,
+        cost_estimate=pl.CostEstimate(flops=6 * items * hid * ny * width, bytes_accessed=6 << 20, transcendentals=0),
         name="back",
-    )(place, *grads, hidden, slope, w_out)
+    )(place, *grads, hidden, slope, w_out, feats_there)
 
 
 def cut_by_x(feats_t, pre, came, out_mine, out_came, order, nz, nx, c):
@@ -289,7 +299,7 @@
     feats_t = feats_t.reshape(-1, items)
     out_mine = out_mine.reshape(ny * width, -1)
     out_came = out_came.reshape(ny * width, -1)
-    group = 2
+    group = 4
     many, few = group * nx * in_rows, group * nx * out_rows
     ahead = hy * width // few
 
@@ -324,26 +334,6 @@
             flops=2 * nz * nx * in_rows * items * hid, bytes_accessed=8 << 20, transcendentals=0),
         name="cut_by_x",
     )(order, feats_t, pre, came, out_mine, out_came)
-
-
-def finish(parts, in_rows):
-    _, both, step = parts[0].shape
-    hid = step * len(parts)
-
-    def kernel(*refs):
-        in_ref, out_ref = refs[-2:]
-        for c, ref in enumerate(refs[:-2]):
-            total = jnp.sum(ref[...].astype(F32), axis=0)
-            in_ref[:, c * step:(c + 1) * step] = total[:in_rows]
-            out_ref[:, c * step:(c + 1) * step] = total[in_rows:]
-
-    return pl.pallas_call(
-        kernel,
-        out_shape=[jax.ShapeDtypeStruct((in_rows, hid), F32), jax.ShapeDtypeStruct((both - in_rows, hid), F32)],
-        in_specs=[VMEM] * len(parts),
-        out_specs=[VMEM] * 2,
-        name="finish",
-    )(*parts)
 
 
 def shards(features, w_in, w_out, codebook, codes, decoder_grad):
@@ -422,27 +412,26 @@
     incoming = exchange(jnp.concatenate(outgoing, axis=1), OWN)
     code_sums = collect(asked, incoming, rows_own)
 
-    pre_grad, out_part = back(grads, hidden, slope, w_out_all, y_place)
-    out_came = shift(out_part, "s", 1)
     pieces = 2
     step = hid // pieces
     there_rows = feats_there.reshape(hy * depth, items)
-    sends = []
+    pre_grad, out_part, there_first = back(grads, hidden, slope, w_out_all, there_rows, y_place, step)
+    out_came = shift(out_part, "s", 1)
+    sums_x = []
     for c in range(pieces):
-        there = mm(there_rows, pre_grad[:, c * step:(c + 1) * step]).astype(BF)
+        there = there_first if c == 0 else mm(there_rows, pre_grad[:, c * step:(c + 1) * step]).astype(BF)
         came = shift(there, "s", 1)
-        sends.append(cut_by_x(feats_here, pre_grad, came, out_part, out_came, x_send, nz, nx, c))
-    over_z = []
-    for c in range(pieces):
-        own, to_1, to_2, to_3 = sends[c]
+        own, to_1, to_2, to_3 = cut_by_x(feats_here, pre_grad, came, out_part, out_came, x_send, nz, nx, c)
         sum_x = (
             own
             + shift(to_1, "x", 1).astype(F32)
             + shift(to_2, "x", 2).astype(F32)
             + shift(to_3, "x", -1).astype(F32)
-        )
-        over_z.append(exchange(sum_x.astype(BF), "z"))
-    in_grad, out_grad = finish(over_z, in_rows)
+        ).astype(BF)
+        sums_x.append(sum_x if c == pieces - 1 else lax.optimization_barrier(sum_x))
+    over_z = exchange(jnp.concatenate(sums_x, axis=2), "z")
+    in_grad = jnp.sum(over_z[:, :in_rows].astype(F32), axis=0)
+    out_grad = jnp.sum(over_z[:, in_rows:].astype(F32), axis=0)
     return (in_grad, out_grad, code_sums)
 
 

time: 219 us -> 230 us (1.050)
  waiting for transfers between devices: 61.9 us -> 79.4 us
  starting transfers between devices: 58.8 us -> 53.4 us
    ppermute x31, waiting for transfers between devices: 49.4 us -> 65.9 us  [shift(): lax.ppermute(value, axis, [(i, (i + by) % size) for i in range(size)])]
    all_to_all x4 -> x3, starting transfers between devices: 22.8 us -> 18.7 us  [exchange(): return lax.all_to_all(value, axis, split_axis=0, concat_axis=0, tiled=True)]
    convert_element_type x2, other arithmetic: 2.76 us -> 0.26 us  [shards(): sum_x = (own + shift(to_1, 'x', 1).astype(F32) + shift(to_2, 'x', 2).asty...]
    pallas_call x1, Pallas kernels: 3.84 us -> 6.26 us  [back(): pl.pallas_call(kernel, out_shape=[jax.ShapeDtypeStruct((items, hid), BF),...]
    all_to_all x4 -> x3, waiting for transfers between devices: 12.4 us -> 13.5 us  [exchange(): return lax.all_to_all(value, axis, split_axis=0, concat_axis=0, tiled=True)]
    unnamed x39 -> x33, local copies, waits for them, and re-layouts: 5.65 us -> 4.82 us
    dot_general x9 -> x8, matrix products: 7.28 us -> 7.29 us  [mm(): return lax.dot_general(a, b, (dims, ((), ())), preferred_element_type=F32)]
  transfers between devices with their start and end apart: 35 -> 34, of which waited for: 12 -> 13; matrix products, arithmetic and copies ran while one was open for 7% -> 6% of each run, Pallas kernels for 18% -> 15%
where the time goes in v2:
time: 230 us; the launch traced here: 226 us
  waiting for transfers between devices  79.4 us (35%)
  starting transfers between devices  53.4 us (23%)
  Pallas kernels  43.6 us (19%)
  blocking collectives  28.8 us (13%)
  local copies, waits for them, and re-layouts  8.72 us (4%)
  matrix products  7.29 us (3%)
  other arithmetic  4.24 us (2%)
    ppermute x31, waiting for transfers between devices, shift(): lax.ppermute(value, axis, [(i, (i + by) % size) for i in range(size)])  65.9 us
    ppermute x31, starting transfers between devices, shift(): lax.ppermute(value, axis, [(i, (i + by) % size) for i in range(size)])  34.7 us
    all_to_all x1, blocking collectives, exchange(): return lax.all_to_all(value, axis, split_axis=0, concat_axis=0, tiled=True)  28.8 us
    all_to_all x3, starting transfers between devices, exchange(): return lax.all_to_all(value, axis, split_axis=0, concat_axis=0, tiled=True)  18.7 us
    all_to_all x3, waiting for transfers between devices, exchange(): return lax.all_to_all(value, axis, split_axis=0, concat_axis=0, tiled=True)  13.5 us
    pallas_call x1, Pallas kernels, pick(): pl.pallas_call(kernel, out_shape=jax.ShapeDtypeStruct((owners, levels * c...  7.37 us
    pallas_call x1, Pallas kernels, encode(): pl.pallas_call(kernel, out_shape=[jax.ShapeDtypeStruct((items, hid), BF),...  7.31 us
    dot_general x8, matrix products, mm(): return lax.dot_general(a, b, (dims, ((), ())), preferred_element_type=F32)  7.29 us
  transfers between devices with their start and end apart: 34, of which 13 were waited for; matrix products, arithmetic and copies ran while one was open for 6% of the time, Pallas kernels for 15%

profile of v2, /device:TPU:8, one launch (start us, length us, event | category | flops | bytes accessed | tf_op | source)
XLA Modules:
  0.0 226.3 jit_solution(12819627725259511023)
XLA Ops:
  0.6 4.3 %ask.1 = (s32[3,512,1]{2,1,0:T(8,128)}, bf16[8,80,512]{2,1,0:T(8,128)(2,1)}) custom-call(s32[3,512]{1,0:T(4,128)} %codes_ref.1, bf16[64,512]{1,0:T(8,128)(2,1)} %wi_ref.1, bf16[8,512]{1,0:T(8,128)(2,1)} %wo_ref.1), custom_call_target="tpu_custom_call" | custom-call | tf_op jit(solution)/shard_map/ask/pallas_call | solution.py:143
  5.0 28.8 %all_to_all.20 = bf16[8,80,512]{2,1,0:T(8,128)(2,1)S(1)} all-to-all(bf16[8,80,512]{2,1,0:T(8,128)(2,1)} %get-tuple-element.29), channel_id=1, replica_groups=mesh['s'=2,'z'=8,'x'=4,'y'=4] {'z'}, dimensions={0} | all-to-all | bytes 1310720 | tf_op jit(solution)/shard_map/all_to_all | solution.py:23
  33.7 3.0 %collective-permute-start.16 = (bf16[8,8,128]{2,1,0:T(8,128)(2,1)S(1)}, bf16[8,8,128]{2,1,0:T(8,128)(2,1)S(1)}, u32[]{:S(2)}, u32[]{:S(2)}) collective-permute-start(bf16[8,8,128]{2,1,0:T(8,128)(2,1)S(1)} %slice.67), channel_id=1, source_target_pairs={{0,8},{4,12},{8,0},{12,4},{1,9},{5,13},{9,1},{13,5},{2,10},{6,14},... | collective-permute-start | bytes 49160 | tf_op jit(solution)/shard_map/ppermute | solution.py:19
  36.8 0.6 collective-permute-start.15
  37.3 2.6 %collective-permute-start.17 = (bf16[8,8,128]{2,1,0:T(8,128)(2,1)S(1)}, bf16[8,8,128]{2,1,0:T(8,128)(2,1)S(1)}, u32[]{:S(2)}, u32[]{:S(2)}) collective-permute-start(bf16[8,8,128]{2,1,0:T(8,128)(2,1)S(1)} %slice.67), channel_id=1, source_target_pairs={{0,12},{4,0},{8,4},{12,8},{1,13},{5,1},{9,5},{13,9},{2,14},{6,2},{... | collective-permute-start | bytes 49160 | tf_op jit(solution)/shard_map/ppermute | solution.py:19
  40.4 2.6 %collective-permute-start.1 = (bf16[512,1024]{1,0:T(8,128)(2,1)}, bf16[512,1024]{1,0:T(8,128)(2,1)}, u32[]{:S(2)}, u32[]{:S(2)}) collective-permute-start(bf16[512,1024]{1,0:T(8,128)(2,1)} %refs_0_.3), channel_id=1, source_target_pairs={{0,2},{1,3},{2,0},{3,1},{4,6},{5,7},{6,4},{7,5},{8,10},{9,11},{10,... | collective-permute-start | bytes 3145736 | tf_op jit(solution)/shard_map/ppermute | solution.py:19
  43.0 1.9 collective-permute-start
  45.1 1.2 collective-permute-done.18
  47.1 0.6 copy.13
  47.7 7.4 %pick.1 = bf16[64,48,128]{2,1,0:T(8,128)(2,1)} custom-call(s32[3,8,128]{2,1,0:T(8,128)} %bitcast.52, bf16[3,1024,128]{2,1,0:T(8,128)(2,1)} %book_ref.1), custom_call_target="tpu_custom_call" | custom-call | tf_op jit(solution)/shard_map/pick/pallas_call | solution.py:177
  55.1 5.5 %all-to-all-start.1 = ((bf16[64,48,128]{2,1,0:T(8,128)(2,1)}), bf16[64,48,128]{2,1,0:T(8,128)(2,1)}, u32[]{:S(2)}, u32[]{:S(2)}) async-start(bf16[64,48,128]{2,1,0:T(8,128)(2,1)} %pick.1), calls=%async_computation.1 | async-start | bytes 1572864 | tf_op jit(solution)/shard_map/all_to_all | solution.py:23
  60.6 2.7 %collective-permute-start.4 = (bf16[8,72,512]{2,1,0:T(8,128)(2,1)S(1)}, bf16[8,72,512]{2,1,0:T(8,128)(2,1)S(1)}, u32[]{:S(2)}, u32[]{:S(2)}) collective-permute-start(bf16[8,72,512]{2,1,0:T(8,128)(2,1)S(1)} %slice.64.refs_4_), channel_id=1, source_target_pairs={{0,12},{4,0},{8,4},{12,8},{1,13},{5,1},{9,5},{13,9},{2,14},{6,2},{... | collective-permute-start | bytes 1769480 | tf_op jit(solution)/shard_map/ppermute | solution.py:19
  63.3 20.6 %collective-permute-done.4.refs_6_ = bf16[8,72,512]{2,1,0:T(8,128)(2,1)S(1)} collective-permute-done((bf16[8,72,512]{2,1,0:T(8,128)(2,1)S(1)}, bf16[8,72,512]{2,1,0:T(8,128)(2,1)S(1)}, u32[]{:S(2)}, u32[]{:S(2)}) %collective-permute-start.4) | collective-permute-done | bytes 589856 | tf_op jit(solution)/shard_map/ppermute | solution.py:19
  83.9 3.3 %collective-permute-start.6 = (bf16[4,72,512]{2,1,0:T(8,128)(2,1)S(1)}, bf16[4,72,512]{2,1,0:T(8,128)(2,1)S(1)}, u32[]{:S(2)}, u32[]{:S(2)}) collective-permute-start(bf16[4,72,512]{2,1,0:T(8,128)(2,1)S(1)} %slice.66), channel_id=1, source_target_pairs={{0,12},{4,0},{8,4},{12,8},{1,13},{5,1},{9,5},{13,9},{2,14},{6,2},{... | collective-permute-start | bytes 884744 | tf_op jit(solution)/shard_map/ppermute | solution.py:19
  87.2 0.7 slice.65
  88.7 4.6 %collective-permute-done.6.refs_8_ = bf16[4,72,512]{2,1,0:T(8,128)(2,1)S(1)} collective-permute-done((bf16[4,72,512]{2,1,0:T(8,128)(2,1)S(1)}, bf16[4,72,512]{2,1,0:T(8,128)(2,1)S(1)}, u32[]{:S(2)}, u32[]{:S(2)}) %collective-permute-start.6) | collective-permute-done | bytes 294944 | tf_op jit(solution)/shard_map/ppermute | solution.py:19
  93.3 4.4 %collective-permute-done.5.refs_7_ = bf16[4,72,512]{2,1,0:T(8,128)(2,1)S(1)} collective-permute-done((bf16[4,72,512]{2,1,0:T(8,128)(2,1)}, bf16[4,72,512]{2,1,0:T(8,128)(2,1)S(1)}, u32[]{:S(2)}, u32[]{:S(2)}) %collective-permute-start.5) | collective-permute-done | bytes 294944 | tf_op jit(solution)/shard_map/ppermute | solution.py:19
  97.7 1.4 slice_reduce_fusion
  99.1 5.8 %turn.1 = (bf16[2,1024,512]{2,1,0:T(8,128)(2,1)}, bf16[2,1024,512]{2,1,0:T(8,128)(2,1)}) custom-call(s32[4]{0:T(128)} %copy-done.15, bf16[512,1024]{1,0:T(8,128)(2,1)} %refs_0_.3, bf16[512,1024]{1,0:T(8,128)(2,1)} %collective-permute-done.refs_1_, bf16[512,1024]{1,0:T(8,128)(2,1)} %collective-permute-done.1.refs_2_, ...), custom_call_target="tpu_custom_call" | custom-call | bytes 8388608 | tf_op jit(solution)/shard_map/turn/pallas_call | solution.py:244
  105.0 7.3 %encode.1 = (bf16[512,512]{1,0:T(8,128)(2,1)S(1)}, f32[512,512]{1,0:T(8,128)}, bf16[4,128,512]{2,1,0:T(8,128)(2,1)S(1)}, f32[512,128]{1,0:T(8,128)S(1)}, f32[512...) custom-call(s32[12]{0:T(128)S(1)} %pad_add_fusion.place_ref, bf16[512,1024]{1,0:T(8,128)(2,1)} %refs_0_.3, ...), custom_call_target="tpu_custom_call" | custom-call | flops 2415919104 | bytes 12582912 | tf_op jit(solution)/shard_map/encode/pallas_call | solution.py:79
  112.3 0.8 copy-done
  113.1 0.8 copy-done.1
  113.9 2.0 collective-permute-start.13
  115.9 1.3 collective-permute-start.14
  117.2 1.3 fusion.34
  118.5 0.5 fusion.2
  119.0 0.5 fusion.1
  119.5 0.5 fusion
  120.0 3.2 %collective-permute-done.12 = f32[512,128]{1,0:T(8,128)S(1)} collective-permute-done((f32[512,128]{1,0:T(8,128)}, f32[512,128]{1,0:T(8,128)S(1)}, u32[]{:S(2)}, u32[]{:S(2)}) %collective-permute-start.12) | collective-permute-done | bytes 262176 | tf_op jit(solution)/shard_map/ppermute | solution.py:19
  123.3 6.2 %collective-permute-done.14 = f32[512,128]{1,0:T(8,128)S(1)} collective-permute-done((f32[512,128]{1,0:T(8,128)}, f32[512,128]{1,0:T(8,128)S(1)}, u32[]{:S(2)}, u32[]{:S(2)}) %collective-permute-start.14) | collective-permute-done | bytes 262176 | tf_op jit(solution)/shard_map/ppermute | solution.py:19
  129.6 1.0 collective-permute-start.21
  130.6 1.4 collective-permute-start.20
  132.0 2.5 %collective-permute-start.19 = (bf16[512,128]{1,0:T(8,128)(2,1)S(1)}, bf16[512,128]{1,0:T(8,128)(2,1)S(1)}, u32[]{:S(2)}, u32[]{:S(2)}) collective-permute-start(bf16[512,128]{1,0:T(8,128)(2,1)S(1)} %get-tuple-element.56.refs_0_), channel_id=1, source_target_pairs={{0,1},{1,2},{2,3},{3,0},{4,5},{5,6},{6,7},{7,4},{8,9},{9,10},{10,1... | collective-permute-start | bytes 393224 | tf_op jit(solution)/shard_map/ppermute | solution.py:19
  134.5 1.2 fusion.6
  135.7 1.2 fusion.7
  136.9 0.8 collective-permute-done.20.refs_2_
  137.7 1.4 collective-permute-done.19.refs_1_
  139.1 0.6 copy-done.14
  139.7 6.3 %back.1 = (bf16[512,512]{1,0:T(8,128)(2,1)}, f32[4,128,512]{2,1,0:T(8,128)}, bf16[2048,256]{1,0:T(8,128)(2,1)}) custom-call(s32[4]{0:T(128)} %copy-done.15, bf16[512,128]{1,0:T(8,128)(2,1)} %copy-done.8, bf16[512,128]{1,0:T(8,128)(2,1)} %copy-done.14, bf16[512,128]{1,0:T(8,128)(2,1)} %copy-done.13, bf16[512,128]{1,0:T(8,128)(2,1)} %copy-done.12, ...), custom_call_target="tpu_custom_call" | custom-call | flops 805306368 | bytes 6291456 | tf_op jit(solution)/shard_map/back/pallas_call | solution.py:277
  146.0 0.5 collective-permute-start.23
  146.5 2.7 %convolution_convert_fusion = bf16[2048,256]{1,0:T(8,128)(2,1)} fusion(bf16[2048,512]{1,0:T(8,128)(2,1)S(1)} %bitcast.45, bf16[512,512]{1,0:T(8,128)(2,1)} %get-tuple-element.42.p_ref), kind=kOutput, calls=%fused_computation | convolution fusion | flops 537395200 | bytes 3407872 | tf_op jit(solution)/shard_map/dot_general | solution.py:27
  149.7 0.9 pad_maximum_fusion
  150.7 7.3 %all-to-all-start.3 = ((bf16[64,48,128]{2,1,0:T(8,128)(2,1)}), bf16[64,48,128]{2,1,0:T(8,128)(2,1)S(1)}, u32[]{:S(2)}, u32[]{:S(2)}) async-start(bf16[64,48,128]{2,1,0:T(8,128)(2,1)} %pad_maximum_fusion), calls=%async_computation.3 | async-start | bytes 1572864 | tf_op jit(solution)/shard_map/all_to_all | solution.py:23
  158.0 0.5 and_select_fusion.3.order_ref
  158.5 1.0 copy-done.2
  159.5 3.5 %cut_by_x.2 = (f32[8,72,256]{2,1,0:T(8,128)}, bf16[8,72,256]{2,1,0:T(8,128)(2,1)}, bf16[8,72,256]{2,1,0:T(8,128)(2,1)}, bf16[8,72,256]{2,1,0:T(8,128)(2,1)}) custom-call(s32[4]{0:T(128)} %and_select_fusion.3.order_ref, bf16[2048,512]{1,0:T(8,128)(2,1)} %bitcast.38, bf16[512,512]{1,0:T(8,128)(2,1)} %get-tuple-element.42.p_ref, ...), custom_call_target="tpu_custom_call" | custom-call | flops 536870912 | bytes 8388608 | tf_op jit(solution)/shard_map/cut_by_x/pallas_call | solution.py:318
  163.0 1.6 collective-permute-start.24
  164.6 2.7 %collective-permute-start.25 = (bf16[8,72,256]{2,1,0:T(8,128)(2,1)}, bf16[8,72,256]{2,1,0:T(8,128)(2,1)S(1)}, u32[]{:S(2)}, u32[]{:S(2)}) collective-permute-start(bf16[8,72,256]{2,1,0:T(8,128)(2,1)} %get-tuple-element.47), channel_id=1, source_target_pairs={{0,8},{4,12},{8,0},{12,4},{1,9},{5,13},{9,1},{13,5},{2,10},{6,14},... | collective-permute-start | bytes 884744 | tf_op jit(solution)/shard_map/ppermute | solution.py:19
  167.3 1.5 collective-permute-start.26
  168.8 1.0 copy-done.5
  169.8 3.5 %cut_by_x.3 = (f32[8,72,256]{2,1,0:T(8,128)}, bf16[8,72,256]{2,1,0:T(8,128)(2,1)}, bf16[8,72,256]{2,1,0:T(8,128)(2,1)}, bf16[8,72,256]{2,1,0:T(8,128)(2,1)}) custom-call(s32[4]{0:T(128)} %and_select_fusion.3.order_ref, bf16[2048,512]{1,0:T(8,128)(2,1)} %bitcast.39, bf16[512,512]{1,0:T(8,128)(2,1)} %get-tuple-element.42.p_ref, bf16[2048,256]{1,0:T(8,128)(2,1)} %copy-done.5, ...), custom_call_target="tpu_custom_call" | custom-call | flops 536870912 | bytes 8388608 | tf_op jit(solution)/shard_map/cut_by_x/pallas_call | solution.py:318
  173.3 0.6 collective-permute-start.28
  174.0 0.9 collective-permute-start.29
  174.9 5.1 %collective-permute-done.24 = bf16[8,72,256]{2,1,0:T(8,128)(2,1)S(1)} collective-permute-done((bf16[8,72,256]{2,1,0:T(8,128)(2,1)}, bf16[8,72,256]{2,1,0:T(8,128)(2,1)S(1)}, u32[]{:S(2)}, u32[]{:S(2)}) %collective-permute-start.24) | collective-permute-done | bytes 294944 | tf_op jit(solution)/shard_map/ppermute | solution.py:19
  179.9 0.6 collective-permute-start.30
  180.5 6.2 %collective-permute-done.25 = bf16[8,72,256]{2,1,0:T(8,128)(2,1)S(1)} collective-permute-done((bf16[8,72,256]{2,1,0:T(8,128)(2,1)}, bf16[8,72,256]{2,1,0:T(8,128)(2,1)S(1)}, u32[]{:S(2)}, u32[]{:S(2)}) %collective-permute-start.25) | collective-permute-done | bytes 294944 | tf_op jit(solution)/shard_map/ppermute | solution.py:19
  186.8 5.2 %collective-permute-done.28 = bf16[8,72,256]{2,1,0:T(8,128)(2,1)S(1)} collective-permute-done((bf16[8,72,256]{2,1,0:T(8,128)(2,1)}, bf16[8,72,256]{2,1,0:T(8,128)(2,1)S(1)}, u32[]{:S(2)}, u32[]{:S(2)}) %collective-permute-start.28) | collective-permute-done | bytes 294944 | tf_op jit(solution)/shard_map/ppermute | solution.py:19
  192.0 7.1 %collective-permute-done.29 = bf16[8,72,256]{2,1,0:T(8,128)(2,1)S(1)} collective-permute-done((bf16[8,72,256]{2,1,0:T(8,128)(2,1)}, bf16[8,72,256]{2,1,0:T(8,128)(2,1)S(1)}, u32[]{:S(2)}, u32[]{:S(2)}) %collective-permute-start.29) | collective-permute-done | bytes 294944 | tf_op jit(solution)/shard_map/ppermute | solution.py:19
  199.2 0.9 pad_maximum_fusion.1
  200.1 5.9 %all-to-all-start.2 = ((bf16[8,72,512]{2,1,0:T(8,128)(2,1)}), bf16[8,72,512]{2,1,0:T(8,128)(2,1)S(1)}, u32[]{:S(2)}, u32[]{:S(2)}) async-start(bf16[8,72,512]{2,1,0:T(8,128)(2,1)} %pad_maximum_fusion.1), calls=%async_computation.2 | async-start | bytes 1179648 | tf_op jit(solution)/shard_map/all_to_all | solution.py:23
  206.0 5.4 %collect.1 = f32[3,1024,128]{2,1,0:T(8,128)} custom-call(s32[3,8,128]{2,1,0:T(8,128)} %bitcast.53, bf16[64,48,128]{2,1,0:T(8,128)(2,1)} %copy-done.3), custom_call_target="tpu_custom_call" | custom-call | tf_op jit(solution)/shard_map/collect/pallas_call | solution.py:210
  211.4 13.5 %all-to-all-done.2 = bf16[8,72,512]{2,1,0:T(8,128)(2,1)S(1)} async-done(((bf16[8,72,512]{2,1,0:T(8,128)(2,1)}), bf16[8,72,512]{2,1,0:T(8,128)(2,1)S(1)}, u32[]{:S(2)}, u32[]{:S(2)}) %all-to-all-start.2) | async-done | bytes 589856 | tf_op jit(solution)/shard_map/all_to_all | solution.py:23
  225.0 0.6 convert_reduce_fusion.1
  225.6 0.7 convert_reduce_fusion
  (81 shorter events, 3.3 us)
Async XLA Ops:
  33.7 9.3 %collective-permute-start.16 = (bf16[8,8,128]{2,1,0:T(8,128)(2,1)S(1)}, bf16[8,8,128]{2,1,0:T(8,128)(2,1)S(1)}, u32[]{:S(2)}, u32[]{:S(2)}) collective-permute-start(bf16[8,8,128]{2,1,0:T(8,128)(2,1)S(1)} %slice.67), channel_id=1, source_target_pairs={{0,8},{4,12},{8,0},{12,4},{1,9},{5,13},{9,1},{13,5},{2,10},{6,14},... | collective-permute-start | bytes 49160 | tf_op jit(solution)/shard_map/ppermute | solution.py:19
  36.8 8.2 %collective-permute-start.15 = (bf16[8,8,128]{2,1,0:T(8,128)(2,1)S(1)}, bf16[8,8,128]{2,1,0:T(8,128)(2,1)S(1)}, u32[]{:S(2)}, u32[]{:S(2)}) collective-permute-start(bf16[8,8,128]{2,1,0:T(8,128)(2,1)S(1)} %slice.67), channel_id=1, source_target_pairs={{0,4},{4,8},{8,12},{12,0},{1,5},{5,9},{9,13},{13,1},{2,6},{6,10},{... | collective-permute-start | bytes 49160 | tf_op jit(solution)/shard_map/ppermute | solution.py:19
  37.3 7.6 %collective-permute-start.17 = (bf16[8,8,128]{2,1,0:T(8,128)(2,1)S(1)}, bf16[8,8,128]{2,1,0:T(8,128)(2,1)S(1)}, u32[]{:S(2)}, u32[]{:S(2)}) collective-permute-start(bf16[8,8,128]{2,1,0:T(8,128)(2,1)S(1)} %slice.67), channel_id=1, source_target_pairs={{0,12},{4,0},{8,4},{12,8},{1,13},{5,1},{9,5},{13,9},{2,14},{6,2},{... | collective-permute-start | bytes 49160 | tf_op jit(solution)/shard_map/ppermute | solution.py:19
  40.0 47.9 %collective-permute-start.2 = (bf16[512,1024]{1,0:T(8,128)(2,1)}, bf16[512,1024]{1,0:T(8,128)(2,1)}, u32[]{:S(2)}, u32[]{:S(2)}) collective-permute-start(bf16[512,1024]{1,0:T(8,128)(2,1)} %refs_0_.3), channel_id=1, source_target_pairs={{0,3},{1,0},{2,1},{3,2},{4,7},{5,4},{6,5},{7,6},{8,11},{9,8},{10,9... | collective-permute-start | bytes 3145736 | tf_op jit(solution)/shard_map/ppermute | solution.py:19
  40.4 47.5 %collective-permute-start.1 = (bf16[512,1024]{1,0:T(8,128)(2,1)}, bf16[512,1024]{1,0:T(8,128)(2,1)}, u32[]{:S(2)}, u32[]{:S(2)}) collective-permute-start(bf16[512,1024]{1,0:T(8,128)(2,1)} %refs_0_.3), channel_id=1, source_target_pairs={{0,2},{1,3},{2,0},{3,1},{4,6},{5,7},{6,4},{7,5},{8,10},{9,11},{10,... | collective-permute-start | bytes 3145736 | tf_op jit(solution)/shard_map/ppermute | solution.py:19
  43.0 45.4 %collective-permute-start = (bf16[512,1024]{1,0:T(8,128)(2,1)}, bf16[512,1024]{1,0:T(8,128)(2,1)}, u32[]{:S(2)}, u32[]{:S(2)}) collective-permute-start(bf16[512,1024]{1,0:T(8,128)(2,1)} %refs_0_.3), channel_id=1, source_target_pairs={{0,1},{1,2},{2,3},{3,0},{4,5},{5,6},{6,7},{7,4},{8,9},{9,10},{10,1... | collective-permute-start | bytes 3145736 | tf_op jit(solution)/shard_map/ppermute | solution.py:19
  45.0 1.3 collective-permute-start.18
  55.1 62.2 %all-to-all-start.1 = ((bf16[64,48,128]{2,1,0:T(8,128)(2,1)}), bf16[64,48,128]{2,1,0:T(8,128)(2,1)}, u32[]{:S(2)}, u32[]{:S(2)}) async-start(bf16[64,48,128]{2,1,0:T(8,128)(2,1)} %pick.1), calls=%async_computation.1 | async-start | bytes 1572864 | tf_op jit(solution)/shard_map/all_to_all | solution.py:23
  60.6 23.3 %collective-permute-start.4 = (bf16[8,72,512]{2,1,0:T(8,128)(2,1)S(1)}, bf16[8,72,512]{2,1,0:T(8,128)(2,1)S(1)}, u32[]{:S(2)}, u32[]{:S(2)}) collective-permute-start(bf16[8,72,512]{2,1,0:T(8,128)(2,1)S(1)} %slice.64.refs_4_), channel_id=1, source_target_pairs={{0,12},{4,0},{8,4},{12,8},{1,13},{5,1},{9,5},{13,9},{2,14},{6,2},{... | collective-permute-start | bytes 1769480 | tf_op jit(solution)/shard_map/ppermute | solution.py:19
  63.3 23.9 %collective-permute-start.3 = (bf16[8,72,512]{2,1,0:T(8,128)(2,1)S(1)}, bf16[8,72,512]{2,1,0:T(8,128)(2,1)S(1)}, u32[]{:S(2)}, u32[]{:S(2)}) collective-permute-start(bf16[8,72,512]{2,1,0:T(8,128)(2,1)S(1)} %slice.64.refs_4_), channel_id=1, source_target_pairs={{0,4},{4,8},{8,12},{12,0},{1,5},{5,9},{9,13},{13,1},{2,6},{6,10},{... | collective-permute-start | bytes 1769480 | tf_op jit(solution)/shard_map/ppermute | solution.py:19
  83.9 9.4 %collective-permute-start.6 = (bf16[4,72,512]{2,1,0:T(8,128)(2,1)S(1)}, bf16[4,72,512]{2,1,0:T(8,128)(2,1)S(1)}, u32[]{:S(2)}, u32[]{:S(2)}) collective-permute-start(bf16[4,72,512]{2,1,0:T(8,128)(2,1)S(1)} %slice.66), channel_id=1, source_target_pairs={{0,12},{4,0},{8,4},{12,8},{1,13},{5,1},{9,5},{13,9},{2,14},{6,2},{... | collective-permute-start | bytes 884744 | tf_op jit(solution)/shard_map/ppermute | solution.py:19
  87.9 9.7 %collective-permute-start.5 = (bf16[4,72,512]{2,1,0:T(8,128)(2,1)}, bf16[4,72,512]{2,1,0:T(8,128)(2,1)S(1)}, u32[]{:S(2)}, u32[]{:S(2)}) collective-permute-start(bf16[4,72,512]{2,1,0:T(8,128)(2,1)} %slice.65), channel_id=1, source_target_pairs={{0,4},{4,8},{8,12},{12,0},{1,5},{5,9},{9,13},{13,1},{2,6},{6,10},{... | collective-permute-start | bytes 884744 | tf_op jit(solution)/shard_map/ppermute | solution.py:19
  87.9 17.0 %collective-permute-start.7 = (bf16[8,72,512]{2,1,0:T(8,128)(2,1)S(1)}, bf16[8,72,512]{2,1,0:T(8,128)(2,1)S(1)}, u32[]{:S(2)}, u32[]{:S(2)}) collective-permute-start(bf16[8,72,512]{2,1,0:T(8,128)(2,1)S(1)} %slice.64.refs_4_), channel_id=1, source_target_pairs={{0,128},{128,0},{1,129},{129,1},{2,130},{130,2},{3,131},{131,3},{4... | collective-permute-start | bytes 1769480 | tf_op jit(solution)/shard_map/ppermute | solution.py:19
  87.9 17.0 %collective-permute-start.9 = (bf16[8,72,512]{2,1,0:T(8,128)(2,1)S(1)}, bf16[8,72,512]{2,1,0:T(8,128)(2,1)}, u32[]{:S(2)}, u32[]{:S(2)}) collective-permute-start(bf16[8,72,512]{2,1,0:T(8,128)(2,1)S(1)} %collective-permute-done.4.refs_6_), channel_id=1, source_target_pairs={{0,128},{128,0},{1,129},{129,1},{2,130},{130,2},{3,131},{131,3},{4... | collective-permute-start | bytes 1769480 | tf_op jit(solution)/shard_map/ppermute | solution.py:19
  88.4 16.5 %collective-permute-start.8 = (bf16[8,72,512]{2,1,0:T(8,128)(2,1)S(1)}, bf16[8,72,512]{2,1,0:T(8,128)(2,1)}, u32[]{:S(2)}, u32[]{:S(2)}) collective-permute-start(bf16[8,72,512]{2,1,0:T(8,128)(2,1)S(1)} %collective-permute-done.3.refs_5_), channel_id=1, source_target_pairs={{0,128},{128,0},{1,129},{129,1},{2,130},{130,2},{3,131},{131,3},{4... | collective-permute-start | bytes 1769480 | tf_op jit(solution)/shard_map/ppermute | solution.py:19
  88.7 10.4 %copy-start.15 = (s32[4]{0:T(128)}, s32[4]{0:T(128)S(1)}, u32[]{:S(2)}) copy-start(s32[4]{0:T(128)S(1)} %get-tuple-element.67.place_ref) | copy-start | bytes 52
  93.3 11.6 %collective-permute-start.11 = (bf16[4,72,512]{2,1,0:T(8,128)(2,1)S(1)}, bf16[4,72,512]{2,1,0:T(8,128)(2,1)S(1)}, u32[]{:S(2)}, u32[]{:S(2)}) collective-permute-start(bf16[4,72,512]{2,1,0:T(8,128)(2,1)S(1)} %collective-permute-done.6.refs_8_), channel_id=1, source_target_pairs={{0,128},{128,0},{1,129},{129,1},{2,130},{130,2},{3,131},{131,3},{4... | collective-permute-start | bytes 884744 | tf_op jit(solution)/shard_map/ppermute | solution.py:19
  97.6 7.3 %collective-permute-start.10 = (bf16[4,72,512]{2,1,0:T(8,128)(2,1)S(1)}, bf16[4,72,512]{2,1,0:T(8,128)(2,1)}, u32[]{:S(2)}, u32[]{:S(2)}) collective-permute-start(bf16[4,72,512]{2,1,0:T(8,128)(2,1)S(1)} %collective-permute-done.5.refs_7_), channel_id=1, source_target_pairs={{0,128},{128,0},{1,129},{129,1},{2,130},{130,2},{3,131},{131,3},{4... | collective-permute-start | bytes 884744 | tf_op jit(solution)/shard_map/ppermute | solution.py:19
  112.3 0.8 copy-start
  113.1 0.8 copy-start.1
  113.9 9.4 %collective-permute-start.12 = (f32[512,128]{1,0:T(8,128)}, f32[512,128]{1,0:T(8,128)S(1)}, u32[]{:S(2)}, u32[]{:S(2)}) collective-permute-start(f32[512,128]{1,0:T(8,128)} %get-tuple-element.31), channel_id=1, source_target_pairs={{0,1},{1,2},{2,3},{3,0},{4,5},{5,6},{6,7},{7,4},{8,9},{9,10},{10,1... | collective-permute-start | bytes 786440 | tf_op jit(solution)/shard_map/ppermute | solution.py:19
  113.9 9.4 %collective-permute-start.13 = (f32[512,128]{1,0:T(8,128)}, f32[512,128]{1,0:T(8,128)S(1)}, u32[]{:S(2)}, u32[]{:S(2)}) collective-permute-start(f32[512,128]{1,0:T(8,128)} %get-tuple-element.32), channel_id=1, source_target_pairs={{0,3},{1,0},{2,1},{3,2},{4,7},{5,4},{6,5},{7,6},{8,11},{9,8},{10,9... | collective-permute-start | bytes 786440 | tf_op jit(solution)/shard_map/ppermute | solution.py:19
  115.9 13.6 %copy-start.11 = (bf16[512,128]{1,0:T(8,128)(2,1)S(1)}, bf16[512,128]{1,0:T(8,128)(2,1)}, u32[]{:S(2)}) copy-start(bf16[512,128]{1,0:T(8,128)(2,1)} %param.11) | copy-start | bytes 393220
  115.9 13.6 %collective-permute-start.14 = (f32[512,128]{1,0:T(8,128)}, f32[512,128]{1,0:T(8,128)S(1)}, u32[]{:S(2)}, u32[]{:S(2)}) collective-permute-start(f32[512,128]{1,0:T(8,128)} %get-tuple-element.33), channel_id=1, source_target_pairs={{0,2},{1,3},{2,0},{3,1},{4,6},{5,7},{6,4},{7,5},{8,10},{9,11},{10,... | collective-permute-start | bytes 786440 | tf_op jit(solution)/shard_map/ppermute | solution.py:19
  129.6 9.5 %copy-start.8 = (bf16[512,128]{1,0:T(8,128)(2,1)}, bf16[512,128]{1,0:T(8,128)(2,1)S(1)}, u32[]{:S(2)}) copy-start(bf16[512,128]{1,0:T(8,128)(2,1)S(1)} %get-tuple-element.56.refs_0_) | copy-start | bytes 393220
  129.6 7.3 %collective-permute-start.21 = (bf16[512,128]{1,0:T(8,128)(2,1)S(1)}, bf16[512,128]{1,0:T(8,128)(2,1)S(1)}, u32[]{:S(2)}, u32[]{:S(2)}) collective-permute-start(bf16[512,128]{1,0:T(8,128)(2,1)S(1)} %get-tuple-element.56.refs_0_), channel_id=1, source_target_pairs={{0,3},{1,0},{2,1},{3,2},{4,7},{5,4},{6,5},{7,6},{8,11},{9,8},{10,9... | collective-permute-start | bytes 393224 | tf_op jit(solution)/shard_map/ppermute | solution.py:19
  130.6 7.1 %collective-permute-start.20 = (bf16[512,128]{1,0:T(8,128)(2,1)S(1)}, bf16[512,128]{1,0:T(8,128)(2,1)S(1)}, u32[]{:S(2)}, u32[]{:S(2)}) collective-permute-start(bf16[512,128]{1,0:T(8,128)(2,1)S(1)} %get-tuple-element.56.refs_0_), channel_id=1, source_target_pairs={{0,2},{1,3},{2,0},{3,1},{4,6},{5,7},{6,4},{7,5},{8,10},{9,11},{10,... | collective-permute-start | bytes 393224 | tf_op jit(solution)/shard_map/ppermute | solution.py:19
  132.0 7.1 %collective-permute-start.19 = (bf16[512,128]{1,0:T(8,128)(2,1)S(1)}, bf16[512,128]{1,0:T(8,128)(2,1)S(1)}, u32[]{:S(2)}, u32[]{:S(2)}) collective-permute-start(bf16[512,128]{1,0:T(8,128)(2,1)S(1)} %get-tuple-element.56.refs_0_), channel_id=1, source_target_pairs={{0,1},{1,2},{2,3},{3,0},{4,5},{5,6},{6,7},{7,4},{8,9},{9,10},{10,1... | collective-permute-start | bytes 393224 | tf_op jit(solution)/shard_map/ppermute | solution.py:19
  136.9 2.2 copy-start.12
  137.7 1.4 copy-start.13
  139.1 0.7 copy-start.14
  139.7 6.8 %copy-start.4 = (bf16[2,1024,512]{2,1,0:T(8,128)(2,1)S(1)}, bf16[2,1024,512]{2,1,0:T(8,128)(2,1)}, u32[]{:S(2)}) copy-start(bf16[2,1024,512]{2,1,0:T(8,128)(2,1)} %get-tuple-element.41) | copy-start | bytes 6291460
  146.0 12.5 %collective-permute-start.22 = (bf16[2048,256]{1,0:T(8,128)(2,1)}, bf16[2048,256]{1,0:T(8,128)(2,1)}, u32[]{:S(2)}, u32[]{:S(2)}) collective-permute-start(bf16[2048,256]{1,0:T(8,128)(2,1)} %get-tuple-element.43), channel_id=1, source_target_pairs={{0,128},{128,0},{1,129},{129,1},{2,130},{130,2},{3,131},{131,3},{4... | collective-permute-start | bytes 3145736 | tf_op jit(solution)/shard_map/ppermute | solution.py:19
  146.0 12.5 %collective-permute-start.23 = (f32[4,128,512]{2,1,0:T(8,128)}, f32[4,128,512]{2,1,0:T(8,128)S(1)}, u32[]{:S(2)}, u32[]{:S(2)}) collective-permute-start(f32[4,128,512]{2,1,0:T(8,128)} %get-tuple-element.44), channel_id=1, source_target_pairs={{0,128},{128,0},{1,129},{129,1},{2,130},{130,2},{3,131},{131,3},{4... | collective-permute-start | bytes 3145736 | tf_op jit(solution)/shard_map/ppermute | solution.py:19
  146.5 3.2 %copy-start.9 = (bf16[1024,128]{1,0:T(8,128)(2,1)S(1)}, bf16[1024,128]{1,0:T(8,128)(2,1)}, u32[]{:S(2)}) copy-start(bf16[1024,128]{1,0:T(8,128)(2,1)} %fusion.6) | copy-start | bytes 786436
  146.5 3.2 %copy-start.10 = (bf16[1024,128]{1,0:T(8,128)(2,1)S(1)}, bf16[1024,128]{1,0:T(8,128)(2,1)}, u32[]{:S(2)}) copy-start(bf16[1024,128]{1,0:T(8,128)(2,1)} %fusion.7) | copy-start | bytes 786436
  149.2 19.6 %collective-permute-start.27 = (bf16[2048,256]{1,0:T(8,128)(2,1)}, bf16[2048,256]{1,0:T(8,128)(2,1)S(1)}, u32[]{:S(2)}, u32[]{:S(2)}) collective-permute-start(bf16[2048,256]{1,0:T(8,128)(2,1)} %convolution_convert_fusion), channel_id=1, source_target_pairs={{0,128},{128,0},{1,129},{129,1},{2,130},{130,2},{3,131},{131,3},{4... | collective-permute-start | bytes 3145736 | tf_op jit(solution)/shard_map/ppermute | solution.py:19
  150.7 49.5 %all-to-all-start.3 = ((bf16[64,48,128]{2,1,0:T(8,128)(2,1)}), bf16[64,48,128]{2,1,0:T(8,128)(2,1)S(1)}, u32[]{:S(2)}, u32[]{:S(2)}) async-start(bf16[64,48,128]{2,1,0:T(8,128)(2,1)} %pad_maximum_fusion), calls=%async_computation.3 | async-start | bytes 1572864 | tf_op jit(solution)/shard_map/all_to_all | solution.py:23
  158.5 1.0 copy-start.2
  163.0 16.9 %collective-permute-start.24 = (bf16[8,72,256]{2,1,0:T(8,128)(2,1)}, bf16[8,72,256]{2,1,0:T(8,128)(2,1)S(1)}, u32[]{:S(2)}, u32[]{:S(2)}) collective-permute-start(bf16[8,72,256]{2,1,0:T(8,128)(2,1)} %get-tuple-element.46), channel_id=1, source_target_pairs={{0,4},{4,8},{8,12},{12,0},{1,5},{5,9},{9,13},{13,1},{2,6},{6,10},{... | collective-permute-start | bytes 884744 | tf_op jit(solution)/shard_map/ppermute | solution.py:19
  164.6 22.0 %collective-permute-start.25 = (bf16[8,72,256]{2,1,0:T(8,128)(2,1)}, bf16[8,72,256]{2,1,0:T(8,128)(2,1)S(1)}, u32[]{:S(2)}, u32[]{:S(2)}) collective-permute-start(bf16[8,72,256]{2,1,0:T(8,128)(2,1)} %get-tuple-element.47), channel_id=1, source_target_pairs={{0,8},{4,12},{8,0},{12,4},{1,9},{5,13},{9,1},{13,5},{2,10},{6,14},... | collective-permute-start | bytes 884744 | tf_op jit(solution)/shard_map/ppermute | solution.py:19
  167.3 19.4 %copy-start.6 = (f32[8,72,256]{2,1,0:T(8,128)S(1)}, f32[8,72,256]{2,1,0:T(8,128)}, u32[]{:S(2)}) copy-start(f32[8,72,256]{2,1,0:T(8,128)} %get-tuple-element.45) | copy-start | bytes 1769476
  167.3 19.3 %collective-permute-start.26 = (bf16[8,72,256]{2,1,0:T(8,128)(2,1)}, bf16[8,72,256]{2,1,0:T(8,128)(2,1)S(1)}, u32[]{:S(2)}, u32[]{:S(2)}) collective-permute-start(bf16[8,72,256]{2,1,0:T(8,128)(2,1)} %get-tuple-element.48), channel_id=1, source_target_pairs={{0,12},{4,0},{8,4},{12,8},{1,13},{5,1},{9,5},{13,9},{2,14},{6,2},{... | collective-permute-start | bytes 884744 | tf_op jit(solution)/shard_map/ppermute | solution.py:19
  168.8 1.0 copy-start.5
  173.3 25.8 %copy-start.7 = (f32[8,72,256]{2,1,0:T(8,128)S(1)}, f32[8,72,256]{2,1,0:T(8,128)}, u32[]{:S(2)}) copy-start(f32[8,72,256]{2,1,0:T(8,128)} %get-tuple-element.49) | copy-start | bytes 1769476
  173.3 18.7 %collective-permute-start.28 = (bf16[8,72,256]{2,1,0:T(8,128)(2,1)}, bf16[8,72,256]{2,1,0:T(8,128)(2,1)S(1)}, u32[]{:S(2)}, u32[]{:S(2)}) collective-permute-start(bf16[8,72,256]{2,1,0:T(8,128)(2,1)} %get-tuple-element.50), channel_id=1, source_target_pairs={{0,4},{4,8},{8,12},{12,0},{1,5},{5,9},{9,13},{13,1},{2,6},{6,10},{... | collective-permute-start | bytes 884744 | tf_op jit(solution)/shard_map/ppermute | solution.py:19
  174.0 25.1 %collective-permute-start.29 = (bf16[8,72,256]{2,1,0:T(8,128)(2,1)}, bf16[8,72,256]{2,1,0:T(8,128)(2,1)S(1)}, u32[]{:S(2)}, u32[]{:S(2)}) collective-permute-start(bf16[8,72,256]{2,1,0:T(8,128)(2,1)} %get-tuple-element.51), channel_id=1, source_target_pairs={{0,8},{4,12},{8,0},{12,4},{1,9},{5,13},{9,1},{13,5},{2,10},{6,14},... | collective-permute-start | bytes 884744 | tf_op jit(solution)/shard_map/ppermute | solution.py:19
  179.9 19.2 %collective-permute-start.30 = (bf16[8,72,256]{2,1,0:T(8,128)(2,1)}, bf16[8,72,256]{2,1,0:T(8,128)(2,1)S(1)}, u32[]{:S(2)}, u32[]{:S(2)}) collective-permute-start(bf16[8,72,256]{2,1,0:T(8,128)(2,1)} %get-tuple-element.52), channel_id=1, source_target_pairs={{0,12},{4,0},{8,4},{12,8},{1,13},{5,1},{9,5},{13,9},{2,14},{6,2},{... | collective-permute-start | bytes 884744 | tf_op jit(solution)/shard_map/ppermute | solution.py:19
  200.1 5.9 %copy-start.3 = (bf16[64,48,128]{2,1,0:T(8,128)(2,1)}, bf16[64,48,128]{2,1,0:T(8,128)(2,1)S(1)}, u32[]{:S(2)}) copy-start(bf16[64,48,128]{2,1,0:T(8,128)(2,1)S(1)} %all-to-all-done.3.in_ref) | copy-start | bytes 2359300
  200.1 24.8 %all-to-all-start.2 = ((bf16[8,72,512]{2,1,0:T(8,128)(2,1)}), bf16[8,72,512]{2,1,0:T(8,128)(2,1)S(1)}, u32[]{:S(2)}, u32[]{:S(2)}) async-start(bf16[8,72,512]{2,1,0:T(8,128)(2,1)} %pad_maximum_fusion.1), calls=%async_computation.2 | async-start | bytes 1179648 | tf_op jit(solution)/shard_map/all_to_all | solution.py:23

commit v3 on v2

--- a/solution.py
+++ b/solution.py
@@ -417,7 +417,7 @@
     there_rows = feats_there.reshape(hy * depth, items)
     pre_grad, out_part, there_first = back(grads, hidden, slope, w_out_all, there_rows, y_place, step)
     out_came = shift(out_part, "s", 1)
-    sums_x = []
+    in_list, out_list = [], []
     for c in range(pieces):
         there = there_first if c == 0 else mm(there_rows, pre_grad[:, c * step:(c + 1) * step]).astype(BF)
         came = shift(there, "s", 1)
@@ -428,11 +428,10 @@
             + shift(to_2, "x", 2).astype(F32)
             + shift(to_3, "x", -1).astype(F32)
         ).astype(BF)
-        sums_x.append(sum_x if c == pieces - 1 else lax.optimization_barrier(sum_x))
-    over_z = exchange(jnp.concatenate(sums_x, axis=2), "z")
-    in_grad = jnp.sum(over_z[:, :in_rows].astype(F32), axis=0)
-    out_grad = jnp.sum(over_z[:, in_rows:].astype(F32), axis=0)
-    return (in_grad, out_grad, code_sums)
+        over_z = exchange(sum_x, "z")
+        in_list.append(jnp.sum(over_z[:, :in_rows].astype(F32), axis=0))
+        out_list.append(jnp.sum(over_z[:, in_rows:].astype(F32), axis=0))
+    return (jnp.concatenate(in_list, axis=1), jnp.concatenate(out_list, axis=1), code_sums)
 
 
 def solution(mesh):

time: 230 us -> 218 us (0.948)
  waiting for transfers between devices: 79.4 us -> 61.1 us
  starting transfers between devices: 53.4 us -> 59.2 us
    ppermute x31, waiting for transfers between devices: 65.9 us -> 48.9 us  [shift(): lax.ppermute(value, axis, [(i, (i + by) % size) for i in range(size)])]
    all_to_all x3 -> x4, starting transfers between devices: 18.7 us -> 23.2 us  [exchange(): return lax.all_to_all(value, axis, split_axis=0, concat_axis=0, tiled=True)]
    convert_element_type x2, other arithmetic: 0.26 us -> 2.74 us  [shards(): sum_x = (own + shift(to_1, 'x', 1).astype(F32) + shift(to_2, 'x', 2).asty...]
    all_to_all x3 -> x4, waiting for transfers between devices: 13.5 us -> 12.2 us  [exchange(): return lax.all_to_all(value, axis, split_axis=0, concat_axis=0, tiled=True)]
    unnamed x33 -> x29, local copies, waits for them, and re-layouts: 4.82 us -> 5.85 us
  transfers between devices with their start and end apart: 34 -> 35, of which waited for: 13 -> 11; matrix products, arithmetic and copies ran while one was open for 6% -> 6% of each run, Pallas kernels for 15% -> 18%
where the time goes in v3:
time: 218 us; the launch traced here: 216 us
  waiting for transfers between devices  61.1 us (28%)
  starting transfers between devices  59.2 us (27%)
  Pallas kernels  43.5 us (20%)
  blocking collectives  28.8 us (13%)
  local copies, waits for them, and re-layouts  9.76 us (4%)
  matrix products  6.43 us (3%)
  other arithmetic  5.87 us (3%)
    ppermute x31, waiting for transfers between devices, shift(): lax.ppermute(value, axis, [(i, (i + by) % size) for i in range(size)])  48.9 us
    ppermute x31, starting transfers between devices, shift(): lax.ppermute(value, axis, [(i, (i + by) % size) for i in range(size)])  36 us
    all_to_all x1, blocking collectives, exchange(): return lax.all_to_all(value, axis, split_axis=0, concat_axis=0, tiled=True)  28.8 us
    all_to_all x4, starting transfers between devices, exchange(): return lax.all_to_all(value, axis, split_axis=0, concat_axis=0, tiled=True)  23.2 us
    all_to_all x4, waiting for transfers between devices, exchange(): return lax.all_to_all(value, axis, split_axis=0, concat_axis=0, tiled=True)  12.2 us
    pallas_call x1, Pallas kernels, pick(): pl.pallas_call(kernel, out_shape=jax.ShapeDtypeStruct((owners, levels * c...  7.36 us
    pallas_call x1, Pallas kernels, encode(): pl.pallas_call(kernel, out_shape=[jax.ShapeDtypeStruct((items, hid), BF),...  7.33 us
    pallas_call x2, Pallas kernels, cut_by_x(): pl.pallas_call(kernel, out_shape=[jax.ShapeDtypeStruct((nz, both, hid), F...  7.09 us
  transfers between devices with their start and end apart: 35, of which 11 were waited for; matrix products, arithmetic and copies ran while one was open for 6% of the time, Pallas kernels for 18%

profile of v3, /device:TPU:8, one launch (start us, length us, event | category | flops | bytes accessed | tf_op | source)
XLA Modules:
  0.0 215.5 jit_solution(13910958665306971329)
XLA Ops:
  0.6 4.3 %ask.1 = (s32[3,512,1]{2,1,0:T(8,128)}, bf16[8,80,512]{2,1,0:T(8,128)(2,1)}) custom-call(s32[3,512]{1,0:T(4,128)} %codes_ref.1, bf16[64,512]{1,0:T(8,128)(2,1)} %wi_ref.1, bf16[8,512]{1,0:T(8,128)(2,1)} %wo_ref.1), custom_call_target="tpu_custom_call" | custom-call | tf_op jit(solution)/shard_map/ask/pallas_call | solution.py:143
  4.9 28.8 %all_to_all.25 = bf16[8,80,512]{2,1,0:T(8,128)(2,1)S(1)} all-to-all(bf16[8,80,512]{2,1,0:T(8,128)(2,1)} %get-tuple-element.29), channel_id=1, replica_groups=mesh['s'=2,'z'=8,'x'=4,'y'=4] {'z'}, dimensions={0} | all-to-all | bytes 1310720 | tf_op jit(solution)/shard_map/all_to_all | solution.py:23
  33.7 3.0 %collective-permute-start.16 = (bf16[8,8,128]{2,1,0:T(8,128)(2,1)S(1)}, bf16[8,8,128]{2,1,0:T(8,128)(2,1)S(1)}, u32[]{:S(2)}, u32[]{:S(2)}) collective-permute-start(bf16[8,8,128]{2,1,0:T(8,128)(2,1)S(1)} %slice.75), channel_id=1, source_target_pairs={{0,8},{4,12},{8,0},{12,4},{1,9},{5,13},{9,1},{13,5},{2,10},{6,14},... | collective-permute-start | bytes 49160 | tf_op jit(solution)/shard_map/ppermute | solution.py:19
  36.7 0.6 collective-permute-start.15
  37.3 2.6 %collective-permute-start.17 = (bf16[8,8,128]{2,1,0:T(8,128)(2,1)S(1)}, bf16[8,8,128]{2,1,0:T(8,128)(2,1)S(1)}, u32[]{:S(2)}, u32[]{:S(2)}) collective-permute-start(bf16[8,8,128]{2,1,0:T(8,128)(2,1)S(1)} %slice.75), channel_id=1, source_target_pairs={{0,12},{4,0},{8,4},{12,8},{1,13},{5,1},{9,5},{13,9},{2,14},{6,2},{... | collective-permute-start | bytes 49160 | tf_op jit(solution)/shard_map/ppermute | solution.py:19
  40.4 2.6 %collective-permute-start.1 = (bf16[512,1024]{1,0:T(8,128)(2,1)}, bf16[512,1024]{1,0:T(8,128)(2,1)}, u32[]{:S(2)}, u32[]{:S(2)}) collective-permute-start(bf16[512,1024]{1,0:T(8,128)(2,1)} %refs_0_.3), channel_id=1, source_target_pairs={{0,2},{1,3},{2,0},{3,1},{4,6},{5,7},{6,4},{7,5},{8,10},{9,11},{10,... | collective-permute-start | bytes 3145736 | tf_op jit(solution)/shard_map/ppermute | solution.py:19
  43.0 1.9 collective-permute-start
  45.1 1.2 collective-permute-done.18
  47.1 0.6 copy.13
  47.7 7.4 %pick.1 = bf16[64,48,128]{2,1,0:T(8,128)(2,1)} custom-call(s32[3,8,128]{2,1,0:T(8,128)} %bitcast.52, bf16[3,1024,128]{2,1,0:T(8,128)(2,1)} %book_ref.1), custom_call_target="tpu_custom_call" | custom-call | tf_op jit(solution)/shard_map/pick/pallas_call | solution.py:177
  55.0 5.5 %all-to-all-start.1 = ((bf16[64,48,128]{2,1,0:T(8,128)(2,1)}), bf16[64,48,128]{2,1,0:T(8,128)(2,1)}, u32[]{:S(2)}, u32[]{:S(2)}) async-start(bf16[64,48,128]{2,1,0:T(8,128)(2,1)} %pick.1), calls=%async_computation.1 | async-start | bytes 1572864 | tf_op jit(solution)/shard_map/all_to_all | solution.py:23
  60.5 2.7 %collective-permute-start.4 = (bf16[8,72,512]{2,1,0:T(8,128)(2,1)S(1)}, bf16[8,72,512]{2,1,0:T(8,128)(2,1)S(1)}, u32[]{:S(2)}, u32[]{:S(2)}) collective-permute-start(bf16[8,72,512]{2,1,0:T(8,128)(2,1)S(1)} %slice.72.refs_4_), channel_id=1, source_target_pairs={{0,12},{4,0},{8,4},{12,8},{1,13},{5,1},{9,5},{13,9},{2,14},{6,2},{... | collective-permute-start | bytes 1769480 | tf_op jit(solution)/shard_map/ppermute | solution.py:19
  63.2 20.6 %collective-permute-done.4.refs_6_ = bf16[8,72,512]{2,1,0:T(8,128)(2,1)S(1)} collective-permute-done((bf16[8,72,512]{2,1,0:T(8,128)(2,1)S(1)}, bf16[8,72,512]{2,1,0:T(8,128)(2,1)S(1)}, u32[]{:S(2)}, u32[]{:S(2)}) %collective-permute-start.4) | collective-permute-done | bytes 589856 | tf_op jit(solution)/shard_map/ppermute | solution.py:19
  83.8 3.3 %collective-permute-start.6 = (bf16[4,72,512]{2,1,0:T(8,128)(2,1)S(1)}, bf16[4,72,512]{2,1,0:T(8,128)(2,1)S(1)}, u32[]{:S(2)}, u32[]{:S(2)}) collective-permute-start(bf16[4,72,512]{2,1,0:T(8,128)(2,1)S(1)} %slice.74), channel_id=1, source_target_pairs={{0,12},{4,0},{8,4},{12,8},{1,13},{5,1},{9,5},{13,9},{2,14},{6,2},{... | collective-permute-start | bytes 884744 | tf_op jit(solution)/shard_map/ppermute | solution.py:19
  87.1 0.7 slice.73
  87.9 0.5 collective-permute-start.9
  88.7 4.5 %collective-permute-done.6.refs_8_ = bf16[4,72,512]{2,1,0:T(8,128)(2,1)S(1)} collective-permute-done((bf16[4,72,512]{2,1,0:T(8,128)(2,1)S(1)}, bf16[4,72,512]{2,1,0:T(8,128)(2,1)S(1)}, u32[]{:S(2)}, u32[]{:S(2)}) %collective-permute-start.6) | collective-permute-done | bytes 294944 | tf_op jit(solution)/shard_map/ppermute | solution.py:19
  93.3 4.4 %collective-permute-done.5.refs_7_ = bf16[4,72,512]{2,1,0:T(8,128)(2,1)S(1)} collective-permute-done((bf16[4,72,512]{2,1,0:T(8,128)(2,1)}, bf16[4,72,512]{2,1,0:T(8,128)(2,1)S(1)}, u32[]{:S(2)}, u32[]{:S(2)}) %collective-permute-start.5) | collective-permute-done | bytes 294944 | tf_op jit(solution)/shard_map/ppermute | solution.py:19
  97.7 1.4 slice_reduce_fusion
  99.1 5.8 %turn.1 = (bf16[2,1024,512]{2,1,0:T(8,128)(2,1)}, bf16[2,1024,512]{2,1,0:T(8,128)(2,1)}) custom-call(s32[4]{0:T(128)} %copy-done.13, bf16[512,1024]{1,0:T(8,128)(2,1)} %refs_0_.3, bf16[512,1024]{1,0:T(8,128)(2,1)} %collective-permute-done.refs_1_, bf16[512,1024]{1,0:T(8,128)(2,1)} %collective-permute-done.1.refs_2_, ...), custom_call_target="tpu_custom_call" | custom-call | bytes 8388608 | tf_op jit(solution)/shard_map/turn/pallas_call | solution.py:244
  105.0 7.3 %encode.1 = (bf16[512,512]{1,0:T(8,128)(2,1)S(1)}, f32[512,512]{1,0:T(8,128)}, bf16[4,128,512]{2,1,0:T(8,128)(2,1)S(1)}, f32[512,128]{1,0:T(8,128)S(1)}, f32[512...) custom-call(s32[12]{0:T(128)S(1)} %pad_add_fusion.place_ref, bf16[512,1024]{1,0:T(8,128)(2,1)} %refs_0_.3, ...), custom_call_target="tpu_custom_call" | custom-call | flops 2415919104 | bytes 12582912 | tf_op jit(solution)/shard_map/encode/pallas_call | solution.py:79
  112.3 0.8 copy-done
  113.1 0.8 copy-done.1
  113.9 2.0 collective-permute-start.13
  115.9 1.3 collective-permute-start.14
  117.3 1.3 fusion.34
  118.5 0.5 fusion.2
  119.0 0.5 fusion.1
  119.5 0.5 fusion
  120.1 3.2 %collective-permute-done.12 = f32[512,128]{1,0:T(8,128)S(1)} collective-permute-done((f32[512,128]{1,0:T(8,128)}, f32[512,128]{1,0:T(8,128)S(1)}, u32[]{:S(2)}, u32[]{:S(2)}) %collective-permute-start.12) | collective-permute-done | bytes 262176 | tf_op jit(solution)/shard_map/ppermute | solution.py:19
  123.3 6.2 %collective-permute-done.14 = f32[512,128]{1,0:T(8,128)S(1)} collective-permute-done((f32[512,128]{1,0:T(8,128)}, f32[512,128]{1,0:T(8,128)S(1)}, u32[]{:S(2)}, u32[]{:S(2)}) %collective-permute-start.14) | collective-permute-done | bytes 262176 | tf_op jit(solution)/shard_map/ppermute | solution.py:19
  129.6 0.5 fusion.6
  131.1 1.0 collective-permute-start.21
  132.0 1.4 collective-permute-start.20
  133.4 2.5 %collective-permute-start.19 = (bf16[512,128]{1,0:T(8,128)(2,1)S(1)}, bf16[512,128]{1,0:T(8,128)(2,1)S(1)}, u32[]{:S(2)}, u32[]{:S(2)}) collective-permute-start(bf16[512,128]{1,0:T(8,128)(2,1)S(1)} %get-tuple-element.56.refs_0_), channel_id=1, source_target_pairs={{0,1},{1,2},{2,3},{3,0},{4,5},{5,6},{6,7},{7,4},{8,9},{9,10},{10,1... | collective-permute-start | bytes 393224 | tf_op jit(solution)/shard_map/ppermute | solution.py:19
  136.0 0.9 pad_maximum_fusion
  136.9 7.5 %all-to-all-start.4 = ((bf16[64,48,128]{2,1,0:T(8,128)(2,1)}), bf16[64,48,128]{2,1,0:T(8,128)(2,1)S(1)}, u32[]{:S(2)}, u32[]{:S(2)}) async-start(bf16[64,48,128]{2,1,0:T(8,128)(2,1)} %pad_maximum_fusion), calls=%async_computation.4 | async-start | bytes 1572864 | tf_op jit(solution)/shard_map/all_to_all | solution.py:23
  144.5 0.6 copy-done.10
  145.2 6.2 %back.1 = (bf16[512,512]{1,0:T(8,128)(2,1)}, f32[4,128,512]{2,1,0:T(8,128)}, bf16[2048,256]{1,0:T(8,128)(2,1)}) custom-call(s32[4]{0:T(128)} %copy-done.13, bf16[512,128]{1,0:T(8,128)(2,1)} %copy-done.8, bf16[512,128]{1,0:T(8,128)(2,1)} %copy-done.12, bf16[512,128]{1,0:T(8,128)(2,1)} %copy-done.11, bf16[512,128]{1,0:T(8,128)(2,1)} %copy-done.10, ...), custom_call_target="tpu_custom_call" | custom-call | flops 805306368 | bytes 6291456 | tf_op jit(solution)/shard_map/back/pallas_call | solution.py:277
  151.4 0.5 collective-permute-start.23
  151.9 3.3 %convolution_convert_fusion = bf16[2048,256]{1,0:T(8,128)(2,1)} fusion(bf16[2048,512]{1,0:T(8,128)(2,1)} %bitcast.45, bf16[512,512]{1,0:T(8,128)(2,1)} %get-tuple-element.42.p_ref), kind=kOutput, calls=%fused_computation | convolution fusion | flops 537395200 | bytes 3407872 | tf_op jit(solution)/shard_map/dot_general | solution.py:27
  155.2 0.5 and_select_fusion.3.order_ref
  155.8 0.9 copy-done.5
  156.7 1.0 copy-done.2
  157.7 3.5 %cut_by_x.2 = (f32[8,72,256]{2,1,0:T(8,128)}, bf16[8,72,256]{2,1,0:T(8,128)(2,1)}, bf16[8,72,256]{2,1,0:T(8,128)(2,1)}, bf16[8,72,256]{2,1,0:T(8,128)(2,1)}) custom-call(s32[4]{0:T(128)} %and_select_fusion.3.order_ref, bf16[2048,512]{1,0:T(8,128)(2,1)} %bitcast.38, bf16[512,512]{1,0:T(8,128)(2,1)} %get-tuple-element.42.p_ref, bf16[2048,256]{1,0:T(8,128)(2,1)} %copy-done.5, ...), custom_call_target="tpu_custom_call" | custom-call | flops 536870912 | bytes 8388608 | tf_op jit(solution)/shard_map/cut_by_x/pallas_call | solution.py:318
  161.2 1.6 collective-permute-start.24
  162.8 2.7 %collective-permute-start.25 = (bf16[8,72,256]{2,1,0:T(8,128)(2,1)}, bf16[8,72,256]{2,1,0:T(8,128)(2,1)}, u32[]{:S(2)}, u32[]{:S(2)}) collective-permute-start(bf16[8,72,256]{2,1,0:T(8,128)(2,1)} %get-tuple-element.47), channel_id=1, source_target_pairs={{0,8},{4,12},{8,0},{12,4},{1,9},{5,13},{9,1},{13,5},{2,10},{6,14},... | collective-permute-start | bytes 884744 | tf_op jit(solution)/shard_map/ppermute | solution.py:19
  165.5 1.5 collective-permute-start.26
  167.0 1.0 copy-done.4
  168.0 3.5 %cut_by_x.3 = (f32[8,72,256]{2,1,0:T(8,128)}, bf16[8,72,256]{2,1,0:T(8,128)(2,1)}, bf16[8,72,256]{2,1,0:T(8,128)(2,1)}, bf16[8,72,256]{2,1,0:T(8,128)(2,1)}) custom-call(s32[4]{0:T(128)} %and_select_fusion.3.order_ref, bf16[2048,512]{1,0:T(8,128)(2,1)} %bitcast.39, bf16[512,512]{1,0:T(8,128)(2,1)} %get-tuple-element.42.p_ref, bf16[2048,256]{1,0:T(8,128)(2,1)} %copy-done.4, ...), custom_call_target="tpu_custom_call" | custom-call | flops 536870912 | bytes 8388608 | tf_op jit(solution)/shard_map/cut_by_x/pallas_call | solution.py:318
  171.5 0.6 collective-permute-start.28
  172.2 0.9 collective-permute-start.29
  173.1 1.9 collective-permute-start.30
  174.9 5.1 %collective-permute-done.25 = bf16[8,72,256]{2,1,0:T(8,128)(2,1)} collective-permute-done((bf16[8,72,256]{2,1,0:T(8,128)(2,1)}, bf16[8,72,256]{2,1,0:T(8,128)(2,1)}, u32[]{:S(2)}, u32[]{:S(2)}) %collective-permute-start.25) | collective-permute-done | bytes 294944 | tf_op jit(solution)/shard_map/ppermute | solution.py:19
  180.1 1.9 add_convert_fusion.1
  182.0 6.7 %all-to-all-start.2 = ((bf16[8,72,256]{2,1,0:T(8,128)(2,1)}), bf16[8,72,256]{2,1,0:T(8,128)(2,1)S(1)}, u32[]{:S(2)}, u32[]{:S(2)}) async-start(bf16[8,72,256]{2,1,0:T(8,128)(2,1)} %add_convert_fusion.1), calls=%async_computation.2 | async-start | bytes 589824 | tf_op jit(solution)/shard_map/all_to_all | solution.py:23
  188.7 3.5 %collective-permute-done.29 = bf16[8,72,256]{2,1,0:T(8,128)(2,1)S(1)} collective-permute-done((bf16[8,72,256]{2,1,0:T(8,128)(2,1)}, bf16[8,72,256]{2,1,0:T(8,128)(2,1)S(1)}, u32[]{:S(2)}, u32[]{:S(2)}) %collective-permute-start.29) | collective-permute-done | bytes 294944 | tf_op jit(solution)/shard_map/ppermute | solution.py:19
  192.2 0.8 add_convert_fusion
  193.1 6.9 %all-to-all-done.2 = bf16[8,72,256]{2,1,0:T(8,128)(2,1)S(1)} async-done(((bf16[8,72,256]{2,1,0:T(8,128)(2,1)}), bf16[8,72,256]{2,1,0:T(8,128)(2,1)S(1)}, u32[]{:S(2)}, u32[]{:S(2)}) %all-to-all-start.2) | async-done | bytes 294944 | tf_op jit(solution)/shard_map/all_to_all | solution.py:23
  200.0 3.4 %all-to-all-start.3 = ((bf16[8,72,256]{2,1,0:T(8,128)(2,1)}), bf16[8,72,256]{2,1,0:T(8,128)(2,1)S(1)}, u32[]{:S(2)}, u32[]{:S(2)}) async-start(bf16[8,72,256]{2,1,0:T(8,128)(2,1)} %add_convert_fusion), calls=%async_computation.3 | async-start | bytes 589824 | tf_op jit(solution)/shard_map/all_to_all | solution.py:23
  203.5 5.4 %collect.1 = f32[3,1024,128]{2,1,0:T(8,128)} custom-call(s32[3,8,128]{2,1,0:T(8,128)} %bitcast.53, bf16[64,48,128]{2,1,0:T(8,128)(2,1)} %copy-done.3), custom_call_target="tpu_custom_call" | custom-call | tf_op jit(solution)/shard_map/collect/pallas_call | solution.py:210
  208.9 5.3 %all-to-all-done.3 = bf16[8,72,256]{2,1,0:T(8,128)(2,1)S(1)} async-done(((bf16[8,72,256]{2,1,0:T(8,128)(2,1)}), bf16[8,72,256]{2,1,0:T(8,128)(2,1)S(1)}, u32[]{:S(2)}, u32[]{:S(2)}) %all-to-all-start.3) | async-done | bytes 294944 | tf_op jit(solution)/shard_map/all_to_all | solution.py:23
  214.2 0.7 pad_maximum_fusion.1
  214.9 0.6 pad_maximum_fusion.3
  (82 shorter events, 3.2 us)
Async XLA Ops:
  33.7 9.3 %collective-permute-start.16 = (bf16[8,8,128]{2,1,0:T(8,128)(2,1)S(1)}, bf16[8,8,128]{2,1,0:T(8,128)(2,1)S(1)}, u32[]{:S(2)}, u32[]{:S(2)}) collective-permute-start(bf16[8,8,128]{2,1,0:T(8,128)(2,1)S(1)} %slice.75), channel_id=1, source_target_pairs={{0,8},{4,12},{8,0},{12,4},{1,9},{5,13},{9,1},{13,5},{2,10},{6,14},... | collective-permute-start | bytes 49160 | tf_op jit(solution)/shard_map/ppermute | solution.py:19
  36.7 8.2 %collective-permute-start.15 = (bf16[8,8,128]{2,1,0:T(8,128)(2,1)S(1)}, bf16[8,8,128]{2,1,0:T(8,128)(2,1)S(1)}, u32[]{:S(2)}, u32[]{:S(2)}) collective-permute-start(bf16[8,8,128]{2,1,0:T(8,128)(2,1)S(1)} %slice.75), channel_id=1, source_target_pairs={{0,4},{4,8},{8,12},{12,0},{1,5},{5,9},{9,13},{13,1},{2,6},{6,10},{... | collective-permute-start | bytes 49160 | tf_op jit(solution)/shard_map/ppermute | solution.py:19
  37.3 7.6 %collective-permute-start.17 = (bf16[8,8,128]{2,1,0:T(8,128)(2,1)S(1)}, bf16[8,8,128]{2,1,0:T(8,128)(2,1)S(1)}, u32[]{:S(2)}, u32[]{:S(2)}) collective-permute-start(bf16[8,8,128]{2,1,0:T(8,128)(2,1)S(1)} %slice.75), channel_id=1, source_target_pairs={{0,12},{4,0},{8,4},{12,8},{1,13},{5,1},{9,5},{13,9},{2,14},{6,2},{... | collective-permute-start | bytes 49160 | tf_op jit(solution)/shard_map/ppermute | solution.py:19
  40.0 47.9 %collective-permute-start.2 = (bf16[512,1024]{1,0:T(8,128)(2,1)}, bf16[512,1024]{1,0:T(8,128)(2,1)}, u32[]{:S(2)}, u32[]{:S(2)}) collective-permute-start(bf16[512,1024]{1,0:T(8,128)(2,1)} %refs_0_.3), channel_id=1, source_target_pairs={{0,3},{1,0},{2,1},{3,2},{4,7},{5,4},{6,5},{7,6},{8,11},{9,8},{10,9... | collective-permute-start | bytes 3145736 | tf_op jit(solution)/shard_map/ppermute | solution.py:19
  40.4 47.5 %collective-permute-start.1 = (bf16[512,1024]{1,0:T(8,128)(2,1)}, bf16[512,1024]{1,0:T(8,128)(2,1)}, u32[]{:S(2)}, u32[]{:S(2)}) collective-permute-start(bf16[512,1024]{1,0:T(8,128)(2,1)} %refs_0_.3), channel_id=1, source_target_pairs={{0,2},{1,3},{2,0},{3,1},{4,6},{5,7},{6,4},{7,5},{8,10},{9,11},{10,... | collective-permute-start | bytes 3145736 | tf_op jit(solution)/shard_map/ppermute | solution.py:19
  43.0 45.4 %collective-permute-start = (bf16[512,1024]{1,0:T(8,128)(2,1)}, bf16[512,1024]{1,0:T(8,128)(2,1)}, u32[]{:S(2)}, u32[]{:S(2)}) collective-permute-start(bf16[512,1024]{1,0:T(8,128)(2,1)} %refs_0_.3), channel_id=1, source_target_pairs={{0,1},{1,2},{2,3},{3,0},{4,5},{5,6},{6,7},{7,4},{8,9},{9,10},{10,1... | collective-permute-start | bytes 3145736 | tf_op jit(solution)/shard_map/ppermute | solution.py:19
  45.0 1.3 collective-permute-start.18
  55.0 62.2 %all-to-all-start.1 = ((bf16[64,48,128]{2,1,0:T(8,128)(2,1)}), bf16[64,48,128]{2,1,0:T(8,128)(2,1)}, u32[]{:S(2)}, u32[]{:S(2)}) async-start(bf16[64,48,128]{2,1,0:T(8,128)(2,1)} %pick.1), calls=%async_computation.1 | async-start | bytes 1572864 | tf_op jit(solution)/shard_map/all_to_all | solution.py:23
  60.5 23.3 %collective-permute-start.4 = (bf16[8,72,512]{2,1,0:T(8,128)(2,1)S(1)}, bf16[8,72,512]{2,1,0:T(8,128)(2,1)S(1)}, u32[]{:S(2)}, u32[]{:S(2)}) collective-permute-start(bf16[8,72,512]{2,1,0:T(8,128)(2,1)S(1)} %slice.72.refs_4_), channel_id=1, source_target_pairs={{0,12},{4,0},{8,4},{12,8},{1,13},{5,1},{9,5},{13,9},{2,14},{6,2},{... | collective-permute-start | bytes 1769480 | tf_op jit(solution)/shard_map/ppermute | solution.py:19
  63.2 23.9 %collective-permute-start.3 = (bf16[8,72,512]{2,1,0:T(8,128)(2,1)S(1)}, bf16[8,72,512]{2,1,0:T(8,128)(2,1)S(1)}, u32[]{:S(2)}, u32[]{:S(2)}) collective-permute-start(bf16[8,72,512]{2,1,0:T(8,128)(2,1)S(1)} %slice.72.refs_4_), channel_id=1, source_target_pairs={{0,4},{4,8},{8,12},{12,0},{1,5},{5,9},{9,13},{13,1},{2,6},{6,10},{... | collective-permute-start | bytes 1769480 | tf_op jit(solution)/shard_map/ppermute | solution.py:19
  83.8 9.4 %collective-permute-start.6 = (bf16[4,72,512]{2,1,0:T(8,128)(2,1)S(1)}, bf16[4,72,512]{2,1,0:T(8,128)(2,1)S(1)}, u32[]{:S(2)}, u32[]{:S(2)}) collective-permute-start(bf16[4,72,512]{2,1,0:T(8,128)(2,1)S(1)} %slice.74), channel_id=1, source_target_pairs={{0,12},{4,0},{8,4},{12,8},{1,13},{5,1},{9,5},{13,9},{2,14},{6,2},{... | collective-permute-start | bytes 884744 | tf_op jit(solution)/shard_map/ppermute | solution.py:19
  87.9 9.7 %collective-permute-start.5 = (bf16[4,72,512]{2,1,0:T(8,128)(2,1)}, bf16[4,72,512]{2,1,0:T(8,128)(2,1)S(1)}, u32[]{:S(2)}, u32[]{:S(2)}) collective-permute-start(bf16[4,72,512]{2,1,0:T(8,128)(2,1)} %slice.73), channel_id=1, source_target_pairs={{0,4},{4,8},{8,12},{12,0},{1,5},{5,9},{9,13},{13,1},{2,6},{6,10},{... | collective-permute-start | bytes 884744 | tf_op jit(solution)/shard_map/ppermute | solution.py:19
  87.9 17.0 %collective-permute-start.7 = (bf16[8,72,512]{2,1,0:T(8,128)(2,1)S(1)}, bf16[8,72,512]{2,1,0:T(8,128)(2,1)S(1)}, u32[]{:S(2)}, u32[]{:S(2)}) collective-permute-start(bf16[8,72,512]{2,1,0:T(8,128)(2,1)S(1)} %slice.72.refs_4_), channel_id=1, source_target_pairs={{0,128},{128,0},{1,129},{129,1},{2,130},{130,2},{3,131},{131,3},{4... | collective-permute-start | bytes 1769480 | tf_op jit(solution)/shard_map/ppermute | solution.py:19
  87.9 17.0 %collective-permute-start.9 = (bf16[8,72,512]{2,1,0:T(8,128)(2,1)S(1)}, bf16[8,72,512]{2,1,0:T(8,128)(2,1)}, u32[]{:S(2)}, u32[]{:S(2)}) collective-permute-start(bf16[8,72,512]{2,1,0:T(8,128)(2,1)S(1)} %collective-permute-done.4.refs_6_), channel_id=1, source_target_pairs={{0,128},{128,0},{1,129},{129,1},{2,130},{130,2},{3,131},{131,3},{4... | collective-permute-start | bytes 1769480 | tf_op jit(solution)/shard_map/ppermute | solution.py:19
  88.4 16.5 %collective-permute-start.8 = (bf16[8,72,512]{2,1,0:T(8,128)(2,1)S(1)}, bf16[8,72,512]{2,1,0:T(8,128)(2,1)}, u32[]{:S(2)}, u32[]{:S(2)}) collective-permute-start(bf16[8,72,512]{2,1,0:T(8,128)(2,1)S(1)} %collective-permute-done.3.refs_5_), channel_id=1, source_target_pairs={{0,128},{128,0},{1,129},{129,1},{2,130},{130,2},{3,131},{131,3},{4... | collective-permute-start | bytes 1769480 | tf_op jit(solution)/shard_map/ppermute | solution.py:19
  88.7 10.4 %copy-start.13 = (s32[4]{0:T(128)}, s32[4]{0:T(128)S(1)}, u32[]{:S(2)}) copy-start(s32[4]{0:T(128)S(1)} %get-tuple-element.67.place_ref) | copy-start | bytes 52
  93.3 11.7 %collective-permute-start.11 = (bf16[4,72,512]{2,1,0:T(8,128)(2,1)S(1)}, bf16[4,72,512]{2,1,0:T(8,128)(2,1)S(1)}, u32[]{:S(2)}, u32[]{:S(2)}) collective-permute-start(bf16[4,72,512]{2,1,0:T(8,128)(2,1)S(1)} %collective-permute-done.6.refs_8_), channel_id=1, source_target_pairs={{0,128},{128,0},{1,129},{129,1},{2,130},{130,2},{3,131},{131,3},{4... | collective-permute-start | bytes 884744 | tf_op jit(solution)/shard_map/ppermute | solution.py:19
  97.6 7.3 %collective-permute-start.10 = (bf16[4,72,512]{2,1,0:T(8,128)(2,1)S(1)}, bf16[4,72,512]{2,1,0:T(8,128)(2,1)}, u32[]{:S(2)}, u32[]{:S(2)}) collective-permute-start(bf16[4,72,512]{2,1,0:T(8,128)(2,1)S(1)} %collective-permute-done.5.refs_7_), channel_id=1, source_target_pairs={{0,128},{128,0},{1,129},{129,1},{2,130},{130,2},{3,131},{131,3},{4... | collective-permute-start | bytes 884744 | tf_op jit(solution)/shard_map/ppermute | solution.py:19
  112.3 0.8 copy-start
  113.1 0.8 copy-start.1
  113.9 9.4 %collective-permute-start.12 = (f32[512,128]{1,0:T(8,128)}, f32[512,128]{1,0:T(8,128)S(1)}, u32[]{:S(2)}, u32[]{:S(2)}) collective-permute-start(f32[512,128]{1,0:T(8,128)} %get-tuple-element.31), channel_id=1, source_target_pairs={{0,1},{1,2},{2,3},{3,0},{4,5},{5,6},{6,7},{7,4},{8,9},{9,10},{10,1... | collective-permute-start | bytes 786440 | tf_op jit(solution)/shard_map/ppermute | solution.py:19
  113.9 9.4 %collective-permute-start.13 = (f32[512,128]{1,0:T(8,128)}, f32[512,128]{1,0:T(8,128)S(1)}, u32[]{:S(2)}, u32[]{:S(2)}) collective-permute-start(f32[512,128]{1,0:T(8,128)} %get-tuple-element.32), channel_id=1, source_target_pairs={{0,3},{1,0},{2,1},{3,2},{4,7},{5,4},{6,5},{7,6},{8,11},{9,8},{10,9... | collective-permute-start | bytes 786440 | tf_op jit(solution)/shard_map/ppermute | solution.py:19
  115.9 13.6 %copy-start.9 = (bf16[512,128]{1,0:T(8,128)(2,1)S(1)}, bf16[512,128]{1,0:T(8,128)(2,1)}, u32[]{:S(2)}) copy-start(bf16[512,128]{1,0:T(8,128)(2,1)} %param.11) | copy-start | bytes 393220
  115.9 13.6 %collective-permute-start.14 = (f32[512,128]{1,0:T(8,128)}, f32[512,128]{1,0:T(8,128)S(1)}, u32[]{:S(2)}, u32[]{:S(2)}) collective-permute-start(f32[512,128]{1,0:T(8,128)} %get-tuple-element.33), channel_id=1, source_target_pairs={{0,2},{1,3},{2,0},{3,1},{4,6},{5,7},{6,4},{7,5},{8,10},{9,11},{10,... | collective-permute-start | bytes 786440 | tf_op jit(solution)/shard_map/ppermute | solution.py:19
  129.6 7.3 %copy-start.8 = (bf16[512,128]{1,0:T(8,128)(2,1)}, bf16[512,128]{1,0:T(8,128)(2,1)S(1)}, u32[]{:S(2)}) copy-start(bf16[512,128]{1,0:T(8,128)(2,1)S(1)} %get-tuple-element.56.refs_0_) | copy-start | bytes 393220
  131.1 13.4 %collective-permute-start.21 = (bf16[512,128]{1,0:T(8,128)(2,1)S(1)}, bf16[512,128]{1,0:T(8,128)(2,1)S(1)}, u32[]{:S(2)}, u32[]{:S(2)}) collective-permute-start(bf16[512,128]{1,0:T(8,128)(2,1)S(1)} %get-tuple-element.56.refs_0_), channel_id=1, source_target_pairs={{0,3},{1,0},{2,1},{3,2},{4,7},{5,4},{6,5},{7,6},{8,11},{9,8},{10,9... | collective-permute-start | bytes 393224 | tf_op jit(solution)/shard_map/ppermute | solution.py:19
  132.0 12.4 %collective-permute-start.20 = (bf16[512,128]{1,0:T(8,128)(2,1)S(1)}, bf16[512,128]{1,0:T(8,128)(2,1)S(1)}, u32[]{:S(2)}, u32[]{:S(2)}) collective-permute-start(bf16[512,128]{1,0:T(8,128)(2,1)S(1)} %get-tuple-element.56.refs_0_), channel_id=1, source_target_pairs={{0,2},{1,3},{2,0},{3,1},{4,6},{5,7},{6,4},{7,5},{8,10},{9,11},{10,... | collective-permute-start | bytes 393224 | tf_op jit(solution)/shard_map/ppermute | solution.py:19
  133.4 11.1 %collective-permute-start.19 = (bf16[512,128]{1,0:T(8,128)(2,1)S(1)}, bf16[512,128]{1,0:T(8,128)(2,1)S(1)}, u32[]{:S(2)}, u32[]{:S(2)}) collective-permute-start(bf16[512,128]{1,0:T(8,128)(2,1)S(1)} %get-tuple-element.56.refs_0_), channel_id=1, source_target_pairs={{0,1},{1,2},{2,3},{3,0},{4,5},{5,6},{6,7},{7,4},{8,9},{9,10},{10,1... | collective-permute-start | bytes 393224 | tf_op jit(solution)/shard_map/ppermute | solution.py:19
  136.9 45.1 %all-to-all-start.4 = ((bf16[64,48,128]{2,1,0:T(8,128)(2,1)}), bf16[64,48,128]{2,1,0:T(8,128)(2,1)S(1)}, u32[]{:S(2)}, u32[]{:S(2)}) async-start(bf16[64,48,128]{2,1,0:T(8,128)(2,1)} %pad_maximum_fusion), calls=%async_computation.4 | async-start | bytes 1572864 | tf_op jit(solution)/shard_map/all_to_all | solution.py:23
  144.5 0.7 copy-start.10
  144.5 0.7 copy-start.11
  144.5 0.7 copy-start.12
  151.4 4.3 %collective-permute-start.22 = (bf16[2048,256]{1,0:T(8,128)(2,1)}, bf16[2048,256]{1,0:T(8,128)(2,1)S(1)}, u32[]{:S(2)}, u32[]{:S(2)}) collective-permute-start(bf16[2048,256]{1,0:T(8,128)(2,1)} %get-tuple-element.43), channel_id=1, source_target_pairs={{0,128},{128,0},{1,129},{129,1},{2,130},{130,2},{3,131},{131,3},{4... | collective-permute-start | bytes 3145736 | tf_op jit(solution)/shard_map/ppermute | solution.py:19
  151.4 4.4 %collective-permute-start.23 = (f32[4,128,512]{2,1,0:T(8,128)}, f32[4,128,512]{2,1,0:T(8,128)S(1)}, u32[]{:S(2)}, u32[]{:S(2)}) collective-permute-start(f32[4,128,512]{2,1,0:T(8,128)} %get-tuple-element.44), channel_id=1, source_target_pairs={{0,128},{128,0},{1,129},{129,1},{2,130},{130,2},{3,131},{131,3},{4... | collective-permute-start | bytes 3145736 | tf_op jit(solution)/shard_map/ppermute | solution.py:19
  155.2 11.8 %collective-permute-start.27 = (bf16[2048,256]{1,0:T(8,128)(2,1)}, bf16[2048,256]{1,0:T(8,128)(2,1)S(1)}, u32[]{:S(2)}, u32[]{:S(2)}) collective-permute-start(bf16[2048,256]{1,0:T(8,128)(2,1)} %convolution_convert_fusion), channel_id=1, source_target_pairs={{0,128},{128,0},{1,129},{129,1},{2,130},{130,2},{3,131},{131,3},{4... | collective-permute-start | bytes 3145736 | tf_op jit(solution)/shard_map/ppermute | solution.py:19
  155.7 1.0 copy-start.5
  156.7 1.0 copy-start.2
  161.2 11.8 %collective-permute-start.24 = (bf16[8,72,256]{2,1,0:T(8,128)(2,1)}, bf16[8,72,256]{2,1,0:T(8,128)(2,1)S(1)}, u32[]{:S(2)}, u32[]{:S(2)}) collective-permute-start(bf16[8,72,256]{2,1,0:T(8,128)(2,1)} %get-tuple-element.46), channel_id=1, source_target_pairs={{0,4},{4,8},{8,12},{12,0},{1,5},{5,9},{9,13},{13,1},{2,6},{6,10},{... | collective-permute-start | bytes 884744 | tf_op jit(solution)/shard_map/ppermute | solution.py:19
  162.8 17.2 %collective-permute-start.25 = (bf16[8,72,256]{2,1,0:T(8,128)(2,1)}, bf16[8,72,256]{2,1,0:T(8,128)(2,1)}, u32[]{:S(2)}, u32[]{:S(2)}) collective-permute-start(bf16[8,72,256]{2,1,0:T(8,128)(2,1)} %get-tuple-element.47), channel_id=1, source_target_pairs={{0,8},{4,12},{8,0},{12,4},{1,9},{5,13},{9,1},{13,5},{2,10},{6,14},... | collective-permute-start | bytes 884744 | tf_op jit(solution)/shard_map/ppermute | solution.py:19
  165.5 14.5 %copy-start.7 = (f32[8,72,256]{2,1,0:T(8,128)S(1)}, f32[8,72,256]{2,1,0:T(8,128)}, u32[]{:S(2)}) copy-start(f32[8,72,256]{2,1,0:T(8,128)} %get-tuple-element.45) | copy-start | bytes 1769476
  165.5 14.5 %collective-permute-start.26 = (bf16[8,72,256]{2,1,0:T(8,128)(2,1)}, bf16[8,72,256]{2,1,0:T(8,128)(2,1)}, u32[]{:S(2)}, u32[]{:S(2)}) collective-permute-start(bf16[8,72,256]{2,1,0:T(8,128)(2,1)} %get-tuple-element.48), channel_id=1, source_target_pairs={{0,12},{4,0},{8,4},{12,8},{1,13},{5,1},{9,5},{13,9},{2,14},{6,2},{... | collective-permute-start | bytes 884744 | tf_op jit(solution)/shard_map/ppermute | solution.py:19
  167.0 1.0 copy-start.4
  171.5 20.7 %copy-start.6 = (f32[8,72,256]{2,1,0:T(8,128)S(1)}, f32[8,72,256]{2,1,0:T(8,128)}, u32[]{:S(2)}) copy-start(f32[8,72,256]{2,1,0:T(8,128)} %get-tuple-element.49) | copy-start | bytes 1769476
  171.5 17.2 %collective-permute-start.28 = (bf16[8,72,256]{2,1,0:T(8,128)(2,1)}, bf16[8,72,256]{2,1,0:T(8,128)(2,1)S(1)}, u32[]{:S(2)}, u32[]{:S(2)}) collective-permute-start(bf16[8,72,256]{2,1,0:T(8,128)(2,1)} %get-tuple-element.50), channel_id=1, source_target_pairs={{0,4},{4,8},{8,12},{12,0},{1,5},{5,9},{9,13},{13,1},{2,6},{6,10},{... | collective-permute-start | bytes 884744 | tf_op jit(solution)/shard_map/ppermute | solution.py:19
  172.2 20.1 %collective-permute-start.29 = (bf16[8,72,256]{2,1,0:T(8,128)(2,1)}, bf16[8,72,256]{2,1,0:T(8,128)(2,1)S(1)}, u32[]{:S(2)}, u32[]{:S(2)}) collective-permute-start(bf16[8,72,256]{2,1,0:T(8,128)(2,1)} %get-tuple-element.51), channel_id=1, source_target_pairs={{0,8},{4,12},{8,0},{12,4},{1,9},{5,13},{9,1},{13,5},{2,10},{6,14},... | collective-permute-start | bytes 884744 | tf_op jit(solution)/shard_map/ppermute | solution.py:19
  173.1 19.2 %collective-permute-start.30 = (bf16[8,72,256]{2,1,0:T(8,128)(2,1)}, bf16[8,72,256]{2,1,0:T(8,128)(2,1)S(1)}, u32[]{:S(2)}, u32[]{:S(2)}) collective-permute-start(bf16[8,72,256]{2,1,0:T(8,128)(2,1)} %get-tuple-element.52), channel_id=1, source_target_pairs={{0,12},{4,0},{8,4},{12,8},{1,13},{5,1},{9,5},{13,9},{2,14},{6,2},{... | collective-permute-start | bytes 884744 | tf_op jit(solution)/shard_map/ppermute | solution.py:19
  182.0 21.5 %copy-start.3 = (bf16[64,48,128]{2,1,0:T(8,128)(2,1)}, bf16[64,48,128]{2,1,0:T(8,128)(2,1)S(1)}, u32[]{:S(2)}) copy-start(bf16[64,48,128]{2,1,0:T(8,128)(2,1)S(1)} %all-to-all-done.4.in_ref) | copy-start | bytes 2359300
  182.0 18.0 %all-to-all-start.2 = ((bf16[8,72,256]{2,1,0:T(8,128)(2,1)}), bf16[8,72,256]{2,1,0:T(8,128)(2,1)S(1)}, u32[]{:S(2)}, u32[]{:S(2)}) async-start(bf16[8,72,256]{2,1,0:T(8,128)(2,1)} %add_convert_fusion.1), calls=%async_computation.2 | async-start | bytes 589824 | tf_op jit(solution)/shard_map/all_to_all | solution.py:23
  200.0 14.2 %all-to-all-start.3 = ((bf16[8,72,256]{2,1,0:T(8,128)(2,1)}), bf16[8,72,256]{2,1,0:T(8,128)(2,1)S(1)}, u32[]{:S(2)}, u32[]{:S(2)}) async-start(bf16[8,72,256]{2,1,0:T(8,128)(2,1)} %add_convert_fusion), calls=%async_computation.3 | async-start | bytes 589824 | tf_op jit(solution)/shard_map/all_to_all | solution.py:23

commit v4 on v3

--- a/solution.py
+++ b/solution.py
@@ -49,32 +49,33 @@
         o_refs, refs = refs[:many], refs[many:]
         hid_ref, slope_ref, wo_ref = refs[:3]
         lat_refs, (w_ref, wo32_ref) = refs[3:3 + ny], refs[3 + ny:]
-        for (k, low, high), *pair in zip(spans, n_refs, o_refs):
-            xk = place_ref[k]
-            for r, ref in enumerate(pair):
-                for zh in range(low, high):
-                    p = r * (ny // 2) + zh
-                    cut = ref[(zh - low) * hz:(zh - low + 1) * hz]
-                    w_ref[p, :, xk] = cut[:, :in_rows]
-                    wo32_ref[p, :, xk] = cut[:, in_rows:].astype(F32)
-        for p in range(ny):
-            wo_ref[p] = wo32_ref[p].reshape(width, hid).astype(BF)
-
-        def step(t, carry):
-            rows = pl.ds(t * tile, tile)
-            acc = None
-            for k in range(ny):
-                part = mm(f_refs[k][rows, :], w_ref[place_ref[nx + k]].reshape(depth, hid))
-                acc = part if acc is None else acc + part
-            logistic = jax.nn.sigmoid(acc)
-            hidden = (acc * logistic).astype(BF)
-            hid_ref[rows, :] = hidden
-            slope_ref[rows, :] = logistic * (1.0 + acc * (1.0 - logistic))
-            for j in range(ny):
-                lat_refs[j][rows, :] = mm(hidden, wo_ref[place_ref[nx + ny + j]], ((1,), (1,)))
-            return carry
-
-        lax.fori_loop(0, items // tile, step, 0)
+
+        @pl.when(pl.program_id(0) == 0)
+        def _():
+            for (k, low, high), *pair in zip(spans, n_refs, o_refs):
+                xk = place_ref[k]
+                for r, ref in enumerate(pair):
+                    for zh in range(low, high):
+                        p = r * (ny // 2) + zh
+                        cut = ref[(zh - low) * hz:(zh - low + 1) * hz]
+                        w_ref[p, :, xk] = cut[:, :in_rows]
+                        wo32_ref[p, :, xk] = cut[:, in_rows:].astype(F32)
+            for p in range(ny):
+                wo_ref[p] = wo32_ref[p].reshape(width, hid).astype(BF)
+
+        acc = None
+        for k in range(ny):
+            part = mm(f_refs[k][...], w_ref[place_ref[nx + k]].reshape(depth, hid))
+            acc = part if acc is None else acc + part
+        logistic = jax.nn.sigmoid(acc)
+        hidden = (acc * logistic).astype(BF)
+        hid_ref[...] = hidden
+        slope_ref[...] = logistic * (1.0 + acc * (1.0 - logistic))
+        for j in range(ny):
+            lat_refs[j][...] = mm(hidden, wo_ref[place_ref[nx + ny + j]], ((1,), (1,)))
+
+    def rows(cols):
+        return pl.BlockSpec((tile, cols), lambda t: (t, 0))
 
     return pl.pallas_call(
         kernel,
@@ -83,15 +84,16 @@
             jax.ShapeDtypeStruct((items, hid), F32),
             jax.ShapeDtypeStruct((ny, width, hid), BF),
         ] + [jax.ShapeDtypeStruct((items, width), F32)] * ny,
-        in_specs=[SMEM] + [VMEM] * (ny + 2 * many),
-        out_specs=[VMEM] * (3 + ny),
+        grid=(items // tile,),
+        in_specs=[SMEM] + [rows(depth)] * ny + [VMEM] * (2 * many),
+        out_specs=[rows(hid)] * 2 + [pl.BlockSpec((ny, width, hid), lambda t: (0, 0, 0))] + [rows(width)] * ny,
         scratch_shapes=[
             pltpu.VMEM((ny, hz, nx, in_rows, hid), BF),
             pltpu.VMEM((ny, hz, nx, out_rows, hid), F32),
         ],
-        compiler_params=pltpu.CompilerParams(vmem_limit_bytes=48 * 1024 * 1024),
         cost_estimate=pl.CostEstimate(
             flops=2 * items * hid * ny * (depth + width), bytes_accessed=12 << 20, transcendentals=items * hid),
+        compiler_params=pltpu.CompilerParams(vmem_limit_bytes=48 << 20),
         name="encode",
     )(place, *feats, *near, *other)
 
@@ -216,6 +218,7 @@
             pl.BlockSpec((owners, cap, width), lambda l: (0, l, 0)),
         ],
         out_specs=pl.BlockSpec((1, rows_own, width), lambda l: (l, 0, 0)),
+        compiler_params=pltpu.CompilerParams(vmem_limit_bytes=12 << 20),
         name="collect",
     )(asked, incoming)
 
@@ -259,11 +262,9 @@
 
     def kernel(place_ref, *refs):
         g_refs, (hid_ref, slope_ref, wo_ref, f_ref, pre_ref, out_ref, there_ref) = refs[:ny], refs[ny:]
-        acc = None
-        for k in range(ny):
-            part = mm(g_refs[k][...], wo_ref[place_ref[k]])
-            acc = part if acc is None else acc + part
-        pre_ref[...] = (acc * slope_ref[...]).astype(BF)
+        grads_all = jnp.concatenate([g_refs[k][...] for k in range(ny)], axis=1)
+        w_all = jnp.concatenate([wo_ref[place_ref[k]] for k in range(ny)], axis=0)
+        pre_ref[...] = (mm(grads_all, w_all) * slope_ref[...]).astype(BF)
 
         def product(t, carry):
             cut = pl.ds(pl.multiple_of(t * 512, 512), 512)
@@ -271,8 +272,9 @@
             return carry
 
         lax.fori_loop(0, rows // 512, product, 0)
+        outs = mm(grads_all, hid_ref[...], ((0,), (0,)))
         for k in range(ny):
-            out_ref[place_ref[k]] = mm(g_refs[k][...], hid_ref[...], ((0,), (0,)))
+            out_ref[place_ref[k]] = outs[k * width:(k + 1) * width]
 
     return pl.pallas_call(
         kernel,
@@ -332,6 +334,7 @@
         scratch_shapes=[pltpu.VMEM((nx, both, hid), F32)],
         cost_estimate=pl.CostEstimate(
             flops=2 * nz * nx * in_rows * items * hid, bytes_accessed=8 << 20, transcendentals=0),
+        compiler_params=pltpu.CompilerParams(vmem_limit_bytes=16 << 20),
         name="cut_by_x",
     )(order, feats_t, pre, came, out_mine, out_came)
 

time: 218 us -> 213 us (0.977)
  waiting for transfers between devices: 61.1 us -> 69.6 us
  Pallas kernels: 43.5 us -> 37.9 us
  local copies, waits for them, and re-layouts: 9.76 us -> 6.9 us
    ppermute x31, waiting for transfers between devices: 48.9 us -> 58.1 us  [shift(): lax.ppermute(value, axis, [(i, (i + by) % size) for i in range(size)])]
    pallas_call x2, Pallas kernels: 7.09 us -> 3.17 us  [cut_by_x(): pl.pallas_call(kernel, out_shape=[jax.ShapeDtypeStruct((nz, both, hid), F...]
    unnamed x29 -> x27, local copies, waits for them, and re-layouts: 5.85 us -> 2.99 us
  transfers between devices with their start and end apart: 35 -> 35, of which waited for: 11 -> 13; matrix products, arithmetic and copies ran while one was open for 6% -> 5% of each run, Pallas kernels for 18% -> 16%
where the time goes in v4:
time: 213 us; the launch traced here: 211 us
  waiting for transfers between devices  69.6 us (33%)
  starting transfers between devices  57.3 us (27%)
  Pallas kernels  37.9 us (18%)
  blocking collectives  28.8 us (14%)
  local copies, waits for them, and re-layouts  6.9 us (3%)
  matrix products  4.98 us (2%)
  other arithmetic  4.37 us (2%)
    ppermute x31, waiting for transfers between devices, shift(): lax.ppermute(value, axis, [(i, (i + by) % size) for i in range(size)])  58.1 us
    ppermute x31, starting transfers between devices, shift(): lax.ppermute(value, axis, [(i, (i + by) % size) for i in range(size)])  35.1 us
    all_to_all x1, blocking collectives, exchange(): return lax.all_to_all(value, axis, split_axis=0, concat_axis=0, tiled=True)  28.8 us
    all_to_all x4, starting transfers between devices, exchange(): return lax.all_to_all(value, axis, split_axis=0, concat_axis=0, tiled=True)  22.1 us
    all_to_all x4, waiting for transfers between devices, exchange(): return lax.all_to_all(value, axis, split_axis=0, concat_axis=0, tiled=True)  11.5 us
    pallas_call x1, Pallas kernels, pick(): pl.pallas_call(kernel, out_shape=jax.ShapeDtypeStruct((owners, levels * c...  7.34 us
    pallas_call x1, Pallas kernels, encode(): pl.pallas_call(kernel, out_shape=[jax.ShapeDtypeStruct((items, hid), BF),...  6.75 us
    pallas_call x1, Pallas kernels, back(): pl.pallas_call(kernel, out_shape=[jax.ShapeDtypeStruct((items, hid), BF),...  6.03 us
  transfers between devices with their start and end apart: 35, of which 13 were waited for; matrix products, arithmetic and copies ran while one was open for 5% of the time, Pallas kernels for 16%

profile of v4, /device:TPU:8, one launch (start us, length us, event | category | flops | bytes accessed | tf_op | source)
XLA Modules:
  0.0 210.8 jit_solution(5456705162223823488)
XLA Ops:
  0.6 4.3 %ask.1 = (s32[3,512,1]{2,1,0:T(8,128)}, bf16[8,80,512]{2,1,0:T(8,128)(2,1)}) custom-call(s32[3,512]{1,0:T(4,128)} %codes_ref.1, bf16[64,512]{1,0:T(8,128)(2,1)} %wi_ref.1, bf16[8,512]{1,0:T(8,128)(2,1)} %wo_ref.1), custom_call_target="tpu_custom_call" | custom-call | tf_op jit(solution)/shard_map/ask/pallas_call | solution.py:145
  4.9 28.8 %all_to_all.25 = bf16[8,80,512]{2,1,0:T(8,128)(2,1)S(1)} all-to-all(bf16[8,80,512]{2,1,0:T(8,128)(2,1)} %get-tuple-element.29), channel_id=1, replica_groups=mesh['s'=2,'z'=8,'x'=4,'y'=4] {'z'}, dimensions={0} | all-to-all | bytes 1310720 | tf_op jit(solution)/shard_map/all_to_all | solution.py:23
  33.7 3.0 %collective-permute-start.16 = (bf16[8,8,128]{2,1,0:T(8,128)(2,1)S(1)}, bf16[8,8,128]{2,1,0:T(8,128)(2,1)S(1)}, u32[]{:S(2)}, u32[]{:S(2)}) collective-permute-start(bf16[8,8,128]{2,1,0:T(8,128)(2,1)S(1)} %slice.75), channel_id=1, source_target_pairs={{0,8},{4,12},{8,0},{12,4},{1,9},{5,13},{9,1},{13,5},{2,10},{6,14},... | collective-permute-start | bytes 49160 | tf_op jit(solution)/shard_map/ppermute | solution.py:19
  36.7 0.6 collective-permute-start.15
  37.3 2.6 %collective-permute-start.17 = (bf16[8,8,128]{2,1,0:T(8,128)(2,1)S(1)}, bf16[8,8,128]{2,1,0:T(8,128)(2,1)S(1)}, u32[]{:S(2)}, u32[]{:S(2)}) collective-permute-start(bf16[8,8,128]{2,1,0:T(8,128)(2,1)S(1)} %slice.75), channel_id=1, source_target_pairs={{0,12},{4,0},{8,4},{12,8},{1,13},{5,1},{9,5},{13,9},{2,14},{6,2},{... | collective-permute-start | bytes 49160 | tf_op jit(solution)/shard_map/ppermute | solution.py:19
  40.4 2.6 %collective-permute-start.1 = (bf16[512,1024]{1,0:T(8,128)(2,1)}, bf16[512,1024]{1,0:T(8,128)(2,1)}, u32[]{:S(2)}, u32[]{:S(2)}) collective-permute-start(bf16[512,1024]{1,0:T(8,128)(2,1)} %refs_0_.3), channel_id=1, source_target_pairs={{0,2},{1,3},{2,0},{3,1},{4,6},{5,7},{6,4},{7,5},{8,10},{9,11},{10,... | collective-permute-start | bytes 3145736 | tf_op jit(solution)/shard_map/ppermute | solution.py:19
  43.0 1.9 collective-permute-start
  45.1 1.2 collective-permute-done.18
  47.1 0.6 copy.13
  47.7 7.3 %pick.1 = bf16[64,48,128]{2,1,0:T(8,128)(2,1)} custom-call(s32[3,8,128]{2,1,0:T(8,128)} %bitcast.44, bf16[3,1024,128]{2,1,0:T(8,128)(2,1)} %book_ref.1), custom_call_target="tpu_custom_call" | custom-call | tf_op jit(solution)/shard_map/pick/pallas_call | solution.py:179
  55.0 5.5 %all-to-all-start.1 = ((bf16[64,48,128]{2,1,0:T(8,128)(2,1)}), bf16[64,48,128]{2,1,0:T(8,128)(2,1)}, u32[]{:S(2)}, u32[]{:S(2)}) async-start(bf16[64,48,128]{2,1,0:T(8,128)(2,1)} %pick.1), calls=%async_computation.1 | async-start | bytes 1572864 | tf_op jit(solution)/shard_map/all_to_all | solution.py:23
  60.5 2.7 %collective-permute-start.4 = (bf16[8,72,512]{2,1,0:T(8,128)(2,1)S(1)}, bf16[8,72,512]{2,1,0:T(8,128)(2,1)S(1)}, u32[]{:S(2)}, u32[]{:S(2)}) collective-permute-start(bf16[8,72,512]{2,1,0:T(8,128)(2,1)S(1)} %slice.72.refs_4_), channel_id=1, source_target_pairs={{0,12},{4,0},{8,4},{12,8},{1,13},{5,1},{9,5},{13,9},{2,14},{6,2},{... | collective-permute-start | bytes 1769480 | tf_op jit(solution)/shard_map/ppermute | solution.py:19
  63.2 20.6 %collective-permute-done.4.refs_6_ = bf16[8,72,512]{2,1,0:T(8,128)(2,1)S(1)} collective-permute-done((bf16[8,72,512]{2,1,0:T(8,128)(2,1)S(1)}, bf16[8,72,512]{2,1,0:T(8,128)(2,1)S(1)}, u32[]{:S(2)}, u32[]{:S(2)}) %collective-permute-start.4) | collective-permute-done | bytes 589856 | tf_op jit(solution)/shard_map/ppermute | solution.py:19
  83.8 3.3 %collective-permute-start.6 = (bf16[4,72,512]{2,1,0:T(8,128)(2,1)S(1)}, bf16[4,72,512]{2,1,0:T(8,128)(2,1)S(1)}, u32[]{:S(2)}, u32[]{:S(2)}) collective-permute-start(bf16[4,72,512]{2,1,0:T(8,128)(2,1)S(1)} %slice.74), channel_id=1, source_target_pairs={{0,12},{4,0},{8,4},{12,8},{1,13},{5,1},{9,5},{13,9},{2,14},{6,2},{... | collective-permute-start | bytes 884744 | tf_op jit(solution)/shard_map/ppermute | solution.py:19
  87.1 0.7 slice.73
  87.9 0.5 collective-permute-start.9
  88.7 4.6 %collective-permute-done.6.refs_8_ = bf16[4,72,512]{2,1,0:T(8,128)(2,1)S(1)} collective-permute-done((bf16[4,72,512]{2,1,0:T(8,128)(2,1)S(1)}, bf16[4,72,512]{2,1,0:T(8,128)(2,1)S(1)}, u32[]{:S(2)}, u32[]{:S(2)}) %collective-permute-start.6) | collective-permute-done | bytes 294944 | tf_op jit(solution)/shard_map/ppermute | solution.py:19
  93.2 4.4 %collective-permute-done.5.refs_7_ = bf16[4,72,512]{2,1,0:T(8,128)(2,1)S(1)} collective-permute-done((bf16[4,72,512]{2,1,0:T(8,128)(2,1)}, bf16[4,72,512]{2,1,0:T(8,128)(2,1)S(1)}, u32[]{:S(2)}, u32[]{:S(2)}) %collective-permute-start.5) | collective-permute-done | bytes 294944 | tf_op jit(solution)/shard_map/ppermute | solution.py:19
  97.7 1.4 slice_reduce_fusion
  99.1 5.8 %turn.1 = (bf16[2,1024,512]{2,1,0:T(8,128)(2,1)}, bf16[2,1024,512]{2,1,0:T(8,128)(2,1)}) custom-call(s32[4]{0:T(128)} %copy-done.12, bf16[512,1024]{1,0:T(8,128)(2,1)} %refs_0_.3, bf16[512,1024]{1,0:T(8,128)(2,1)} %collective-permute-done.refs_1_, bf16[512,1024]{1,0:T(8,128)(2,1)} %collective-permute-done.1.refs_2_, ...), custom_call_target="tpu_custom_call" | custom-call | bytes 8388608 | tf_op jit(solution)/shard_map/turn/pallas_call | solution.py:247
  105.0 6.7 %encode.1 = (bf16[512,512]{1,0:T(8,128)(2,1)S(1)}, f32[512,512]{1,0:T(8,128)}, bf16[4,128,512]{2,1,0:T(8,128)(2,1)S(1)}, f32[512,128]{1,0:T(8,128)S(1)}, f32[512...) custom-call(s32[12]{0:T(128)S(1)} %pad_add_fusion.place_ref, bf16[512,1024]{1,0:T(8,128)(2,1)} %refs_0_.3, ...), custom_call_target="tpu_custom_call" | custom-call | flops 2415919104 | bytes 12582912 | tf_op jit(solution)/shard_map/encode/pallas_call | solution.py:80
  111.7 0.8 copy-done.3
  112.5 0.8 copy-done.4
  113.3 2.0 collective-permute-start.13
  115.3 1.3 collective-permute-start.14
  116.7 1.3 fusion.34
  117.9 0.5 fusion.2
  118.4 0.5 fusion.1
  118.9 0.5 fusion
  119.5 3.2 %collective-permute-done.12 = f32[512,128]{1,0:T(8,128)S(1)} collective-permute-done((f32[512,128]{1,0:T(8,128)}, f32[512,128]{1,0:T(8,128)S(1)}, u32[]{:S(2)}, u32[]{:S(2)}) %collective-permute-start.12) | collective-permute-done | bytes 262176 | tf_op jit(solution)/shard_map/ppermute | solution.py:19
  122.7 6.2 %collective-permute-done.14 = f32[512,128]{1,0:T(8,128)S(1)} collective-permute-done((f32[512,128]{1,0:T(8,128)}, f32[512,128]{1,0:T(8,128)S(1)}, u32[]{:S(2)}, u32[]{:S(2)}) %collective-permute-start.14) | collective-permute-done | bytes 262176 | tf_op jit(solution)/shard_map/ppermute | solution.py:19
  129.0 0.5 fusion.6
  129.5 0.5 fusion.7
  130.0 0.5 fusion.8
  130.5 1.0 collective-permute-start.21
  131.4 1.4 collective-permute-start.20
  132.8 2.5 %collective-permute-start.19 = (bf16[512,128]{1,0:T(8,128)(2,1)S(1)}, bf16[512,128]{1,0:T(8,128)(2,1)S(1)}, u32[]{:S(2)}, u32[]{:S(2)}) collective-permute-start(bf16[512,128]{1,0:T(8,128)(2,1)S(1)} %get-tuple-element.56.refs_0_), channel_id=1, source_target_pairs={{0,1},{1,2},{2,3},{3,0},{4,5},{5,6},{6,7},{7,4},{8,9},{9,10},{10,1... | collective-permute-start | bytes 393224 | tf_op jit(solution)/shard_map/ppermute | solution.py:19
  135.4 0.9 pad_maximum_fusion
  136.3 7.5 %all-to-all-start.4 = ((bf16[64,48,128]{2,1,0:T(8,128)(2,1)}), bf16[64,48,128]{2,1,0:T(8,128)(2,1)S(1)}, u32[]{:S(2)}, u32[]{:S(2)}) async-start(bf16[64,48,128]{2,1,0:T(8,128)(2,1)} %pad_maximum_fusion), calls=%async_computation.4 | async-start | bytes 1572864 | tf_op jit(solution)/shard_map/all_to_all | solution.py:23
  143.9 0.6 copy-done.9
  144.7 6.0 %back.1 = (bf16[512,512]{1,0:T(8,128)(2,1)}, f32[4,128,512]{2,1,0:T(8,128)}, bf16[2048,256]{1,0:T(8,128)(2,1)}) custom-call(s32[4]{0:T(128)} %copy-done.12, bf16[512,128]{1,0:T(8,128)(2,1)} %copy-done.7, bf16[512,128]{1,0:T(8,128)(2,1)} %copy-done.11, bf16[512,128]{1,0:T(8,128)(2,1)} %copy-done.10, bf16[512,128]{1,0:T(8,128)(2,1)} %copy-done.9, ...), custom_call_target="tpu_custom_call" | custom-call | flops 805306368 | bytes 6291456 | tf_op jit(solution)/shard_map/back/pallas_call | solution.py:279
  150.7 0.5 collective-permute-start.23
  151.2 1.8 convolution_convert_fusion
  153.6 1.5 collective-permute-done.23
  155.1 1.6 cut_by_x.2
  156.7 1.4 collective-permute-start.24
  158.1 2.7 %collective-permute-start.25 = (bf16[8,72,256]{2,1,0:T(8,128)(2,1)S(1)}, bf16[8,72,256]{2,1,0:T(8,128)(2,1)S(1)}, u32[]{:S(2)}, u32[]{:S(2)}) collective-permute-start(bf16[8,72,256]{2,1,0:T(8,128)(2,1)S(1)} %get-tuple-element.47), channel_id=1, source_target_pairs={{0,8},{4,12},{8,0},{12,4},{1,9},{5,13},{9,1},{13,5},{2,10},{6,14},... | collective-permute-start | bytes 884744 | tf_op jit(solution)/shard_map/ppermute | solution.py:19
  160.8 1.5 collective-permute-start.26
  162.3 1.6 cut_by_x.3
  163.8 0.6 collective-permute-start.28
  164.5 0.9 collective-permute-start.29
  165.4 4.5 %collective-permute-done.24 = bf16[8,72,256]{2,1,0:T(8,128)(2,1)S(1)} collective-permute-done((bf16[8,72,256]{2,1,0:T(8,128)(2,1)S(1)}, bf16[8,72,256]{2,1,0:T(8,128)(2,1)S(1)}, u32[]{:S(2)}, u32[]{:S(2)}) %collective-permute-start.24) | collective-permute-done | bytes 294944 | tf_op jit(solution)/shard_map/ppermute | solution.py:19
  169.8 1.1 collective-permute-start.30
  171.0 5.8 %collective-permute-done.25 = bf16[8,72,256]{2,1,0:T(8,128)(2,1)S(1)} collective-permute-done((bf16[8,72,256]{2,1,0:T(8,128)(2,1)S(1)}, bf16[8,72,256]{2,1,0:T(8,128)(2,1)S(1)}, u32[]{:S(2)}, u32[]{:S(2)}) %collective-permute-start.25) | collective-permute-done | bytes 294944 | tf_op jit(solution)/shard_map/ppermute | solution.py:19
  176.8 0.9 add_convert_fusion.1
  177.7 5.7 %all-to-all-start.2 = ((bf16[8,72,256]{2,1,0:T(8,128)(2,1)}), bf16[8,72,256]{2,1,0:T(8,128)(2,1)S(1)}, u32[]{:S(2)}, u32[]{:S(2)}) async-start(bf16[8,72,256]{2,1,0:T(8,128)(2,1)} %add_convert_fusion.1), calls=%async_computation.2 | async-start | bytes 589824 | tf_op jit(solution)/shard_map/all_to_all | solution.py:23
  183.4 5.8 %collective-permute-done.29 = bf16[8,72,256]{2,1,0:T(8,128)(2,1)S(1)} collective-permute-done((bf16[8,72,256]{2,1,0:T(8,128)(2,1)S(1)}, bf16[8,72,256]{2,1,0:T(8,128)(2,1)S(1)}, u32[]{:S(2)}, u32[]{:S(2)}) %collective-permute-start.29) | collective-permute-done | bytes 294944 | tf_op jit(solution)/shard_map/ppermute | solution.py:19
  189.1 0.9 add_convert_fusion
  190.0 5.3 %all-to-all-done.2 = bf16[8,72,256]{2,1,0:T(8,128)(2,1)S(1)} async-done(((bf16[8,72,256]{2,1,0:T(8,128)(2,1)}), bf16[8,72,256]{2,1,0:T(8,128)(2,1)S(1)}, u32[]{:S(2)}, u32[]{:S(2)}) %all-to-all-start.2) | async-done | bytes 294944 | tf_op jit(solution)/shard_map/all_to_all | solution.py:23
  195.3 3.4 %all-to-all-start.3 = ((bf16[8,72,256]{2,1,0:T(8,128)(2,1)}), bf16[8,72,256]{2,1,0:T(8,128)(2,1)S(1)}, u32[]{:S(2)}, u32[]{:S(2)}) async-start(bf16[8,72,256]{2,1,0:T(8,128)(2,1)} %add_convert_fusion), calls=%async_computation.3 | async-start | bytes 589824 | tf_op jit(solution)/shard_map/all_to_all | solution.py:23
  198.7 4.5 %collect.1 = f32[3,1024,128]{2,1,0:T(8,128)} custom-call(s32[3,8,128]{2,1,0:T(8,128)S(1)} %bitcast.45, bf16[64,48,128]{2,1,0:T(8,128)(2,1)S(1)} %all-to-all-done.4.in_ref), custom_call_target="tpu_custom_call" | custom-call | tf_op jit(solution)/shard_map/collect/pallas_call | solution.py:212
  203.3 6.2 %all-to-all-done.3 = bf16[8,72,256]{2,1,0:T(8,128)(2,1)S(1)} async-done(((bf16[8,72,256]{2,1,0:T(8,128)(2,1)}), bf16[8,72,256]{2,1,0:T(8,128)(2,1)S(1)}, u32[]{:S(2)}, u32[]{:S(2)}) %all-to-all-start.3) | async-done | bytes 294944 | tf_op jit(solution)/shard_map/all_to_all | solution.py:23
  209.5 0.7 pad_maximum_fusion.1
  210.2 0.6 pad_maximum_fusion.3
  (80 shorter events, 2.8 us)
Async XLA Ops:
  33.7 9.3 %collective-permute-start.16 = (bf16[8,8,128]{2,1,0:T(8,128)(2,1)S(1)}, bf16[8,8,128]{2,1,0:T(8,128)(2,1)S(1)}, u32[]{:S(2)}, u32[]{:S(2)}) collective-permute-start(bf16[8,8,128]{2,1,0:T(8,128)(2,1)S(1)} %slice.75), channel_id=1, source_target_pairs={{0,8},{4,12},{8,0},{12,4},{1,9},{5,13},{9,1},{13,5},{2,10},{6,14},... | collective-permute-start | bytes 49160 | tf_op jit(solution)/shard_map/ppermute | solution.py:19
  36.7 8.2 %collective-permute-start.15 = (bf16[8,8,128]{2,1,0:T(8,128)(2,1)S(1)}, bf16[8,8,128]{2,1,0:T(8,128)(2,1)S(1)}, u32[]{:S(2)}, u32[]{:S(2)}) collective-permute-start(bf16[8,8,128]{2,1,0:T(8,128)(2,1)S(1)} %slice.75), channel_id=1, source_target_pairs={{0,4},{4,8},{8,12},{12,0},{1,5},{5,9},{9,13},{13,1},{2,6},{6,10},{... | collective-permute-start | bytes 49160 | tf_op jit(solution)/shard_map/ppermute | solution.py:19
  37.3 7.6 %collective-permute-start.17 = (bf16[8,8,128]{2,1,0:T(8,128)(2,1)S(1)}, bf16[8,8,128]{2,1,0:T(8,128)(2,1)S(1)}, u32[]{:S(2)}, u32[]{:S(2)}) collective-permute-start(bf16[8,8,128]{2,1,0:T(8,128)(2,1)S(1)} %slice.75), channel_id=1, source_target_pairs={{0,12},{4,0},{8,4},{12,8},{1,13},{5,1},{9,5},{13,9},{2,14},{6,2},{... | collective-permute-start | bytes 49160 | tf_op jit(solution)/shard_map/ppermute | solution.py:19
  40.0 47.9 %collective-permute-start.2 = (bf16[512,1024]{1,0:T(8,128)(2,1)}, bf16[512,1024]{1,0:T(8,128)(2,1)}, u32[]{:S(2)}, u32[]{:S(2)}) collective-permute-start(bf16[512,1024]{1,0:T(8,128)(2,1)} %refs_0_.3), channel_id=1, source_target_pairs={{0,3},{1,0},{2,1},{3,2},{4,7},{5,4},{6,5},{7,6},{8,11},{9,8},{10,9... | collective-permute-start | bytes 3145736 | tf_op jit(solution)/shard_map/ppermute | solution.py:19
  40.4 47.5 %collective-permute-start.1 = (bf16[512,1024]{1,0:T(8,128)(2,1)}, bf16[512,1024]{1,0:T(8,128)(2,1)}, u32[]{:S(2)}, u32[]{:S(2)}) collective-permute-start(bf16[512,1024]{1,0:T(8,128)(2,1)} %refs_0_.3), channel_id=1, source_target_pairs={{0,2},{1,3},{2,0},{3,1},{4,6},{5,7},{6,4},{7,5},{8,10},{9,11},{10,... | collective-permute-start | bytes 3145736 | tf_op jit(solution)/shard_map/ppermute | solution.py:19
  43.0 45.4 %collective-permute-start = (bf16[512,1024]{1,0:T(8,128)(2,1)}, bf16[512,1024]{1,0:T(8,128)(2,1)}, u32[]{:S(2)}, u32[]{:S(2)}) collective-permute-start(bf16[512,1024]{1,0:T(8,128)(2,1)} %refs_0_.3), channel_id=1, source_target_pairs={{0,1},{1,2},{2,3},{3,0},{4,5},{5,6},{6,7},{7,4},{8,9},{9,10},{10,1... | collective-permute-start | bytes 3145736 | tf_op jit(solution)/shard_map/ppermute | solution.py:19
  45.0 1.3 collective-permute-start.18
  55.0 61.7 %all-to-all-start.1 = ((bf16[64,48,128]{2,1,0:T(8,128)(2,1)}), bf16[64,48,128]{2,1,0:T(8,128)(2,1)}, u32[]{:S(2)}, u32[]{:S(2)}) async-start(bf16[64,48,128]{2,1,0:T(8,128)(2,1)} %pick.1), calls=%async_computation.1 | async-start | bytes 1572864 | tf_op jit(solution)/shard_map/all_to_all | solution.py:23
  60.5 23.3 %collective-permute-start.4 = (bf16[8,72,512]{2,1,0:T(8,128)(2,1)S(1)}, bf16[8,72,512]{2,1,0:T(8,128)(2,1)S(1)}, u32[]{:S(2)}, u32[]{:S(2)}) collective-permute-start(bf16[8,72,512]{2,1,0:T(8,128)(2,1)S(1)} %slice.72.refs_4_), channel_id=1, source_target_pairs={{0,12},{4,0},{8,4},{12,8},{1,13},{5,1},{9,5},{13,9},{2,14},{6,2},{... | collective-permute-start | bytes 1769480 | tf_op jit(solution)/shard_map/ppermute | solution.py:19
  63.2 23.9 %collective-permute-start.3 = (bf16[8,72,512]{2,1,0:T(8,128)(2,1)S(1)}, bf16[8,72,512]{2,1,0:T(8,128)(2,1)S(1)}, u32[]{:S(2)}, u32[]{:S(2)}) collective-permute-start(bf16[8,72,512]{2,1,0:T(8,128)(2,1)S(1)} %slice.72.refs_4_), channel_id=1, source_target_pairs={{0,4},{4,8},{8,12},{12,0},{1,5},{5,9},{9,13},{13,1},{2,6},{6,10},{... | collective-permute-start | bytes 1769480 | tf_op jit(solution)/shard_map/ppermute | solution.py:19
  83.8 9.4 %collective-permute-start.6 = (bf16[4,72,512]{2,1,0:T(8,128)(2,1)S(1)}, bf16[4,72,512]{2,1,0:T(8,128)(2,1)S(1)}, u32[]{:S(2)}, u32[]{:S(2)}) collective-permute-start(bf16[4,72,512]{2,1,0:T(8,128)(2,1)S(1)} %slice.74), channel_id=1, source_target_pairs={{0,12},{4,0},{8,4},{12,8},{1,13},{5,1},{9,5},{13,9},{2,14},{6,2},{... | collective-permute-start | bytes 884744 | tf_op jit(solution)/shard_map/ppermute | solution.py:19
  87.9 9.7 %collective-permute-start.5 = (bf16[4,72,512]{2,1,0:T(8,128)(2,1)}, bf16[4,72,512]{2,1,0:T(8,128)(2,1)S(1)}, u32[]{:S(2)}, u32[]{:S(2)}) collective-permute-start(bf16[4,72,512]{2,1,0:T(8,128)(2,1)} %slice.73), channel_id=1, source_target_pairs={{0,4},{4,8},{8,12},{12,0},{1,5},{5,9},{9,13},{13,1},{2,6},{6,10},{... | collective-permute-start | bytes 884744 | tf_op jit(solution)/shard_map/ppermute | solution.py:19
  87.9 17.0 %collective-permute-start.7 = (bf16[8,72,512]{2,1,0:T(8,128)(2,1)S(1)}, bf16[8,72,512]{2,1,0:T(8,128)(2,1)S(1)}, u32[]{:S(2)}, u32[]{:S(2)}) collective-permute-start(bf16[8,72,512]{2,1,0:T(8,128)(2,1)S(1)} %slice.72.refs_4_), channel_id=1, source_target_pairs={{0,128},{128,0},{1,129},{129,1},{2,130},{130,2},{3,131},{131,3},{4... | collective-permute-start | bytes 1769480 | tf_op jit(solution)/shard_map/ppermute | solution.py:19
  87.9 17.1 %collective-permute-start.9 = (bf16[8,72,512]{2,1,0:T(8,128)(2,1)S(1)}, bf16[8,72,512]{2,1,0:T(8,128)(2,1)}, u32[]{:S(2)}, u32[]{:S(2)}) collective-permute-start(bf16[8,72,512]{2,1,0:T(8,128)(2,1)S(1)} %collective-permute-done.4.refs_6_), channel_id=1, source_target_pairs={{0,128},{128,0},{1,129},{129,1},{2,130},{130,2},{3,131},{131,3},{4... | collective-permute-start | bytes 1769480 | tf_op jit(solution)/shard_map/ppermute | solution.py:19
  88.4 16.6 %collective-permute-start.8 = (bf16[8,72,512]{2,1,0:T(8,128)(2,1)S(1)}, bf16[8,72,512]{2,1,0:T(8,128)(2,1)}, u32[]{:S(2)}, u32[]{:S(2)}) collective-permute-start(bf16[8,72,512]{2,1,0:T(8,128)(2,1)S(1)} %collective-permute-done.3.refs_5_), channel_id=1, source_target_pairs={{0,128},{128,0},{1,129},{129,1},{2,130},{130,2},{3,131},{131,3},{4... | collective-permute-start | bytes 1769480 | tf_op jit(solution)/shard_map/ppermute | solution.py:19
  88.7 10.4 %copy-start.12 = (s32[4]{0:T(128)}, s32[4]{0:T(128)S(1)}, u32[]{:S(2)}) copy-start(s32[4]{0:T(128)S(1)} %get-tuple-element.67.place_ref) | copy-start | bytes 52
  93.2 11.7 %collective-permute-start.11 = (bf16[4,72,512]{2,1,0:T(8,128)(2,1)S(1)}, bf16[4,72,512]{2,1,0:T(8,128)(2,1)S(1)}, u32[]{:S(2)}, u32[]{:S(2)}) collective-permute-start(bf16[4,72,512]{2,1,0:T(8,128)(2,1)S(1)} %collective-permute-done.6.refs_8_), channel_id=1, source_target_pairs={{0,128},{128,0},{1,129},{129,1},{2,130},{130,2},{3,131},{131,3},{4... | collective-permute-start | bytes 884744 | tf_op jit(solution)/shard_map/ppermute | solution.py:19
  97.6 7.3 %collective-permute-start.10 = (bf16[4,72,512]{2,1,0:T(8,128)(2,1)S(1)}, bf16[4,72,512]{2,1,0:T(8,128)(2,1)}, u32[]{:S(2)}, u32[]{:S(2)}) collective-permute-start(bf16[4,72,512]{2,1,0:T(8,128)(2,1)S(1)} %collective-permute-done.5.refs_7_), channel_id=1, source_target_pairs={{0,128},{128,0},{1,129},{129,1},{2,130},{130,2},{3,131},{131,3},{4... | collective-permute-start | bytes 884744 | tf_op jit(solution)/shard_map/ppermute | solution.py:19
  111.7 0.8 copy-start.3
  112.5 0.8 copy-start.4
  113.3 9.4 %collective-permute-start.12 = (f32[512,128]{1,0:T(8,128)}, f32[512,128]{1,0:T(8,128)S(1)}, u32[]{:S(2)}, u32[]{:S(2)}) collective-permute-start(f32[512,128]{1,0:T(8,128)} %get-tuple-element.31), channel_id=1, source_target_pairs={{0,1},{1,2},{2,3},{3,0},{4,5},{5,6},{6,7},{7,4},{8,9},{9,10},{10,1... | collective-permute-start | bytes 786440 | tf_op jit(solution)/shard_map/ppermute | solution.py:19
  113.3 9.4 %collective-permute-start.13 = (f32[512,128]{1,0:T(8,128)}, f32[512,128]{1,0:T(8,128)S(1)}, u32[]{:S(2)}, u32[]{:S(2)}) collective-permute-start(f32[512,128]{1,0:T(8,128)} %get-tuple-element.32), channel_id=1, source_target_pairs={{0,3},{1,0},{2,1},{3,2},{4,7},{5,4},{6,5},{7,6},{8,11},{9,8},{10,9... | collective-permute-start | bytes 786440 | tf_op jit(solution)/shard_map/ppermute | solution.py:19
  115.3 13.6 %copy-start.8 = (bf16[512,128]{1,0:T(8,128)(2,1)S(1)}, bf16[512,128]{1,0:T(8,128)(2,1)}, u32[]{:S(2)}) copy-start(bf16[512,128]{1,0:T(8,128)(2,1)} %param.11) | copy-start | bytes 393220
  115.3 13.6 %collective-permute-start.14 = (f32[512,128]{1,0:T(8,128)}, f32[512,128]{1,0:T(8,128)S(1)}, u32[]{:S(2)}, u32[]{:S(2)}) collective-permute-start(f32[512,128]{1,0:T(8,128)} %get-tuple-element.33), channel_id=1, source_target_pairs={{0,2},{1,3},{2,0},{3,1},{4,6},{5,7},{6,4},{7,5},{8,10},{9,11},{10,... | collective-permute-start | bytes 786440 | tf_op jit(solution)/shard_map/ppermute | solution.py:19
  129.0 7.3 %copy-start.7 = (bf16[512,128]{1,0:T(8,128)(2,1)}, bf16[512,128]{1,0:T(8,128)(2,1)S(1)}, u32[]{:S(2)}) copy-start(bf16[512,128]{1,0:T(8,128)(2,1)S(1)} %get-tuple-element.56.refs_0_) | copy-start | bytes 393220
  130.5 13.4 %collective-permute-start.21 = (bf16[512,128]{1,0:T(8,128)(2,1)S(1)}, bf16[512,128]{1,0:T(8,128)(2,1)S(1)}, u32[]{:S(2)}, u32[]{:S(2)}) collective-permute-start(bf16[512,128]{1,0:T(8,128)(2,1)S(1)} %get-tuple-element.56.refs_0_), channel_id=1, source_target_pairs={{0,3},{1,0},{2,1},{3,2},{4,7},{5,4},{6,5},{7,6},{8,11},{9,8},{10,9... | collective-permute-start | bytes 393224 | tf_op jit(solution)/shard_map/ppermute | solution.py:19
  131.4 12.4 %collective-permute-start.20 = (bf16[512,128]{1,0:T(8,128)(2,1)S(1)}, bf16[512,128]{1,0:T(8,128)(2,1)S(1)}, u32[]{:S(2)}, u32[]{:S(2)}) collective-permute-start(bf16[512,128]{1,0:T(8,128)(2,1)S(1)} %get-tuple-element.56.refs_0_), channel_id=1, source_target_pairs={{0,2},{1,3},{2,0},{3,1},{4,6},{5,7},{6,4},{7,5},{8,10},{9,11},{10,... | collective-permute-start | bytes 393224 | tf_op jit(solution)/shard_map/ppermute | solution.py:19
  132.8 11.1 %collective-permute-start.19 = (bf16[512,128]{1,0:T(8,128)(2,1)S(1)}, bf16[512,128]{1,0:T(8,128)(2,1)S(1)}, u32[]{:S(2)}, u32[]{:S(2)}) collective-permute-start(bf16[512,128]{1,0:T(8,128)(2,1)S(1)} %get-tuple-element.56.refs_0_), channel_id=1, source_target_pairs={{0,1},{1,2},{2,3},{3,0},{4,5},{5,6},{6,7},{7,4},{8,9},{9,10},{10,1... | collective-permute-start | bytes 393224 | tf_op jit(solution)/shard_map/ppermute | solution.py:19
  136.3 41.4 %all-to-all-start.4 = ((bf16[64,48,128]{2,1,0:T(8,128)(2,1)}), bf16[64,48,128]{2,1,0:T(8,128)(2,1)S(1)}, u32[]{:S(2)}, u32[]{:S(2)}) async-start(bf16[64,48,128]{2,1,0:T(8,128)(2,1)} %pad_maximum_fusion), calls=%async_computation.4 | async-start | bytes 1572864 | tf_op jit(solution)/shard_map/all_to_all | solution.py:23
  143.9 0.7 copy-start.9
  143.9 0.7 copy-start.10
  143.9 0.8 copy-start.11
  144.7 6.6 %copy-start.6 = (bf16[2,1024,512]{2,1,0:T(8,128)(2,1)S(1)}, bf16[2,1024,512]{2,1,0:T(8,128)(2,1)}, u32[]{:S(2)}) copy-start(bf16[2,1024,512]{2,1,0:T(8,128)(2,1)} %get-tuple-element.41) | copy-start | bytes 6291460
  150.7 2.9 %collective-permute-start.22 = (bf16[2048,256]{1,0:T(8,128)(2,1)}, bf16[2048,256]{1,0:T(8,128)(2,1)S(1)}, u32[]{:S(2)}, u32[]{:S(2)}) collective-permute-start(bf16[2048,256]{1,0:T(8,128)(2,1)} %get-tuple-element.43), channel_id=1, source_target_pairs={{0,128},{128,0},{1,129},{129,1},{2,130},{130,2},{3,131},{131,3},{4... | collective-permute-start | bytes 3145736 | tf_op jit(solution)/shard_map/ppermute | solution.py:19
  150.7 4.4 %collective-permute-start.23 = (f32[4,128,512]{2,1,0:T(8,128)}, f32[4,128,512]{2,1,0:T(8,128)S(1)}, u32[]{:S(2)}, u32[]{:S(2)}) collective-permute-start(f32[4,128,512]{2,1,0:T(8,128)} %get-tuple-element.44), channel_id=1, source_target_pairs={{0,128},{128,0},{1,129},{129,1},{2,130},{130,2},{3,131},{131,3},{4... | collective-permute-start | bytes 3145736 | tf_op jit(solution)/shard_map/ppermute | solution.py:19
  151.2 3.9 %copy-start = (bf16[2,1024,512]{2,1,0:T(8,128)(2,1)S(1)}, bf16[2,1024,512]{2,1,0:T(8,128)(2,1)}, u32[]{:S(2)}) copy-start(bf16[2,1024,512]{2,1,0:T(8,128)(2,1)} %get-tuple-element.28) | copy-start | bytes 6291460
  151.2 3.9 %copy-start.1 = (f32[4,128,512]{2,1,0:T(8,128)S(1)}, f32[4,128,512]{2,1,0:T(8,128)}, u32[]{:S(2)}) copy-start(f32[4,128,512]{2,1,0:T(8,128)} %get-tuple-element.44) | copy-start | bytes 3145732
  151.2 3.9 %copy-start.2 = (bf16[512,512]{1,0:T(8,128)(2,1)S(1)}, bf16[512,512]{1,0:T(8,128)(2,1)}, u32[]{:S(2)}) copy-start(bf16[512,512]{1,0:T(8,128)(2,1)} %get-tuple-element.42.p_ref) | copy-start | bytes 1572868
  153.0 9.2 %collective-permute-start.27 = (bf16[2048,256]{1,0:T(8,128)(2,1)S(1)}, bf16[2048,256]{1,0:T(8,128)(2,1)S(1)}, u32[]{:S(2)}, u32[]{:S(2)}) collective-permute-start(bf16[2048,256]{1,0:T(8,128)(2,1)S(1)} %convolution_convert_fusion), channel_id=1, source_target_pairs={{0,128},{128,0},{1,129},{129,1},{2,130},{130,2},{3,131},{131,3},{4... | collective-permute-start | bytes 3145736 | tf_op jit(solution)/shard_map/ppermute | solution.py:19
  156.7 13.1 %collective-permute-start.24 = (bf16[8,72,256]{2,1,0:T(8,128)(2,1)S(1)}, bf16[8,72,256]{2,1,0:T(8,128)(2,1)S(1)}, u32[]{:S(2)}, u32[]{:S(2)}) collective-permute-start(bf16[8,72,256]{2,1,0:T(8,128)(2,1)S(1)} %get-tuple-element.46), channel_id=1, source_target_pairs={{0,4},{4,8},{8,12},{12,0},{1,5},{5,9},{9,13},{13,1},{2,6},{6,10},{... | collective-permute-start | bytes 884744 | tf_op jit(solution)/shard_map/ppermute | solution.py:19
  158.1 18.6 %collective-permute-start.25 = (bf16[8,72,256]{2,1,0:T(8,128)(2,1)S(1)}, bf16[8,72,256]{2,1,0:T(8,128)(2,1)S(1)}, u32[]{:S(2)}, u32[]{:S(2)}) collective-permute-start(bf16[8,72,256]{2,1,0:T(8,128)(2,1)S(1)} %get-tuple-element.47), channel_id=1, source_target_pairs={{0,8},{4,12},{8,0},{12,4},{1,9},{5,13},{9,1},{13,5},{2,10},{6,14},... | collective-permute-start | bytes 884744 | tf_op jit(solution)/shard_map/ppermute | solution.py:19
  160.8 16.0 %collective-permute-start.26 = (bf16[8,72,256]{2,1,0:T(8,128)(2,1)S(1)}, bf16[8,72,256]{2,1,0:T(8,128)(2,1)S(1)}, u32[]{:S(2)}, u32[]{:S(2)}) collective-permute-start(bf16[8,72,256]{2,1,0:T(8,128)(2,1)S(1)} %get-tuple-element.48), channel_id=1, source_target_pairs={{0,12},{4,0},{8,4},{12,8},{1,13},{5,1},{9,5},{13,9},{2,14},{6,2},{... | collective-permute-start | bytes 884744 | tf_op jit(solution)/shard_map/ppermute | solution.py:19
  163.8 19.5 %collective-permute-start.28 = (bf16[8,72,256]{2,1,0:T(8,128)(2,1)S(1)}, bf16[8,72,256]{2,1,0:T(8,128)(2,1)S(1)}, u32[]{:S(2)}, u32[]{:S(2)}) collective-permute-start(bf16[8,72,256]{2,1,0:T(8,128)(2,1)S(1)} %get-tuple-element.50), channel_id=1, source_target_pairs={{0,4},{4,8},{8,12},{12,0},{1,5},{5,9},{9,13},{13,1},{2,6},{6,10},{... | collective-permute-start | bytes 884744 | tf_op jit(solution)/shard_map/ppermute | solution.py:19
  164.5 24.6 %collective-permute-start.29 = (bf16[8,72,256]{2,1,0:T(8,128)(2,1)S(1)}, bf16[8,72,256]{2,1,0:T(8,128)(2,1)S(1)}, u32[]{:S(2)}, u32[]{:S(2)}) collective-permute-start(bf16[8,72,256]{2,1,0:T(8,128)(2,1)S(1)} %get-tuple-element.51), channel_id=1, source_target_pairs={{0,8},{4,12},{8,0},{12,4},{1,9},{5,13},{9,1},{13,5},{2,10},{6,14},... | collective-permute-start | bytes 884744 | tf_op jit(solution)/shard_map/ppermute | solution.py:19
  169.8 19.3 %collective-permute-start.30 = (bf16[8,72,256]{2,1,0:T(8,128)(2,1)S(1)}, bf16[8,72,256]{2,1,0:T(8,128)(2,1)S(1)}, u32[]{:S(2)}, u32[]{:S(2)}) collective-permute-start(bf16[8,72,256]{2,1,0:T(8,128)(2,1)S(1)} %get-tuple-element.52), channel_id=1, source_target_pairs={{0,12},{4,0},{8,4},{12,8},{1,13},{5,1},{9,5},{13,9},{2,14},{6,2},{... | collective-permute-start | bytes 884744 | tf_op jit(solution)/shard_map/ppermute | solution.py:19
  176.8 21.9 %copy-start.5 = (s32[1,3,8,128]{3,2,1,0:T(8,128)S(1)}, s32[1,3,8,128]{3,2,1,0:T(8,128)}, u32[]{:S(2)}) copy-start(s32[1,3,8,128]{3,2,1,0:T(8,128)} %copy.13) | copy-start | bytes 36868
  177.7 17.6 %all-to-all-start.2 = ((bf16[8,72,256]{2,1,0:T(8,128)(2,1)}), bf16[8,72,256]{2,1,0:T(8,128)(2,1)S(1)}, u32[]{:S(2)}, u32[]{:S(2)}) async-start(bf16[8,72,256]{2,1,0:T(8,128)(2,1)} %add_convert_fusion.1), calls=%async_computation.2 | async-start | bytes 589824 | tf_op jit(solution)/shard_map/all_to_all | solution.py:23
  195.3 14.2 %all-to-all-start.3 = ((bf16[8,72,256]{2,1,0:T(8,128)(2,1)}), bf16[8,72,256]{2,1,0:T(8,128)(2,1)S(1)}, u32[]{:S(2)}, u32[]{:S(2)}) async-start(bf16[8,72,256]{2,1,0:T(8,128)(2,1)} %add_convert_fusion), calls=%async_computation.3 | async-start | bytes 589824 | tf_op jit(solution)/shard_map/all_to_all | solution.py:23

commit v5 on v4

--- a/solution.py
+++ b/solution.py
@@ -12,6 +12,7 @@
 OWN = ("s", "z", "x")
 VMEM = pl.BlockSpec(memory_space=pltpu.VMEM)
 SMEM = pl.BlockSpec(memory_space=pltpu.SMEM)
+HBM = pl.BlockSpec(memory_space=pltpu.HBM)
 
 
 def shift(value, axis, by):
@@ -47,8 +48,16 @@
         f_refs, refs = refs[:ny], refs[ny:]
         n_refs, refs = refs[:many], refs[many:]
         o_refs, refs = refs[:many], refs[many:]
-        hid_ref, slope_ref, wo_ref = refs[:3]
-        lat_refs, (w_ref, wo32_ref) = refs[3:3 + ny], refs[3 + ny:]
+        hid_out, slope_ref, wo_out = refs[:3]
+        lat_refs, (w_ref, wo32_ref, wo_ref, hid_ref, wo_sem, hid_sem) = refs[3:3 + ny], refs[3 + ny:]
+        t = pl.program_id(0)
+
+        def send_wo():
+            return pltpu.make_async_copy(wo_ref, wo_out, wo_sem)
+
+        def send_hidden(i):
+            rows_to = hid_out.at[pl.ds(pl.multiple_of(i * tile, tile), tile)]
+            return pltpu.make_async_copy(hid_ref.at[i], rows_to, hid_sem.at[i])
 
         @pl.when(pl.program_id(0) == 0)
         def _():
@@ -62,6 +71,7 @@
                         wo32_ref[p, :, xk] = cut[:, in_rows:].astype(F32)
             for p in range(ny):
                 wo_ref[p] = wo32_ref[p].reshape(width, hid).astype(BF)
+            send_wo().start()
 
         acc = None
         for k in range(ny):
@@ -69,27 +79,38 @@
             acc = part if acc is None else acc + part
         logistic = jax.nn.sigmoid(acc)
         hidden = (acc * logistic).astype(BF)
-        hid_ref[...] = hidden
+        hid_ref[t] = hidden
+        send_hidden(t).start()
         slope_ref[...] = logistic * (1.0 + acc * (1.0 - logistic))
         for j in range(ny):
             lat_refs[j][...] = mm(hidden, wo_ref[place_ref[nx + ny + j]], ((1,), (1,)))
 
+        @pl.when(t == items // tile - 1)
+        def _():
+            send_wo().wait()
+            for i in range(items // tile):
+                send_hidden(i).wait()
+
     def rows(cols):
         return pl.BlockSpec((tile, cols), lambda t: (t, 0))
 
     return pl.pallas_call(
         kernel,
         out_shape=[
-            jax.ShapeDtypeStruct((items, hid), BF),
+            pltpu.HBM((items, hid), BF),
             jax.ShapeDtypeStruct((items, hid), F32),
-            jax.ShapeDtypeStruct((ny, width, hid), BF),
+            pltpu.HBM((ny, width, hid), BF),
         ] + [jax.ShapeDtypeStruct((items, width), F32)] * ny,
         grid=(items // tile,),
         in_specs=[SMEM] + [rows(depth)] * ny + [VMEM] * (2 * many),
-        out_specs=[rows(hid)] * 2 + [pl.BlockSpec((ny, width, hid), lambda t: (0, 0, 0))] + [rows(width)] * ny,
+        out_specs=[HBM, rows(hid), HBM] + [rows(width)] * ny,
         scratch_shapes=[
             pltpu.VMEM((ny, hz, nx, in_rows, hid), BF),
             pltpu.VMEM((ny, hz, nx, out_rows, hid), F32),
+            pltpu.VMEM((ny, width, hid), BF),
+            pltpu.VMEM((items // tile, tile, hid), BF),
+            pltpu.SemaphoreType.DMA,
+            pltpu.SemaphoreType.DMA((items // tile,)),
         ],
         cost_estimate=pl.CostEstimate(
             flops=2 * items * hid * ny * (depth + width), bytes_accessed=12 << 20, transcendentals=items * hid),

time: 213 us -> 213 us (level)
  transfers between devices with their start and end apart: 35 -> 35, of which waited for: 13 -> 13; matrix products, arithmetic and copies ran while one was open for 5% -> 6% of each run, Pallas kernels for 16% -> 16%
where the time goes in v5:
time: 213 us; the launch traced here: 211 us
  waiting for transfers between devices  69.7 us (33%)
  starting transfers between devices  57.3 us (27%)
  Pallas kernels  38.7 us (18%)
  blocking collectives  28.8 us (14%)
  local copies, waits for them, and re-layouts  6.05 us (3%)
  matrix products  4.97 us (2%)
  other arithmetic  4.35 us (2%)
    ppermute x31, waiting for transfers between devices, shift(): lax.ppermute(value, axis, [(i, (i + by) % size) for i in range(size)])  58.2 us
    ppermute x31, starting transfers between devices, shift(): lax.ppermute(value, axis, [(i, (i + by) % size) for i in range(size)])  35.1 us
    all_to_all x1, blocking collectives, exchange(): return lax.all_to_all(value, axis, split_axis=0, concat_axis=0, tiled=True)  28.8 us
    all_to_all x4, starting transfers between devices, exchange(): return lax.all_to_all(value, axis, split_axis=0, concat_axis=0, tiled=True)  22.1 us
    all_to_all x4, waiting for transfers between devices, exchange(): return lax.all_to_all(value, axis, split_axis=0, concat_axis=0, tiled=True)  11.5 us
    pallas_call x1, Pallas kernels, encode(): pl.pallas_call(kernel, out_shape=[pltpu.HBM((items, hid), BF), jax.ShapeD...  7.52 us
    pallas_call x1, Pallas kernels, pick(): pl.pallas_call(kernel, out_shape=jax.ShapeDtypeStruct((owners, levels * c...  7.35 us
    pallas_call x1, Pallas kernels, back(): pl.pallas_call(kernel, out_shape=[jax.ShapeDtypeStruct((items, hid), BF),...  6.03 us
  transfers between devices with their start and end apart: 35, of which 13 were waited for; matrix products, arithmetic and copies ran while one was open for 6% of the time, Pallas kernels for 16%

profile of v5, /device:TPU:8, one launch (start us, length us, event | category | flops | bytes accessed | tf_op | source)
XLA Modules:
  0.0 210.8 jit_solution(5512560833081342611)
XLA Ops:
  0.6 4.3 %ask.1 = (s32[3,512,1]{2,1,0:T(8,128)}, bf16[8,80,512]{2,1,0:T(8,128)(2,1)}) custom-call(s32[3,512]{1,0:T(4,128)} %codes_ref.1, bf16[64,512]{1,0:T(8,128)(2,1)} %wi_ref.1, bf16[8,512]{1,0:T(8,128)(2,1)} %wo_ref.1), custom_call_target="tpu_custom_call" | custom-call | tf_op jit(solution)/shard_map/ask/pallas_call | solution.py:166
  4.9 28.8 %all_to_all.25 = bf16[8,80,512]{2,1,0:T(8,128)(2,1)S(1)} all-to-all(bf16[8,80,512]{2,1,0:T(8,128)(2,1)} %get-tuple-element.29), channel_id=1, replica_groups=mesh['s'=2,'z'=8,'x'=4,'y'=4] {'z'}, dimensions={0} | all-to-all | bytes 1310720 | tf_op jit(solution)/shard_map/all_to_all | solution.py:24
  33.7 3.0 %collective-permute-start.16 = (bf16[8,8,128]{2,1,0:T(8,128)(2,1)S(1)}, bf16[8,8,128]{2,1,0:T(8,128)(2,1)S(1)}, u32[]{:S(2)}, u32[]{:S(2)}) collective-permute-start(bf16[8,8,128]{2,1,0:T(8,128)(2,1)S(1)} %slice.75), channel_id=1, source_target_pairs={{0,8},{4,12},{8,0},{12,4},{1,9},{5,13},{9,1},{13,5},{2,10},{6,14},... | collective-permute-start | bytes 49160 | tf_op jit(solution)/shard_map/ppermute | solution.py:20
  36.7 0.6 collective-permute-start.15
  37.3 2.6 %collective-permute-start.17 = (bf16[8,8,128]{2,1,0:T(8,128)(2,1)S(1)}, bf16[8,8,128]{2,1,0:T(8,128)(2,1)S(1)}, u32[]{:S(2)}, u32[]{:S(2)}) collective-permute-start(bf16[8,8,128]{2,1,0:T(8,128)(2,1)S(1)} %slice.75), channel_id=1, source_target_pairs={{0,12},{4,0},{8,4},{12,8},{1,13},{5,1},{9,5},{13,9},{2,14},{6,2},{... | collective-permute-start | bytes 49160 | tf_op jit(solution)/shard_map/ppermute | solution.py:20
  40.0 0.4 collective-permute-start.2
  40.4 2.6 %collective-permute-start.1 = (bf16[512,1024]{1,0:T(8,128)(2,1)}, bf16[512,1024]{1,0:T(8,128)(2,1)}, u32[]{:S(2)}, u32[]{:S(2)}) collective-permute-start(bf16[512,1024]{1,0:T(8,128)(2,1)} %refs_0_.3), channel_id=1, source_target_pairs={{0,2},{1,3},{2,0},{3,1},{4,6},{5,7},{6,4},{7,5},{8,10},{9,11},{10,... | collective-permute-start | bytes 3145736 | tf_op jit(solution)/shard_map/ppermute | solution.py:20
  43.0 1.9 collective-permute-start
  45.1 1.2 collective-permute-done.18
  47.1 0.6 copy.13
  47.7 7.3 %pick.1 = bf16[64,48,128]{2,1,0:T(8,128)(2,1)} custom-call(s32[3,8,128]{2,1,0:T(8,128)} %bitcast.44, bf16[3,1024,128]{2,1,0:T(8,128)(2,1)} %book_ref.1), custom_call_target="tpu_custom_call" | custom-call | tf_op jit(solution)/shard_map/pick/pallas_call | solution.py:200
  55.0 5.5 %all-to-all-start.1 = ((bf16[64,48,128]{2,1,0:T(8,128)(2,1)}), bf16[64,48,128]{2,1,0:T(8,128)(2,1)}, u32[]{:S(2)}, u32[]{:S(2)}) async-start(bf16[64,48,128]{2,1,0:T(8,128)(2,1)} %pick.1), calls=%async_computation.1 | async-start | bytes 1572864 | tf_op jit(solution)/shard_map/all_to_all | solution.py:24
  60.6 2.7 %collective-permute-start.4 = (bf16[8,72,512]{2,1,0:T(8,128)(2,1)S(1)}, bf16[8,72,512]{2,1,0:T(8,128)(2,1)S(1)}, u32[]{:S(2)}, u32[]{:S(2)}) collective-permute-start(bf16[8,72,512]{2,1,0:T(8,128)(2,1)S(1)} %slice.72.refs_4_), channel_id=1, source_target_pairs={{0,12},{4,0},{8,4},{12,8},{1,13},{5,1},{9,5},{13,9},{2,14},{6,2},{... | collective-permute-start | bytes 1769480 | tf_op jit(solution)/shard_map/ppermute | solution.py:20
  63.2 20.6 %collective-permute-done.4.refs_6_ = bf16[8,72,512]{2,1,0:T(8,128)(2,1)S(1)} collective-permute-done((bf16[8,72,512]{2,1,0:T(8,128)(2,1)S(1)}, bf16[8,72,512]{2,1,0:T(8,128)(2,1)S(1)}, u32[]{:S(2)}, u32[]{:S(2)}) %collective-permute-start.4) | collective-permute-done | bytes 589856 | tf_op jit(solution)/shard_map/ppermute | solution.py:20
  83.8 0.8 slice.74
  84.6 3.2 %collective-permute-start.6 = (bf16[4,72,512]{2,1,0:T(8,128)(2,1)}, bf16[4,72,512]{2,1,0:T(8,128)(2,1)S(1)}, u32[]{:S(2)}, u32[]{:S(2)}) collective-permute-start(bf16[4,72,512]{2,1,0:T(8,128)(2,1)} %slice.74), channel_id=1, source_target_pairs={{0,12},{4,0},{8,4},{12,8},{1,13},{5,1},{9,5},{13,9},{2,14},{6,2},{... | collective-permute-start | bytes 884744 | tf_op jit(solution)/shard_map/ppermute | solution.py:20
  87.8 0.7 slice.73
  88.6 0.5 collective-permute-start.9
  89.4 4.9 %collective-permute-done.6.refs_8_ = bf16[4,72,512]{2,1,0:T(8,128)(2,1)S(1)} collective-permute-done((bf16[4,72,512]{2,1,0:T(8,128)(2,1)}, bf16[4,72,512]{2,1,0:T(8,128)(2,1)S(1)}, u32[]{:S(2)}, u32[]{:S(2)}) %collective-permute-start.6) | collective-permute-done | bytes 294944 | tf_op jit(solution)/shard_map/ppermute | solution.py:20
  94.2 4.2 %collective-permute-done.5.refs_7_ = bf16[4,72,512]{2,1,0:T(8,128)(2,1)} collective-permute-done((bf16[4,72,512]{2,1,0:T(8,128)(2,1)}, bf16[4,72,512]{2,1,0:T(8,128)(2,1)}, u32[]{:S(2)}, u32[]{:S(2)}) %collective-permute-start.5) | collective-permute-done | bytes 294944 | tf_op jit(solution)/shard_map/ppermute | solution.py:20
  98.5 1.4 slice_reduce_fusion
  99.9 5.8 %turn.1 = (bf16[2,1024,512]{2,1,0:T(8,128)(2,1)}, bf16[2,1024,512]{2,1,0:T(8,128)(2,1)}) custom-call(s32[4]{0:T(128)} %copy-done.10, bf16[512,1024]{1,0:T(8,128)(2,1)} %refs_0_.3, bf16[512,1024]{1,0:T(8,128)(2,1)} %collective-permute-done.refs_1_, bf16[512,1024]{1,0:T(8,128)(2,1)} %collective-permute-done.1.refs_2_, ...), custom_call_target="tpu_custom_call" | custom-call | bytes 8388608 | tf_op jit(solution)/shard_map/turn/pallas_call | solution.py:268
  105.7 7.5 %encode.1 = (bf16[512,512]{1,0:T(8,128)(2,1)}, f32[512,512]{1,0:T(8,128)}, bf16[4,128,512]{2,1,0:T(8,128)(2,1)}, f32[512,128]{1,0:T(8,128)S(1)}, f32[512,128]{1,...) custom-call(s32[12]{0:T(128)S(1)} %pad_add_fusion.place_ref, bf16[512,1024]{1,0:T(8,128)(2,1)} %refs_0_.3, ...), custom_call_target="tpu_custom_call" | custom-call | flops 2415919104 | bytes 12582912 | tf_op jit(solution)/shard_map/encode/pallas_call | solution.py:97
  113.3 2.0 collective-permute-start.13
  115.4 1.3 collective-permute-start.14
  116.7 1.3 fusion.34
  117.9 0.5 fusion.2
  118.5 0.5 fusion.1
  119.0 0.5 fusion
  119.5 3.2 %collective-permute-done.12 = f32[512,128]{1,0:T(8,128)S(1)} collective-permute-done((f32[512,128]{1,0:T(8,128)}, f32[512,128]{1,0:T(8,128)S(1)}, u32[]{:S(2)}, u32[]{:S(2)}) %collective-permute-start.12) | collective-permute-done | bytes 262176 | tf_op jit(solution)/shard_map/ppermute | solution.py:20
  122.7 6.2 %collective-permute-done.14 = f32[512,128]{1,0:T(8,128)S(1)} collective-permute-done((f32[512,128]{1,0:T(8,128)}, f32[512,128]{1,0:T(8,128)S(1)}, u32[]{:S(2)}, u32[]{:S(2)}) %collective-permute-start.14) | collective-permute-done | bytes 262176 | tf_op jit(solution)/shard_map/ppermute | solution.py:20
  129.1 0.5 fusion.6
  129.6 0.5 fusion.7
  130.0 0.5 fusion.8
  130.5 1.0 collective-permute-start.21
  131.5 1.4 collective-permute-start.20
  132.9 2.5 %collective-permute-start.19 = (bf16[512,128]{1,0:T(8,128)(2,1)S(1)}, bf16[512,128]{1,0:T(8,128)(2,1)S(1)}, u32[]{:S(2)}, u32[]{:S(2)}) collective-permute-start(bf16[512,128]{1,0:T(8,128)(2,1)S(1)} %get-tuple-element.56.refs_0_), channel_id=1, source_target_pairs={{0,1},{1,2},{2,3},{3,0},{4,5},{5,6},{6,7},{7,4},{8,9},{9,10},{10,1... | collective-permute-start | bytes 393224 | tf_op jit(solution)/shard_map/ppermute | solution.py:20
  135.4 0.9 pad_maximum_fusion
  136.3 7.5 %all-to-all-start.4 = ((bf16[64,48,128]{2,1,0:T(8,128)(2,1)}), bf16[64,48,128]{2,1,0:T(8,128)(2,1)S(1)}, u32[]{:S(2)}, u32[]{:S(2)}) async-start(bf16[64,48,128]{2,1,0:T(8,128)(2,1)} %pad_maximum_fusion), calls=%async_computation.4 | async-start | bytes 1572864 | tf_op jit(solution)/shard_map/all_to_all | solution.py:24
  143.9 0.6 copy-done.7
  144.7 6.0 %back.1 = (bf16[512,512]{1,0:T(8,128)(2,1)}, f32[4,128,512]{2,1,0:T(8,128)}, bf16[2048,256]{1,0:T(8,128)(2,1)}) custom-call(s32[4]{0:T(128)} %copy-done.10, bf16[512,128]{1,0:T(8,128)(2,1)} %copy-done.5, bf16[512,128]{1,0:T(8,128)(2,1)} %copy-done.9, bf16[512,128]{1,0:T(8,128)(2,1)} %copy-done.8, bf16[512,128]{1,0:T(8,128)(2,1)} %copy-done.7, ...), custom_call_target="tpu_custom_call" | custom-call | flops 805306368 | bytes 6291456 | tf_op jit(solution)/shard_map/back/pallas_call | solution.py:300
  150.7 0.5 collective-permute-start.23
  151.2 1.8 convolution_convert_fusion
  153.6 1.5 collective-permute-done.23
  155.1 1.6 cut_by_x.2
  156.7 1.4 collective-permute-start.24
  158.1 2.7 %collective-permute-start.25 = (bf16[8,72,256]{2,1,0:T(8,128)(2,1)S(1)}, bf16[8,72,256]{2,1,0:T(8,128)(2,1)S(1)}, u32[]{:S(2)}, u32[]{:S(2)}) collective-permute-start(bf16[8,72,256]{2,1,0:T(8,128)(2,1)S(1)} %get-tuple-element.47), channel_id=1, source_target_pairs={{0,8},{4,12},{8,0},{12,4},{1,9},{5,13},{9,1},{13,5},{2,10},{6,14},... | collective-permute-start | bytes 884744 | tf_op jit(solution)/shard_map/ppermute | solution.py:20
  160.8 1.5 collective-permute-start.26
  162.3 1.6 cut_by_x.3
  163.9 0.6 collective-permute-start.28
  164.5 0.9 collective-permute-start.29
  165.4 4.5 %collective-permute-done.24 = bf16[8,72,256]{2,1,0:T(8,128)(2,1)S(1)} collective-permute-done((bf16[8,72,256]{2,1,0:T(8,128)(2,1)S(1)}, bf16[8,72,256]{2,1,0:T(8,128)(2,1)S(1)}, u32[]{:S(2)}, u32[]{:S(2)}) %collective-permute-start.24) | collective-permute-done | bytes 294944 | tf_op jit(solution)/shard_map/ppermute | solution.py:20
  169.9 1.1 collective-permute-start.30
  171.0 5.8 %collective-permute-done.25 = bf16[8,72,256]{2,1,0:T(8,128)(2,1)S(1)} collective-permute-done((bf16[8,72,256]{2,1,0:T(8,128)(2,1)S(1)}, bf16[8,72,256]{2,1,0:T(8,128)(2,1)S(1)}, u32[]{:S(2)}, u32[]{:S(2)}) %collective-permute-start.25) | collective-permute-done | bytes 294944 | tf_op jit(solution)/shard_map/ppermute | solution.py:20
  176.8 0.9 add_convert_fusion.1
  177.7 5.7 %all-to-all-start.2 = ((bf16[8,72,256]{2,1,0:T(8,128)(2,1)}), bf16[8,72,256]{2,1,0:T(8,128)(2,1)S(1)}, u32[]{:S(2)}, u32[]{:S(2)}) async-start(bf16[8,72,256]{2,1,0:T(8,128)(2,1)} %add_convert_fusion.1), calls=%async_computation.2 | async-start | bytes 589824 | tf_op jit(solution)/shard_map/all_to_all | solution.py:24
  183.4 5.8 %collective-permute-done.29 = bf16[8,72,256]{2,1,0:T(8,128)(2,1)S(1)} collective-permute-done((bf16[8,72,256]{2,1,0:T(8,128)(2,1)S(1)}, bf16[8,72,256]{2,1,0:T(8,128)(2,1)S(1)}, u32[]{:S(2)}, u32[]{:S(2)}) %collective-permute-start.29) | collective-permute-done | bytes 294944 | tf_op jit(solution)/shard_map/ppermute | solution.py:20
  189.1 0.9 add_convert_fusion
  190.0 5.3 %all-to-all-done.2 = bf16[8,72,256]{2,1,0:T(8,128)(2,1)S(1)} async-done(((bf16[8,72,256]{2,1,0:T(8,128)(2,1)}), bf16[8,72,256]{2,1,0:T(8,128)(2,1)S(1)}, u32[]{:S(2)}, u32[]{:S(2)}) %all-to-all-start.2) | async-done | bytes 294944 | tf_op jit(solution)/shard_map/all_to_all | solution.py:24
  195.3 3.4 %all-to-all-start.3 = ((bf16[8,72,256]{2,1,0:T(8,128)(2,1)}), bf16[8,72,256]{2,1,0:T(8,128)(2,1)S(1)}, u32[]{:S(2)}, u32[]{:S(2)}) async-start(bf16[8,72,256]{2,1,0:T(8,128)(2,1)} %add_convert_fusion), calls=%async_computation.3 | async-start | bytes 589824 | tf_op jit(solution)/shard_map/all_to_all | solution.py:24
  198.7 4.5 %collect.1 = f32[3,1024,128]{2,1,0:T(8,128)} custom-call(s32[3,8,128]{2,1,0:T(8,128)S(1)} %bitcast.45, bf16[64,48,128]{2,1,0:T(8,128)(2,1)S(1)} %all-to-all-done.4.in_ref), custom_call_target="tpu_custom_call" | custom-call | tf_op jit(solution)/shard_map/collect/pallas_call | solution.py:233
  203.3 6.2 %all-to-all-done.3 = bf16[8,72,256]{2,1,0:T(8,128)(2,1)S(1)} async-done(((bf16[8,72,256]{2,1,0:T(8,128)(2,1)}), bf16[8,72,256]{2,1,0:T(8,128)(2,1)S(1)}, u32[]{:S(2)}, u32[]{:S(2)}) %all-to-all-start.3) | async-done | bytes 294944 | tf_op jit(solution)/shard_map/all_to_all | solution.py:24
  209.5 0.7 pad_maximum_fusion.1
  210.2 0.6 pad_maximum_fusion.3
  (76 shorter events, 2.4 us)
Async XLA Ops:
  33.7 9.3 %collective-permute-start.16 = (bf16[8,8,128]{2,1,0:T(8,128)(2,1)S(1)}, bf16[8,8,128]{2,1,0:T(8,128)(2,1)S(1)}, u32[]{:S(2)}, u32[]{:S(2)}) collective-permute-start(bf16[8,8,128]{2,1,0:T(8,128)(2,1)S(1)} %slice.75), channel_id=1, source_target_pairs={{0,8},{4,12},{8,0},{12,4},{1,9},{5,13},{9,1},{13,5},{2,10},{6,14},... | collective-permute-start | bytes 49160 | tf_op jit(solution)/shard_map/ppermute | solution.py:20
  36.7 8.2 %collective-permute-start.15 = (bf16[8,8,128]{2,1,0:T(8,128)(2,1)S(1)}, bf16[8,8,128]{2,1,0:T(8,128)(2,1)S(1)}, u32[]{:S(2)}, u32[]{:S(2)}) collective-permute-start(bf16[8,8,128]{2,1,0:T(8,128)(2,1)S(1)} %slice.75), channel_id=1, source_target_pairs={{0,4},{4,8},{8,12},{12,0},{1,5},{5,9},{9,13},{13,1},{2,6},{6,10},{... | collective-permute-start | bytes 49160 | tf_op jit(solution)/shard_map/ppermute | solution.py:20
  37.3 7.6 %collective-permute-start.17 = (bf16[8,8,128]{2,1,0:T(8,128)(2,1)S(1)}, bf16[8,8,128]{2,1,0:T(8,128)(2,1)S(1)}, u32[]{:S(2)}, u32[]{:S(2)}) collective-permute-start(bf16[8,8,128]{2,1,0:T(8,128)(2,1)S(1)} %slice.75), channel_id=1, source_target_pairs={{0,12},{4,0},{8,4},{12,8},{1,13},{5,1},{9,5},{13,9},{2,14},{6,2},{... | collective-permute-start | bytes 49160 | tf_op jit(solution)/shard_map/ppermute | solution.py:20
  40.0 48.6 %collective-permute-start.2 = (bf16[512,1024]{1,0:T(8,128)(2,1)}, bf16[512,1024]{1,0:T(8,128)(2,1)}, u32[]{:S(2)}, u32[]{:S(2)}) collective-permute-start(bf16[512,1024]{1,0:T(8,128)(2,1)} %refs_0_.3), channel_id=1, source_target_pairs={{0,3},{1,0},{2,1},{3,2},{4,7},{5,4},{6,5},{7,6},{8,11},{9,8},{10,9... | collective-permute-start | bytes 3145736 | tf_op jit(solution)/shard_map/ppermute | solution.py:20
  40.4 48.1 %collective-permute-start.1 = (bf16[512,1024]{1,0:T(8,128)(2,1)}, bf16[512,1024]{1,0:T(8,128)(2,1)}, u32[]{:S(2)}, u32[]{:S(2)}) collective-permute-start(bf16[512,1024]{1,0:T(8,128)(2,1)} %refs_0_.3), channel_id=1, source_target_pairs={{0,2},{1,3},{2,0},{3,1},{4,6},{5,7},{6,4},{7,5},{8,10},{9,11},{10,... | collective-permute-start | bytes 3145736 | tf_op jit(solution)/shard_map/ppermute | solution.py:20
  43.0 46.0 %collective-permute-start = (bf16[512,1024]{1,0:T(8,128)(2,1)}, bf16[512,1024]{1,0:T(8,128)(2,1)}, u32[]{:S(2)}, u32[]{:S(2)}) collective-permute-start(bf16[512,1024]{1,0:T(8,128)(2,1)} %refs_0_.3), channel_id=1, source_target_pairs={{0,1},{1,2},{2,3},{3,0},{4,5},{5,6},{6,7},{7,4},{8,9},{9,10},{10,1... | collective-permute-start | bytes 3145736 | tf_op jit(solution)/shard_map/ppermute | solution.py:20
  45.0 1.3 collective-permute-start.18
  55.0 61.7 %all-to-all-start.1 = ((bf16[64,48,128]{2,1,0:T(8,128)(2,1)}), bf16[64,48,128]{2,1,0:T(8,128)(2,1)}, u32[]{:S(2)}, u32[]{:S(2)}) async-start(bf16[64,48,128]{2,1,0:T(8,128)(2,1)} %pick.1), calls=%async_computation.1 | async-start | bytes 1572864 | tf_op jit(solution)/shard_map/all_to_all | solution.py:24
  60.6 23.3 %collective-permute-start.4 = (bf16[8,72,512]{2,1,0:T(8,128)(2,1)S(1)}, bf16[8,72,512]{2,1,0:T(8,128)(2,1)S(1)}, u32[]{:S(2)}, u32[]{:S(2)}) collective-permute-start(bf16[8,72,512]{2,1,0:T(8,128)(2,1)S(1)} %slice.72.refs_4_), channel_id=1, source_target_pairs={{0,12},{4,0},{8,4},{12,8},{1,13},{5,1},{9,5},{13,9},{2,14},{6,2},{... | collective-permute-start | bytes 1769480 | tf_op jit(solution)/shard_map/ppermute | solution.py:20
  63.2 24.5 %collective-permute-start.3 = (bf16[8,72,512]{2,1,0:T(8,128)(2,1)S(1)}, bf16[8,72,512]{2,1,0:T(8,128)(2,1)S(1)}, u32[]{:S(2)}, u32[]{:S(2)}) collective-permute-start(bf16[8,72,512]{2,1,0:T(8,128)(2,1)S(1)} %slice.72.refs_4_), channel_id=1, source_target_pairs={{0,4},{4,8},{8,12},{12,0},{1,5},{5,9},{9,13},{13,1},{2,6},{6,10},{... | collective-permute-start | bytes 1769480 | tf_op jit(solution)/shard_map/ppermute | solution.py:20
  84.6 9.6 %collective-permute-start.6 = (bf16[4,72,512]{2,1,0:T(8,128)(2,1)}, bf16[4,72,512]{2,1,0:T(8,128)(2,1)S(1)}, u32[]{:S(2)}, u32[]{:S(2)}) collective-permute-start(bf16[4,72,512]{2,1,0:T(8,128)(2,1)} %slice.74), channel_id=1, source_target_pairs={{0,12},{4,0},{8,4},{12,8},{1,13},{5,1},{9,5},{13,9},{2,14},{6,2},{... | collective-permute-start | bytes 884744 | tf_op jit(solution)/shard_map/ppermute | solution.py:20
  88.5 9.9 %collective-permute-start.5 = (bf16[4,72,512]{2,1,0:T(8,128)(2,1)}, bf16[4,72,512]{2,1,0:T(8,128)(2,1)}, u32[]{:S(2)}, u32[]{:S(2)}) collective-permute-start(bf16[4,72,512]{2,1,0:T(8,128)(2,1)} %slice.73), channel_id=1, source_target_pairs={{0,4},{4,8},{8,12},{12,0},{1,5},{5,9},{9,13},{13,1},{2,6},{6,10},{... | collective-permute-start | bytes 884744 | tf_op jit(solution)/shard_map/ppermute | solution.py:20
  88.5 17.1 %collective-permute-start.7 = (bf16[8,72,512]{2,1,0:T(8,128)(2,1)S(1)}, bf16[8,72,512]{2,1,0:T(8,128)(2,1)S(1)}, u32[]{:S(2)}, u32[]{:S(2)}) collective-permute-start(bf16[8,72,512]{2,1,0:T(8,128)(2,1)S(1)} %slice.72.refs_4_), channel_id=1, source_target_pairs={{0,128},{128,0},{1,129},{129,1},{2,130},{130,2},{3,131},{131,3},{4... | collective-permute-start | bytes 1769480 | tf_op jit(solution)/shard_map/ppermute | solution.py:20
  88.6 17.1 %collective-permute-start.9 = (bf16[8,72,512]{2,1,0:T(8,128)(2,1)S(1)}, bf16[8,72,512]{2,1,0:T(8,128)(2,1)S(1)}, u32[]{:S(2)}, u32[]{:S(2)}) collective-permute-start(bf16[8,72,512]{2,1,0:T(8,128)(2,1)S(1)} %collective-permute-done.4.refs_6_), channel_id=1, source_target_pairs={{0,128},{128,0},{1,129},{129,1},{2,130},{130,2},{3,131},{131,3},{4... | collective-permute-start | bytes 1769480 | tf_op jit(solution)/shard_map/ppermute | solution.py:20
  89.1 16.7 %collective-permute-start.8 = (bf16[8,72,512]{2,1,0:T(8,128)(2,1)S(1)}, bf16[8,72,512]{2,1,0:T(8,128)(2,1)}, u32[]{:S(2)}, u32[]{:S(2)}) collective-permute-start(bf16[8,72,512]{2,1,0:T(8,128)(2,1)S(1)} %collective-permute-done.3.refs_5_), channel_id=1, source_target_pairs={{0,128},{128,0},{1,129},{129,1},{2,130},{130,2},{3,131},{131,3},{4... | collective-permute-start | bytes 1769480 | tf_op jit(solution)/shard_map/ppermute | solution.py:20
  89.4 10.5 %copy-start.10 = (s32[4]{0:T(128)}, s32[4]{0:T(128)S(1)}, u32[]{:S(2)}) copy-start(s32[4]{0:T(128)S(1)} %get-tuple-element.67.place_ref) | copy-start | bytes 52
  94.2 11.5 %collective-permute-start.11 = (bf16[4,72,512]{2,1,0:T(8,128)(2,1)S(1)}, bf16[4,72,512]{2,1,0:T(8,128)(2,1)}, u32[]{:S(2)}, u32[]{:S(2)}) collective-permute-start(bf16[4,72,512]{2,1,0:T(8,128)(2,1)S(1)} %collective-permute-done.6.refs_8_), channel_id=1, source_target_pairs={{0,128},{128,0},{1,129},{129,1},{2,130},{130,2},{3,131},{131,3},{4... | collective-permute-start | bytes 884744 | tf_op jit(solution)/shard_map/ppermute | solution.py:20
  98.4 7.3 %collective-permute-start.10 = (bf16[4,72,512]{2,1,0:T(8,128)(2,1)}, bf16[4,72,512]{2,1,0:T(8,128)(2,1)}, u32[]{:S(2)}, u32[]{:S(2)}) collective-permute-start(bf16[4,72,512]{2,1,0:T(8,128)(2,1)} %collective-permute-done.5.refs_7_), channel_id=1, source_target_pairs={{0,128},{128,0},{1,129},{129,1},{2,130},{130,2},{3,131},{131,3},{4... | collective-permute-start | bytes 884744 | tf_op jit(solution)/shard_map/ppermute | solution.py:20
  113.3 9.5 %collective-permute-start.12 = (f32[512,128]{1,0:T(8,128)}, f32[512,128]{1,0:T(8,128)S(1)}, u32[]{:S(2)}, u32[]{:S(2)}) collective-permute-start(f32[512,128]{1,0:T(8,128)} %get-tuple-element.31), channel_id=1, source_target_pairs={{0,1},{1,2},{2,3},{3,0},{4,5},{5,6},{6,7},{7,4},{8,9},{9,10},{10,1... | collective-permute-start | bytes 786440 | tf_op jit(solution)/shard_map/ppermute | solution.py:20
  113.3 9.4 %collective-permute-start.13 = (f32[512,128]{1,0:T(8,128)}, f32[512,128]{1,0:T(8,128)S(1)}, u32[]{:S(2)}, u32[]{:S(2)}) collective-permute-start(f32[512,128]{1,0:T(8,128)} %get-tuple-element.32), channel_id=1, source_target_pairs={{0,3},{1,0},{2,1},{3,2},{4,7},{5,4},{6,5},{7,6},{8,11},{9,8},{10,9... | collective-permute-start | bytes 786440 | tf_op jit(solution)/shard_map/ppermute | solution.py:20
  115.4 13.6 %copy-start.6 = (bf16[512,128]{1,0:T(8,128)(2,1)S(1)}, bf16[512,128]{1,0:T(8,128)(2,1)}, u32[]{:S(2)}) copy-start(bf16[512,128]{1,0:T(8,128)(2,1)} %param.11) | copy-start | bytes 393220
  115.4 13.6 %collective-permute-start.14 = (f32[512,128]{1,0:T(8,128)}, f32[512,128]{1,0:T(8,128)S(1)}, u32[]{:S(2)}, u32[]{:S(2)}) collective-permute-start(f32[512,128]{1,0:T(8,128)} %get-tuple-element.33), channel_id=1, source_target_pairs={{0,2},{1,3},{2,0},{3,1},{4,6},{5,7},{6,4},{7,5},{8,10},{9,11},{10,... | collective-permute-start | bytes 786440 | tf_op jit(solution)/shard_map/ppermute | solution.py:20
  129.1 7.3 %copy-start.5 = (bf16[512,128]{1,0:T(8,128)(2,1)}, bf16[512,128]{1,0:T(8,128)(2,1)S(1)}, u32[]{:S(2)}) copy-start(bf16[512,128]{1,0:T(8,128)(2,1)S(1)} %get-tuple-element.56.refs_0_) | copy-start | bytes 393220
  130.5 13.4 %collective-permute-start.21 = (bf16[512,128]{1,0:T(8,128)(2,1)S(1)}, bf16[512,128]{1,0:T(8,128)(2,1)S(1)}, u32[]{:S(2)}, u32[]{:S(2)}) collective-permute-start(bf16[512,128]{1,0:T(8,128)(2,1)S(1)} %get-tuple-element.56.refs_0_), channel_id=1, source_target_pairs={{0,3},{1,0},{2,1},{3,2},{4,7},{5,4},{6,5},{7,6},{8,11},{9,8},{10,9... | collective-permute-start | bytes 393224 | tf_op jit(solution)/shard_map/ppermute | solution.py:20
  131.5 12.4 %collective-permute-start.20 = (bf16[512,128]{1,0:T(8,128)(2,1)S(1)}, bf16[512,128]{1,0:T(8,128)(2,1)S(1)}, u32[]{:S(2)}, u32[]{:S(2)}) collective-permute-start(bf16[512,128]{1,0:T(8,128)(2,1)S(1)} %get-tuple-element.56.refs_0_), channel_id=1, source_target_pairs={{0,2},{1,3},{2,0},{3,1},{4,6},{5,7},{6,4},{7,5},{8,10},{9,11},{10,... | collective-permute-start | bytes 393224 | tf_op jit(solution)/shard_map/ppermute | solution.py:20
  132.9 11.1 %collective-permute-start.19 = (bf16[512,128]{1,0:T(8,128)(2,1)S(1)}, bf16[512,128]{1,0:T(8,128)(2,1)S(1)}, u32[]{:S(2)}, u32[]{:S(2)}) collective-permute-start(bf16[512,128]{1,0:T(8,128)(2,1)S(1)} %get-tuple-element.56.refs_0_), channel_id=1, source_target_pairs={{0,1},{1,2},{2,3},{3,0},{4,5},{5,6},{6,7},{7,4},{8,9},{9,10},{10,1... | collective-permute-start | bytes 393224 | tf_op jit(solution)/shard_map/ppermute | solution.py:20
  136.3 41.3 %all-to-all-start.4 = ((bf16[64,48,128]{2,1,0:T(8,128)(2,1)}), bf16[64,48,128]{2,1,0:T(8,128)(2,1)S(1)}, u32[]{:S(2)}, u32[]{:S(2)}) async-start(bf16[64,48,128]{2,1,0:T(8,128)(2,1)} %pad_maximum_fusion), calls=%async_computation.4 | async-start | bytes 1572864 | tf_op jit(solution)/shard_map/all_to_all | solution.py:24
  143.9 0.7 copy-start.7
  143.9 0.7 copy-start.8
  143.9 0.8 copy-start.9
  144.7 6.5 %copy-start.4 = (bf16[2,1024,512]{2,1,0:T(8,128)(2,1)S(1)}, bf16[2,1024,512]{2,1,0:T(8,128)(2,1)}, u32[]{:S(2)}) copy-start(bf16[2,1024,512]{2,1,0:T(8,128)(2,1)} %get-tuple-element.41) | copy-start | bytes 6291460
  150.7 2.9 %collective-permute-start.22 = (bf16[2048,256]{1,0:T(8,128)(2,1)}, bf16[2048,256]{1,0:T(8,128)(2,1)S(1)}, u32[]{:S(2)}, u32[]{:S(2)}) collective-permute-start(bf16[2048,256]{1,0:T(8,128)(2,1)} %get-tuple-element.43), channel_id=1, source_target_pairs={{0,128},{128,0},{1,129},{129,1},{2,130},{130,2},{3,131},{131,3},{4... | collective-permute-start | bytes 3145736 | tf_op jit(solution)/shard_map/ppermute | solution.py:20
  150.7 4.4 %collective-permute-start.23 = (f32[4,128,512]{2,1,0:T(8,128)}, f32[4,128,512]{2,1,0:T(8,128)S(1)}, u32[]{:S(2)}, u32[]{:S(2)}) collective-permute-start(f32[4,128,512]{2,1,0:T(8,128)} %get-tuple-element.44), channel_id=1, source_target_pairs={{0,128},{128,0},{1,129},{129,1},{2,130},{130,2},{3,131},{131,3},{4... | collective-permute-start | bytes 3145736 | tf_op jit(solution)/shard_map/ppermute | solution.py:20
  151.2 3.9 %copy-start = (bf16[2,1024,512]{2,1,0:T(8,128)(2,1)S(1)}, bf16[2,1024,512]{2,1,0:T(8,128)(2,1)}, u32[]{:S(2)}) copy-start(bf16[2,1024,512]{2,1,0:T(8,128)(2,1)} %get-tuple-element.28) | copy-start | bytes 6291460
  151.2 3.9 %copy-start.1 = (f32[4,128,512]{2,1,0:T(8,128)S(1)}, f32[4,128,512]{2,1,0:T(8,128)}, u32[]{:S(2)}) copy-start(f32[4,128,512]{2,1,0:T(8,128)} %get-tuple-element.44) | copy-start | bytes 3145732
  151.2 3.9 %copy-start.2 = (bf16[512,512]{1,0:T(8,128)(2,1)S(1)}, bf16[512,512]{1,0:T(8,128)(2,1)}, u32[]{:S(2)}) copy-start(bf16[512,512]{1,0:T(8,128)(2,1)} %get-tuple-element.42.p_ref) | copy-start | bytes 1572868
  153.1 9.2 %collective-permute-start.27 = (bf16[2048,256]{1,0:T(8,128)(2,1)S(1)}, bf16[2048,256]{1,0:T(8,128)(2,1)S(1)}, u32[]{:S(2)}, u32[]{:S(2)}) collective-permute-start(bf16[2048,256]{1,0:T(8,128)(2,1)S(1)} %convolution_convert_fusion), channel_id=1, source_target_pairs={{0,128},{128,0},{1,129},{129,1},{2,130},{130,2},{3,131},{131,3},{4... | collective-permute-start | bytes 3145736 | tf_op jit(solution)/shard_map/ppermute | solution.py:20
  156.7 13.1 %collective-permute-start.24 = (bf16[8,72,256]{2,1,0:T(8,128)(2,1)S(1)}, bf16[8,72,256]{2,1,0:T(8,128)(2,1)S(1)}, u32[]{:S(2)}, u32[]{:S(2)}) collective-permute-start(bf16[8,72,256]{2,1,0:T(8,128)(2,1)S(1)} %get-tuple-element.46), channel_id=1, source_target_pairs={{0,4},{4,8},{8,12},{12,0},{1,5},{5,9},{9,13},{13,1},{2,6},{6,10},{... | collective-permute-start | bytes 884744 | tf_op jit(solution)/shard_map/ppermute | solution.py:20
  158.1 18.6 %collective-permute-start.25 = (bf16[8,72,256]{2,1,0:T(8,128)(2,1)S(1)}, bf16[8,72,256]{2,1,0:T(8,128)(2,1)S(1)}, u32[]{:S(2)}, u32[]{:S(2)}) collective-permute-start(bf16[8,72,256]{2,1,0:T(8,128)(2,1)S(1)} %get-tuple-element.47), channel_id=1, source_target_pairs={{0,8},{4,12},{8,0},{12,4},{1,9},{5,13},{9,1},{13,5},{2,10},{6,14},... | collective-permute-start | bytes 884744 | tf_op jit(solution)/shard_map/ppermute | solution.py:20
  160.8 16.0 %collective-permute-start.26 = (bf16[8,72,256]{2,1,0:T(8,128)(2,1)S(1)}, bf16[8,72,256]{2,1,0:T(8,128)(2,1)S(1)}, u32[]{:S(2)}, u32[]{:S(2)}) collective-permute-start(bf16[8,72,256]{2,1,0:T(8,128)(2,1)S(1)} %get-tuple-element.48), channel_id=1, source_target_pairs={{0,12},{4,0},{8,4},{12,8},{1,13},{5,1},{9,5},{13,9},{2,14},{6,2},{... | collective-permute-start | bytes 884744 | tf_op jit(solution)/shard_map/ppermute | solution.py:20
  163.9 19.5 %collective-permute-start.28 = (bf16[8,72,256]{2,1,0:T(8,128)(2,1)S(1)}, bf16[8,72,256]{2,1,0:T(8,128)(2,1)S(1)}, u32[]{:S(2)}, u32[]{:S(2)}) collective-permute-start(bf16[8,72,256]{2,1,0:T(8,128)(2,1)S(1)} %get-tuple-element.50), channel_id=1, source_target_pairs={{0,4},{4,8},{8,12},{12,0},{1,5},{5,9},{9,13},{13,1},{2,6},{6,10},{... | collective-permute-start | bytes 884744 | tf_op jit(solution)/shard_map/ppermute | solution.py:20
  164.5 24.6 %collective-permute-start.29 = (bf16[8,72,256]{2,1,0:T(8,128)(2,1)S(1)}, bf16[8,72,256]{2,1,0:T(8,128)(2,1)S(1)}, u32[]{:S(2)}, u32[]{:S(2)}) collective-permute-start(bf16[8,72,256]{2,1,0:T(8,128)(2,1)S(1)} %get-tuple-element.51), channel_id=1, source_target_pairs={{0,8},{4,12},{8,0},{12,4},{1,9},{5,13},{9,1},{13,5},{2,10},{6,14},... | collective-permute-start | bytes 884744 | tf_op jit(solution)/shard_map/ppermute | solution.py:20
  169.9 19.3 %collective-permute-start.30 = (bf16[8,72,256]{2,1,0:T(8,128)(2,1)S(1)}, bf16[8,72,256]{2,1,0:T(8,128)(2,1)S(1)}, u32[]{:S(2)}, u32[]{:S(2)}) collective-permute-start(bf16[8,72,256]{2,1,0:T(8,128)(2,1)S(1)} %get-tuple-element.52), channel_id=1, source_target_pairs={{0,12},{4,0},{8,4},{12,8},{1,13},{5,1},{9,5},{13,9},{2,14},{6,2},{... | collective-permute-start | bytes 884744 | tf_op jit(solution)/shard_map/ppermute | solution.py:20
  176.8 21.9 %copy-start.3 = (s32[1,3,8,128]{3,2,1,0:T(8,128)S(1)}, s32[1,3,8,128]{3,2,1,0:T(8,128)}, u32[]{:S(2)}) copy-start(s32[1,3,8,128]{3,2,1,0:T(8,128)} %copy.13) | copy-start | bytes 36868
  177.7 17.6 %all-to-all-start.2 = ((bf16[8,72,256]{2,1,0:T(8,128)(2,1)}), bf16[8,72,256]{2,1,0:T(8,128)(2,1)S(1)}, u32[]{:S(2)}, u32[]{:S(2)}) async-start(bf16[8,72,256]{2,1,0:T(8,128)(2,1)} %add_convert_fusion.1), calls=%async_computation.2 | async-start | bytes 589824 | tf_op jit(solution)/shard_map/all_to_all | solution.py:24
  195.3 14.2 %all-to-all-start.3 = ((bf16[8,72,256]{2,1,0:T(8,128)(2,1)}), bf16[8,72,256]{2,1,0:T(8,128)(2,1)S(1)}, u32[]{:S(2)}, u32[]{:S(2)}) async-start(bf16[8,72,256]{2,1,0:T(8,128)(2,1)} %add_convert_fusion), calls=%async_computation.3 | async-start | bytes 589824 | tf_op jit(solution)/shard_map/all_to_all | solution.py:24

commit v6 on v5

--- a/solution.py
+++ b/solution.py
@@ -279,33 +279,51 @@
 def back(grads, hidden, slope, w_out, feats_there, place, step):
     items, hid = hidden.shape
     ny, width = w_out.shape[:2]
+    hy = ny // 2
     rows = feats_there.shape[0]
+    tile = rows // 4
 
     def kernel(place_ref, *refs):
-        g_refs, (hid_ref, slope_ref, wo_ref, f_ref, pre_ref, out_ref, there_ref) = refs[:ny], refs[ny:]
-        grads_all = jnp.concatenate([g_refs[k][...] for k in range(ny)], axis=1)
-        w_all = jnp.concatenate([wo_ref[place_ref[k]] for k in range(ny)], axis=0)
-        pre_ref[...] = (mm(grads_all, w_all) * slope_ref[...]).astype(BF)
-
-        def product(t, carry):
-            cut = pl.ds(pl.multiple_of(t * 512, 512), 512)
-            there_ref[cut, :] = mm(f_ref[cut, :], pre_ref[:, :step]).astype(BF)
-            return carry
-
-        lax.fori_loop(0, rows // 512, product, 0)
-        outs = mm(grads_all, hid_ref[...], ((0,), (0,)))
-        for k in range(ny):
-            out_ref[place_ref[k]] = outs[k * width:(k + 1) * width]
+        g_refs, refs = refs[:ny], refs[ny:]
+        hid_ref, slope_ref, wo_ref, f_ref, pre_ref, here_ref, away_ref, there_ref = refs
+
+        @pl.when(pl.program_id(0) == 0)
+        def _():
+            grads_all = jnp.concatenate([g_refs[k][...] for k in range(ny)], axis=1)
+            w_all = jnp.concatenate([wo_ref[place_ref[k]] for k in range(ny)], axis=0)
+            pre_ref[...] = (mm(grads_all, w_all) * slope_ref[...]).astype(BF)
+            outs = mm(grads_all, hid_ref[...], ((0,), (0,)))
+            for k in range(ny):
+                spot = place_ref[k]
+                block = outs[k * width:(k + 1) * width]
+
+                @pl.when(spot < hy)
+                def _():
+                    here_ref[spot] = block
+
+                @pl.when(spot >= hy)
+                def _():
+                    away_ref[spot - hy] = block.astype(BF)
+
+        there_ref[...] = mm(f_ref[...], pre_ref[:, :step]).astype(BF)
+
+    def whole(*shape):
+        return pl.BlockSpec(shape, lambda t: (0,) * len(shape))
 
     return pl.pallas_call(
         kernel,
         out_shape=[
             jax.ShapeDtypeStruct((items, hid), BF),
-            jax.ShapeDtypeStruct((ny, width, hid), F32),
+            jax.ShapeDtypeStruct((hy, width, hid), F32),
+            pltpu.HBM((hy, width, hid), BF),
             jax.ShapeDtypeStruct((rows, step), BF),
         ],
-        in_specs=[SMEM] + [VMEM] * (ny + 4),
-        out_specs=[VMEM] * 3,
+        grid=(rows // tile,),
+        in_specs=[SMEM] + [VMEM] * (ny + 3) + [pl.BlockSpec((tile, items), lambda t: (t, 0))],
+        out_specs=[
+            whole(items, hid), whole(hy, width, hid), whole(hy, width, hid),
+            pl.BlockSpec((tile, step), lambda t: (t, 0)),
+        ],
         cost_estimate=pl.CostEstimate(flops=6 * items * hid * ny * width, bytes_accessed=6 << 20, transcendentals=0),
         name="back",
     )(place, *grads, hidden, slope, w_out, feats_there)
@@ -316,20 +334,19 @@
     hid = came.shape[1]
     in_rows = came.shape[0] // (nz * nx)
     hy = feats_t.shape[0]
-    ny, width = out_mine.shape[:2]
+    width = out_mine.shape[1]
     out_rows = hy * width // (nz * nx)
     both = in_rows + out_rows
     feats_t = feats_t.reshape(-1, items)
-    out_mine = out_mine.reshape(ny * width, -1)
-    out_came = out_came.reshape(ny * width, -1)
+    out_mine = out_mine.reshape(hy * width, -1)
+    out_came = out_came.reshape(hy * width, -1)
     group = 4
     many, few = group * nx * in_rows, group * nx * out_rows
-    ahead = hy * width // few
 
     def kernel(order_ref, f_ref, p_ref, came_ref, om_ref, oc_ref, own_ref, *rest):
         sends, part = rest[:-1], rest[-1]
         total = (mm(f_ref[...], p_ref[...]) + came_ref[...].astype(F32)).reshape(group, nx, in_rows, hid)
-        outs = (om_ref[...] + oc_ref[...]).reshape(group, nx, out_rows, hid)
+        outs = (om_ref[...] + oc_ref[...].astype(F32)).reshape(group, nx, out_rows, hid)
         for g in range(group):
             part[:, :in_rows] = total[g]
             part[:, in_rows:] = outs[g]
@@ -349,7 +366,7 @@
             pl.BlockSpec((items, hid), lambda t: (0, c)),
             pl.BlockSpec((many, hid), lambda t: (t, 0)),
             pl.BlockSpec((few, hid), lambda t: (t, c)),
-            pl.BlockSpec((few, hid), lambda t: (ahead + t, c)),
+            pl.BlockSpec((few, hid), lambda t: (t, c)),
         ],
         out_specs=[block] * nx,
         scratch_shapes=[pltpu.VMEM((nx, both, hid), F32)],
@@ -439,13 +456,13 @@
     pieces = 2
     step = hid // pieces
     there_rows = feats_there.reshape(hy * depth, items)
-    pre_grad, out_part, there_first = back(grads, hidden, slope, w_out_all, there_rows, y_place, step)
-    out_came = shift(out_part, "s", 1)
+    pre_grad, out_here, out_away, there_first = back(grads, hidden, slope, w_out_all, there_rows, y_place, step)
+    out_came = shift(out_away, "s", 1)
     in_list, out_list = [], []
     for c in range(pieces):
         there = there_first if c == 0 else mm(there_rows, pre_grad[:, c * step:(c + 1) * step]).astype(BF)
         came = shift(there, "s", 1)
-        own, to_1, to_2, to_3 = cut_by_x(feats_here, pre_grad, came, out_part, out_came, x_send, nz, nx, c)
+        own, to_1, to_2, to_3 = cut_by_x(feats_here, pre_grad, came, out_here, out_came, x_send, nz, nx, c)
         sum_x = (
             own
             + shift(to_1, "x", 1).astype(F32)

time: 213 us -> 214 us (level)
  transfers between devices with their start and end apart: 35 -> 35, of which waited for: 13 -> 12; matrix products, arithmetic and copies ran while one was open for 6% -> 6% of each run, Pallas kernels for 16% -> 16%
where the time goes in v6:
time: 214 us; the launch traced here: 211 us
  waiting for transfers between devices  69.7 us (33%)
  starting transfers between devices  57.7 us (27%)
  Pallas kernels  38.7 us (18%)
  blocking collectives  28.8 us (13%)
  local copies, waits for them, and re-layouts  6.02 us (3%)
  matrix products  4.97 us (2%)
  other arithmetic  4.38 us (2%)
    ppermute x31, waiting for transfers between devices, shift(): lax.ppermute(value, axis, [(i, (i + by) % size) for i in range(size)])  58.2 us
    ppermute x31, starting transfers between devices, shift(): lax.ppermute(value, axis, [(i, (i + by) % size) for i in range(size)])  35.2 us
    all_to_all x1, blocking collectives, exchange(): return lax.all_to_all(value, axis, split_axis=0, concat_axis=0, tiled=True)  28.8 us
    all_to_all x4, starting transfers between devices, exchange(): return lax.all_to_all(value, axis, split_axis=0, concat_axis=0, tiled=True)  22.5 us
    all_to_all x4, waiting for transfers between devices, exchange(): return lax.all_to_all(value, axis, split_axis=0, concat_axis=0, tiled=True)  11.5 us
    pallas_call x1, Pallas kernels, encode(): pl.pallas_call(kernel, out_shape=[pltpu.HBM((items, hid), BF), jax.ShapeD...  7.52 us
    pallas_call x1, Pallas kernels, pick(): pl.pallas_call(kernel, out_shape=jax.ShapeDtypeStruct((owners, levels * c...  7.39 us
    pallas_call x1, Pallas kernels, back(): pl.pallas_call(kernel, out_shape=[jax.ShapeDtypeStruct((items, hid), BF),...  6.05 us
  transfers between devices with their start and end apart: 35, of which 12 were waited for; matrix products, arithmetic and copies ran while one was open for 6% of the time, Pallas kernels for 16%

profile of v6, /device:TPU:8, one launch (start us, length us, event | category | flops | bytes accessed | tf_op | source)
XLA Modules:
  0.0 211.3 jit_solution(881650925765100088)
XLA Ops:
  0.6 4.3 %ask.1 = (s32[3,512,1]{2,1,0:T(8,128)}, bf16[8,80,512]{2,1,0:T(8,128)(2,1)}) custom-call(s32[3,512]{1,0:T(4,128)} %codes_ref.1, bf16[64,512]{1,0:T(8,128)(2,1)} %wi_ref.1, bf16[8,512]{1,0:T(8,128)(2,1)} %wo_ref.1), custom_call_target="tpu_custom_call" | custom-call | tf_op jit(solution)/shard_map/ask/pallas_call | solution.py:166
  4.9 28.8 %all_to_all.25 = bf16[8,80,512]{2,1,0:T(8,128)(2,1)S(1)} all-to-all(bf16[8,80,512]{2,1,0:T(8,128)(2,1)} %get-tuple-element.30), channel_id=1, replica_groups=mesh['s'=2,'z'=8,'x'=4,'y'=4] {'z'}, dimensions={0} | all-to-all | bytes 1310720 | tf_op jit(solution)/shard_map/all_to_all | solution.py:24
  33.7 3.0 %collective-permute-start.16 = (bf16[8,8,128]{2,1,0:T(8,128)(2,1)S(1)}, bf16[8,8,128]{2,1,0:T(8,128)(2,1)S(1)}, u32[]{:S(2)}, u32[]{:S(2)}) collective-permute-start(bf16[8,8,128]{2,1,0:T(8,128)(2,1)S(1)} %slice.75), channel_id=1, source_target_pairs={{0,8},{4,12},{8,0},{12,4},{1,9},{5,13},{9,1},{13,5},{2,10},{6,14},... | collective-permute-start | bytes 49160 | tf_op jit(solution)/shard_map/ppermute | solution.py:20
  36.7 0.6 collective-permute-start.15
  37.3 2.6 %collective-permute-start.17 = (bf16[8,8,128]{2,1,0:T(8,128)(2,1)S(1)}, bf16[8,8,128]{2,1,0:T(8,128)(2,1)S(1)}, u32[]{:S(2)}, u32[]{:S(2)}) collective-permute-start(bf16[8,8,128]{2,1,0:T(8,128)(2,1)S(1)} %slice.75), channel_id=1, source_target_pairs={{0,12},{4,0},{8,4},{12,8},{1,13},{5,1},{9,5},{13,9},{2,14},{6,2},{... | collective-permute-start | bytes 49160 | tf_op jit(solution)/shard_map/ppermute | solution.py:20
  40.0 0.4 collective-permute-start.2
  40.4 2.6 %collective-permute-start.1 = (bf16[512,1024]{1,0:T(8,128)(2,1)}, bf16[512,1024]{1,0:T(8,128)(2,1)}, u32[]{:S(2)}, u32[]{:S(2)}) collective-permute-start(bf16[512,1024]{1,0:T(8,128)(2,1)} %refs_0_.3), channel_id=1, source_target_pairs={{0,2},{1,3},{2,0},{3,1},{4,6},{5,7},{6,4},{7,5},{8,10},{9,11},{10,... | collective-permute-start | bytes 3145736 | tf_op jit(solution)/shard_map/ppermute | solution.py:20
  43.0 1.9 collective-permute-start
  45.1 1.2 collective-permute-done.18
  47.1 0.6 copy.13
  47.7 7.4 %pick.1 = bf16[64,48,128]{2,1,0:T(8,128)(2,1)} custom-call(s32[3,8,128]{2,1,0:T(8,128)} %bitcast.44, bf16[3,1024,128]{2,1,0:T(8,128)(2,1)} %book_ref.1), custom_call_target="tpu_custom_call" | custom-call | tf_op jit(solution)/shard_map/pick/pallas_call | solution.py:200
  55.1 5.5 %all-to-all-start.1 = ((bf16[64,48,128]{2,1,0:T(8,128)(2,1)}), bf16[64,48,128]{2,1,0:T(8,128)(2,1)}, u32[]{:S(2)}, u32[]{:S(2)}) async-start(bf16[64,48,128]{2,1,0:T(8,128)(2,1)} %pick.1), calls=%async_computation.1 | async-start | bytes 1572864 | tf_op jit(solution)/shard_map/all_to_all | solution.py:24
  60.6 2.7 %collective-permute-start.4 = (bf16[8,72,512]{2,1,0:T(8,128)(2,1)S(1)}, bf16[8,72,512]{2,1,0:T(8,128)(2,1)S(1)}, u32[]{:S(2)}, u32[]{:S(2)}) collective-permute-start(bf16[8,72,512]{2,1,0:T(8,128)(2,1)S(1)} %slice.72.refs_4_), channel_id=1, source_target_pairs={{0,12},{4,0},{8,4},{12,8},{1,13},{5,1},{9,5},{13,9},{2,14},{6,2},{... | collective-permute-start | bytes 1769480 | tf_op jit(solution)/shard_map/ppermute | solution.py:20
  63.3 20.6 %collective-permute-done.4.refs_6_ = bf16[8,72,512]{2,1,0:T(8,128)(2,1)S(1)} collective-permute-done((bf16[8,72,512]{2,1,0:T(8,128)(2,1)S(1)}, bf16[8,72,512]{2,1,0:T(8,128)(2,1)S(1)}, u32[]{:S(2)}, u32[]{:S(2)}) %collective-permute-start.4) | collective-permute-done | bytes 589856 | tf_op jit(solution)/shard_map/ppermute | solution.py:20
  83.9 0.8 slice.74
  84.6 3.2 %collective-permute-start.6 = (bf16[4,72,512]{2,1,0:T(8,128)(2,1)}, bf16[4,72,512]{2,1,0:T(8,128)(2,1)S(1)}, u32[]{:S(2)}, u32[]{:S(2)}) collective-permute-start(bf16[4,72,512]{2,1,0:T(8,128)(2,1)} %slice.74), channel_id=1, source_target_pairs={{0,12},{4,0},{8,4},{12,8},{1,13},{5,1},{9,5},{13,9},{2,14},{6,2},{... | collective-permute-start | bytes 884744 | tf_op jit(solution)/shard_map/ppermute | solution.py:20
  87.8 0.7 slice.73
  88.6 0.5 collective-permute-start.9
  89.4 4.9 %collective-permute-done.6.refs_8_ = bf16[4,72,512]{2,1,0:T(8,128)(2,1)S(1)} collective-permute-done((bf16[4,72,512]{2,1,0:T(8,128)(2,1)}, bf16[4,72,512]{2,1,0:T(8,128)(2,1)S(1)}, u32[]{:S(2)}, u32[]{:S(2)}) %collective-permute-start.6) | collective-permute-done | bytes 294944 | tf_op jit(solution)/shard_map/ppermute | solution.py:20
  94.3 4.1 %collective-permute-done.5.refs_7_ = bf16[4,72,512]{2,1,0:T(8,128)(2,1)} collective-permute-done((bf16[4,72,512]{2,1,0:T(8,128)(2,1)}, bf16[4,72,512]{2,1,0:T(8,128)(2,1)}, u32[]{:S(2)}, u32[]{:S(2)}) %collective-permute-start.5) | collective-permute-done | bytes 294944 | tf_op jit(solution)/shard_map/ppermute | solution.py:20
  98.5 1.4 slice_reduce_fusion
  99.9 5.8 %turn.1 = (bf16[2,1024,512]{2,1,0:T(8,128)(2,1)}, bf16[2,1024,512]{2,1,0:T(8,128)(2,1)}) custom-call(s32[4]{0:T(128)} %copy-done.10, bf16[512,1024]{1,0:T(8,128)(2,1)} %refs_0_.3, bf16[512,1024]{1,0:T(8,128)(2,1)} %collective-permute-done.refs_1_, bf16[512,1024]{1,0:T(8,128)(2,1)} %collective-permute-done.1.refs_2_, ...), custom_call_target="tpu_custom_call" | custom-call | bytes 8388608 | tf_op jit(solution)/shard_map/turn/pallas_call | solution.py:268
  105.8 7.5 %encode.1 = (bf16[512,512]{1,0:T(8,128)(2,1)}, f32[512,512]{1,0:T(8,128)}, bf16[4,128,512]{2,1,0:T(8,128)(2,1)}, f32[512,128]{1,0:T(8,128)S(1)}, f32[512,128]{1,...) custom-call(s32[12]{0:T(128)S(1)} %pad_add_fusion.place_ref, bf16[512,1024]{1,0:T(8,128)(2,1)} %refs_0_.3, ...), custom_call_target="tpu_custom_call" | custom-call | flops 2415919104 | bytes 12582912 | tf_op jit(solution)/shard_map/encode/pallas_call | solution.py:97
  113.4 2.0 collective-permute-start.13
  115.4 1.3 collective-permute-start.14
  116.7 1.3 fusion.34
  118.0 0.5 fusion.2
  118.5 0.5 fusion.1
  119.0 0.5 fusion
  119.5 3.2 %collective-permute-done.12 = f32[512,128]{1,0:T(8,128)S(1)} collective-permute-done((f32[512,128]{1,0:T(8,128)}, f32[512,128]{1,0:T(8,128)S(1)}, u32[]{:S(2)}, u32[]{:S(2)}) %collective-permute-start.12) | collective-permute-done | bytes 262176 | tf_op jit(solution)/shard_map/ppermute | solution.py:20
  122.8 6.2 %collective-permute-done.14 = f32[512,128]{1,0:T(8,128)S(1)} collective-permute-done((f32[512,128]{1,0:T(8,128)}, f32[512,128]{1,0:T(8,128)S(1)}, u32[]{:S(2)}, u32[]{:S(2)}) %collective-permute-start.14) | collective-permute-done | bytes 262176 | tf_op jit(solution)/shard_map/ppermute | solution.py:20
  129.1 0.5 fusion.6
  129.6 0.5 fusion.7
  130.1 0.5 fusion.8
  130.5 1.0 collective-permute-start.21
  131.5 1.4 collective-permute-start.20
  132.9 2.5 %collective-permute-start.19 = (bf16[512,128]{1,0:T(8,128)(2,1)S(1)}, bf16[512,128]{1,0:T(8,128)(2,1)S(1)}, u32[]{:S(2)}, u32[]{:S(2)}) collective-permute-start(bf16[512,128]{1,0:T(8,128)(2,1)S(1)} %get-tuple-element.58.refs_0_), channel_id=1, source_target_pairs={{0,1},{1,2},{2,3},{3,0},{4,5},{5,6},{6,7},{7,4},{8,9},{9,10},{10,1... | collective-permute-start | bytes 393224 | tf_op jit(solution)/shard_map/ppermute | solution.py:20
  135.4 1.0 pad_maximum_fusion
  136.4 7.5 %all-to-all-start.4 = ((bf16[64,48,128]{2,1,0:T(8,128)(2,1)}), bf16[64,48,128]{2,1,0:T(8,128)(2,1)S(1)}, u32[]{:S(2)}, u32[]{:S(2)}) async-start(bf16[64,48,128]{2,1,0:T(8,128)(2,1)} %pad_maximum_fusion), calls=%async_computation.4 | async-start | bytes 1572864 | tf_op jit(solution)/shard_map/all_to_all | solution.py:24
  144.0 0.6 copy-done.7
  144.7 6.0 %back.1 = (bf16[512,512]{1,0:T(8,128)(2,1)}, f32[2,128,512]{2,1,0:T(8,128)}, bf16[2,128,512]{2,1,0:T(8,128)(2,1)}, bf16[2048,256]{1,0:T(8,128)(2,1)}) custom-call(s32[4]{0:T(128)} %copy-done.10, bf16[512,128]{1,0:T(8,128)(2,1)} %copy-done.5, bf16[512,128]{1,0:T(8,128)(2,1)} %copy-done.9, bf16[512,128]{1,0:T(8,128)(2,1)} %copy-done.8, ...), custom_call_target="tpu_custom_call" | custom-call | flops 805306368 | bytes 6291456 | tf_op jit(solution)/shard_map/back/pallas_call | solution.py:313
  150.8 1.8 convolution_convert_fusion
  152.7 0.6 collective-permute-start.27
  153.3 2.5 %collective-permute-done.23 = bf16[2,128,512]{2,1,0:T(8,128)(2,1)S(1)} collective-permute-done((bf16[2,128,512]{2,1,0:T(8,128)(2,1)S(1)}, bf16[2,128,512]{2,1,0:T(8,128)(2,1)S(1)}, u32[]{:S(2)}, u32[]{:S(2)}) %collective-permute-start.23) | collective-permute-done | bytes 262176 | tf_op jit(solution)/shard_map/ppermute | solution.py:20
  155.9 1.6 cut_by_x.2
  157.5 1.6 collective-permute-start.24
  159.0 2.7 %collective-permute-start.25 = (bf16[8,72,256]{2,1,0:T(8,128)(2,1)S(1)}, bf16[8,72,256]{2,1,0:T(8,128)(2,1)S(1)}, u32[]{:S(2)}, u32[]{:S(2)}) collective-permute-start(bf16[8,72,256]{2,1,0:T(8,128)(2,1)S(1)} %get-tuple-element.49), channel_id=1, source_target_pairs={{0,8},{4,12},{8,0},{12,4},{1,9},{5,13},{9,1},{13,5},{2,10},{6,14},... | collective-permute-start | bytes 884744 | tf_op jit(solution)/shard_map/ppermute | solution.py:20
  161.7 1.4 collective-permute-start.26
  163.2 1.5 cut_by_x.3
  164.7 0.7 collective-permute-start.28
  165.4 0.9 collective-permute-start.29
  166.3 4.2 %collective-permute-done.24 = bf16[8,72,256]{2,1,0:T(8,128)(2,1)S(1)} collective-permute-done((bf16[8,72,256]{2,1,0:T(8,128)(2,1)S(1)}, bf16[8,72,256]{2,1,0:T(8,128)(2,1)S(1)}, u32[]{:S(2)}, u32[]{:S(2)}) %collective-permute-start.24) | collective-permute-done | bytes 294944 | tf_op jit(solution)/shard_map/ppermute | solution.py:20
  170.4 1.0 collective-permute-start.30
  171.4 5.8 %collective-permute-done.25 = bf16[8,72,256]{2,1,0:T(8,128)(2,1)S(1)} collective-permute-done((bf16[8,72,256]{2,1,0:T(8,128)(2,1)S(1)}, bf16[8,72,256]{2,1,0:T(8,128)(2,1)S(1)}, u32[]{:S(2)}, u32[]{:S(2)}) %collective-permute-start.25) | collective-permute-done | bytes 294944 | tf_op jit(solution)/shard_map/ppermute | solution.py:20
  177.2 0.9 add_convert_fusion.1
  178.1 6.1 %all-to-all-start.2 = ((bf16[8,72,256]{2,1,0:T(8,128)(2,1)}), bf16[8,72,256]{2,1,0:T(8,128)(2,1)S(1)}, u32[]{:S(2)}, u32[]{:S(2)}) async-start(bf16[8,72,256]{2,1,0:T(8,128)(2,1)} %add_convert_fusion.1), calls=%async_computation.2 | async-start | bytes 589824 | tf_op jit(solution)/shard_map/all_to_all | solution.py:24
  184.2 5.3 %collective-permute-done.29 = bf16[8,72,256]{2,1,0:T(8,128)(2,1)S(1)} collective-permute-done((bf16[8,72,256]{2,1,0:T(8,128)(2,1)S(1)}, bf16[8,72,256]{2,1,0:T(8,128)(2,1)S(1)}, u32[]{:S(2)}, u32[]{:S(2)}) %collective-permute-start.29) | collective-permute-done | bytes 294944 | tf_op jit(solution)/shard_map/ppermute | solution.py:20
  189.5 0.9 add_convert_fusion
  190.4 5.3 %all-to-all-done.2 = bf16[8,72,256]{2,1,0:T(8,128)(2,1)S(1)} async-done(((bf16[8,72,256]{2,1,0:T(8,128)(2,1)}), bf16[8,72,256]{2,1,0:T(8,128)(2,1)S(1)}, u32[]{:S(2)}, u32[]{:S(2)}) %all-to-all-start.2) | async-done | bytes 294944 | tf_op jit(solution)/shard_map/all_to_all | solution.py:24
  195.7 3.4 %all-to-all-start.3 = ((bf16[8,72,256]{2,1,0:T(8,128)(2,1)}), bf16[8,72,256]{2,1,0:T(8,128)(2,1)S(1)}, u32[]{:S(2)}, u32[]{:S(2)}) async-start(bf16[8,72,256]{2,1,0:T(8,128)(2,1)} %add_convert_fusion), calls=%async_computation.3 | async-start | bytes 589824 | tf_op jit(solution)/shard_map/all_to_all | solution.py:24
  199.2 4.5 %collect.1 = f32[3,1024,128]{2,1,0:T(8,128)} custom-call(s32[3,8,128]{2,1,0:T(8,128)S(1)} %bitcast.45, bf16[64,48,128]{2,1,0:T(8,128)(2,1)S(1)} %all-to-all-done.4.in_ref), custom_call_target="tpu_custom_call" | custom-call | tf_op jit(solution)/shard_map/collect/pallas_call | solution.py:233
  203.7 6.2 %all-to-all-done.3 = bf16[8,72,256]{2,1,0:T(8,128)(2,1)S(1)} async-done(((bf16[8,72,256]{2,1,0:T(8,128)(2,1)}), bf16[8,72,256]{2,1,0:T(8,128)(2,1)S(1)}, u32[]{:S(2)}, u32[]{:S(2)}) %all-to-all-start.3) | async-done | bytes 294944 | tf_op jit(solution)/shard_map/all_to_all | solution.py:24
  210.0 0.7 pad_maximum_fusion.1
  210.7 0.6 pad_maximum_fusion.3
  (78 shorter events, 2.0 us)
Async XLA Ops:
  33.7 9.3 %collective-permute-start.16 = (bf16[8,8,128]{2,1,0:T(8,128)(2,1)S(1)}, bf16[8,8,128]{2,1,0:T(8,128)(2,1)S(1)}, u32[]{:S(2)}, u32[]{:S(2)}) collective-permute-start(bf16[8,8,128]{2,1,0:T(8,128)(2,1)S(1)} %slice.75), channel_id=1, source_target_pairs={{0,8},{4,12},{8,0},{12,4},{1,9},{5,13},{9,1},{13,5},{2,10},{6,14},... | collective-permute-start | bytes 49160 | tf_op jit(solution)/shard_map/ppermute | solution.py:20
  36.7 8.2 %collective-permute-start.15 = (bf16[8,8,128]{2,1,0:T(8,128)(2,1)S(1)}, bf16[8,8,128]{2,1,0:T(8,128)(2,1)S(1)}, u32[]{:S(2)}, u32[]{:S(2)}) collective-permute-start(bf16[8,8,128]{2,1,0:T(8,128)(2,1)S(1)} %slice.75), channel_id=1, source_target_pairs={{0,4},{4,8},{8,12},{12,0},{1,5},{5,9},{9,13},{13,1},{2,6},{6,10},{... | collective-permute-start | bytes 49160 | tf_op jit(solution)/shard_map/ppermute | solution.py:20
  37.3 7.6 %collective-permute-start.17 = (bf16[8,8,128]{2,1,0:T(8,128)(2,1)S(1)}, bf16[8,8,128]{2,1,0:T(8,128)(2,1)S(1)}, u32[]{:S(2)}, u32[]{:S(2)}) collective-permute-start(bf16[8,8,128]{2,1,0:T(8,128)(2,1)S(1)} %slice.75), channel_id=1, source_target_pairs={{0,12},{4,0},{8,4},{12,8},{1,13},{5,1},{9,5},{13,9},{2,14},{6,2},{... | collective-permute-start | bytes 49160 | tf_op jit(solution)/shard_map/ppermute | solution.py:20
  40.0 48.6 %collective-permute-start.2 = (bf16[512,1024]{1,0:T(8,128)(2,1)}, bf16[512,1024]{1,0:T(8,128)(2,1)}, u32[]{:S(2)}, u32[]{:S(2)}) collective-permute-start(bf16[512,1024]{1,0:T(8,128)(2,1)} %refs_0_.3), channel_id=1, source_target_pairs={{0,3},{1,0},{2,1},{3,2},{4,7},{5,4},{6,5},{7,6},{8,11},{9,8},{10,9... | collective-permute-start | bytes 3145736 | tf_op jit(solution)/shard_map/ppermute | solution.py:20
  40.4 48.2 %collective-permute-start.1 = (bf16[512,1024]{1,0:T(8,128)(2,1)}, bf16[512,1024]{1,0:T(8,128)(2,1)}, u32[]{:S(2)}, u32[]{:S(2)}) collective-permute-start(bf16[512,1024]{1,0:T(8,128)(2,1)} %refs_0_.3), channel_id=1, source_target_pairs={{0,2},{1,3},{2,0},{3,1},{4,6},{5,7},{6,4},{7,5},{8,10},{9,11},{10,... | collective-permute-start | bytes 3145736 | tf_op jit(solution)/shard_map/ppermute | solution.py:20
  43.0 46.1 %collective-permute-start = (bf16[512,1024]{1,0:T(8,128)(2,1)}, bf16[512,1024]{1,0:T(8,128)(2,1)}, u32[]{:S(2)}, u32[]{:S(2)}) collective-permute-start(bf16[512,1024]{1,0:T(8,128)(2,1)} %refs_0_.3), channel_id=1, source_target_pairs={{0,1},{1,2},{2,3},{3,0},{4,5},{5,6},{6,7},{7,4},{8,9},{9,10},{10,1... | collective-permute-start | bytes 3145736 | tf_op jit(solution)/shard_map/ppermute | solution.py:20
  45.0 1.3 collective-permute-start.18
  55.1 61.7 %all-to-all-start.1 = ((bf16[64,48,128]{2,1,0:T(8,128)(2,1)}), bf16[64,48,128]{2,1,0:T(8,128)(2,1)}, u32[]{:S(2)}, u32[]{:S(2)}) async-start(bf16[64,48,128]{2,1,0:T(8,128)(2,1)} %pick.1), calls=%async_computation.1 | async-start | bytes 1572864 | tf_op jit(solution)/shard_map/all_to_all | solution.py:24
  60.6 23.3 %collective-permute-start.4 = (bf16[8,72,512]{2,1,0:T(8,128)(2,1)S(1)}, bf16[8,72,512]{2,1,0:T(8,128)(2,1)S(1)}, u32[]{:S(2)}, u32[]{:S(2)}) collective-permute-start(bf16[8,72,512]{2,1,0:T(8,128)(2,1)S(1)} %slice.72.refs_4_), channel_id=1, source_target_pairs={{0,12},{4,0},{8,4},{12,8},{1,13},{5,1},{9,5},{13,9},{2,14},{6,2},{... | collective-permute-start | bytes 1769480 | tf_op jit(solution)/shard_map/ppermute | solution.py:20
  63.3 24.5 %collective-permute-start.3 = (bf16[8,72,512]{2,1,0:T(8,128)(2,1)S(1)}, bf16[8,72,512]{2,1,0:T(8,128)(2,1)S(1)}, u32[]{:S(2)}, u32[]{:S(2)}) collective-permute-start(bf16[8,72,512]{2,1,0:T(8,128)(2,1)S(1)} %slice.72.refs_4_), channel_id=1, source_target_pairs={{0,4},{4,8},{8,12},{12,0},{1,5},{5,9},{9,13},{13,1},{2,6},{6,10},{... | collective-permute-start | bytes 1769480 | tf_op jit(solution)/shard_map/ppermute | solution.py:20
  84.6 9.6 %collective-permute-start.6 = (bf16[4,72,512]{2,1,0:T(8,128)(2,1)}, bf16[4,72,512]{2,1,0:T(8,128)(2,1)S(1)}, u32[]{:S(2)}, u32[]{:S(2)}) collective-permute-start(bf16[4,72,512]{2,1,0:T(8,128)(2,1)} %slice.74), channel_id=1, source_target_pairs={{0,12},{4,0},{8,4},{12,8},{1,13},{5,1},{9,5},{13,9},{2,14},{6,2},{... | collective-permute-start | bytes 884744 | tf_op jit(solution)/shard_map/ppermute | solution.py:20
  88.6 9.9 %collective-permute-start.5 = (bf16[4,72,512]{2,1,0:T(8,128)(2,1)}, bf16[4,72,512]{2,1,0:T(8,128)(2,1)}, u32[]{:S(2)}, u32[]{:S(2)}) collective-permute-start(bf16[4,72,512]{2,1,0:T(8,128)(2,1)} %slice.73), channel_id=1, source_target_pairs={{0,4},{4,8},{8,12},{12,0},{1,5},{5,9},{9,13},{13,1},{2,6},{6,10},{... | collective-permute-start | bytes 884744 | tf_op jit(solution)/shard_map/ppermute | solution.py:20
  88.6 17.2 %collective-permute-start.7 = (bf16[8,72,512]{2,1,0:T(8,128)(2,1)S(1)}, bf16[8,72,512]{2,1,0:T(8,128)(2,1)S(1)}, u32[]{:S(2)}, u32[]{:S(2)}) collective-permute-start(bf16[8,72,512]{2,1,0:T(8,128)(2,1)S(1)} %slice.72.refs_4_), channel_id=1, source_target_pairs={{0,128},{128,0},{1,129},{129,1},{2,130},{130,2},{3,131},{131,3},{4... | collective-permute-start | bytes 1769480 | tf_op jit(solution)/shard_map/ppermute | solution.py:20
  88.6 17.2 %collective-permute-start.9 = (bf16[8,72,512]{2,1,0:T(8,128)(2,1)S(1)}, bf16[8,72,512]{2,1,0:T(8,128)(2,1)S(1)}, u32[]{:S(2)}, u32[]{:S(2)}) collective-permute-start(bf16[8,72,512]{2,1,0:T(8,128)(2,1)S(1)} %collective-permute-done.4.refs_6_), channel_id=1, source_target_pairs={{0,128},{128,0},{1,129},{129,1},{2,130},{130,2},{3,131},{131,3},{4... | collective-permute-start | bytes 1769480 | tf_op jit(solution)/shard_map/ppermute | solution.py:20
  89.1 16.7 %collective-permute-start.8 = (bf16[8,72,512]{2,1,0:T(8,128)(2,1)S(1)}, bf16[8,72,512]{2,1,0:T(8,128)(2,1)}, u32[]{:S(2)}, u32[]{:S(2)}) collective-permute-start(bf16[8,72,512]{2,1,0:T(8,128)(2,1)S(1)} %collective-permute-done.3.refs_5_), channel_id=1, source_target_pairs={{0,128},{128,0},{1,129},{129,1},{2,130},{130,2},{3,131},{131,3},{4... | collective-permute-start | bytes 1769480 | tf_op jit(solution)/shard_map/ppermute | solution.py:20
  89.4 10.5 %copy-start.10 = (s32[4]{0:T(128)}, s32[4]{0:T(128)S(1)}, u32[]{:S(2)}) copy-start(s32[4]{0:T(128)S(1)} %get-tuple-element.69.place_ref) | copy-start | bytes 52
  94.3 11.5 %collective-permute-start.11 = (bf16[4,72,512]{2,1,0:T(8,128)(2,1)S(1)}, bf16[4,72,512]{2,1,0:T(8,128)(2,1)}, u32[]{:S(2)}, u32[]{:S(2)}) collective-permute-start(bf16[4,72,512]{2,1,0:T(8,128)(2,1)S(1)} %collective-permute-done.6.refs_8_), channel_id=1, source_target_pairs={{0,128},{128,0},{1,129},{129,1},{2,130},{130,2},{3,131},{131,3},{4... | collective-permute-start | bytes 884744 | tf_op jit(solution)/shard_map/ppermute | solution.py:20
  98.4 7.3 %collective-permute-start.10 = (bf16[4,72,512]{2,1,0:T(8,128)(2,1)}, bf16[4,72,512]{2,1,0:T(8,128)(2,1)}, u32[]{:S(2)}, u32[]{:S(2)}) collective-permute-start(bf16[4,72,512]{2,1,0:T(8,128)(2,1)} %collective-permute-done.5.refs_7_), channel_id=1, source_target_pairs={{0,128},{128,0},{1,129},{129,1},{2,130},{130,2},{3,131},{131,3},{4... | collective-permute-start | bytes 884744 | tf_op jit(solution)/shard_map/ppermute | solution.py:20
  113.3 9.5 %collective-permute-start.12 = (f32[512,128]{1,0:T(8,128)}, f32[512,128]{1,0:T(8,128)S(1)}, u32[]{:S(2)}, u32[]{:S(2)}) collective-permute-start(f32[512,128]{1,0:T(8,128)} %get-tuple-element.32), channel_id=1, source_target_pairs={{0,1},{1,2},{2,3},{3,0},{4,5},{5,6},{6,7},{7,4},{8,9},{9,10},{10,1... | collective-permute-start | bytes 786440 | tf_op jit(solution)/shard_map/ppermute | solution.py:20
  113.4 9.4 %collective-permute-start.13 = (f32[512,128]{1,0:T(8,128)}, f32[512,128]{1,0:T(8,128)S(1)}, u32[]{:S(2)}, u32[]{:S(2)}) collective-permute-start(f32[512,128]{1,0:T(8,128)} %get-tuple-element.33), channel_id=1, source_target_pairs={{0,3},{1,0},{2,1},{3,2},{4,7},{5,4},{6,5},{7,6},{8,11},{9,8},{10,9... | collective-permute-start | bytes 786440 | tf_op jit(solution)/shard_map/ppermute | solution.py:20
  115.4 13.6 %copy-start.6 = (bf16[512,128]{1,0:T(8,128)(2,1)S(1)}, bf16[512,128]{1,0:T(8,128)(2,1)}, u32[]{:S(2)}) copy-start(bf16[512,128]{1,0:T(8,128)(2,1)} %param.11) | copy-start | bytes 393220
  115.4 13.6 %collective-permute-start.14 = (f32[512,128]{1,0:T(8,128)}, f32[512,128]{1,0:T(8,128)S(1)}, u32[]{:S(2)}, u32[]{:S(2)}) collective-permute-start(f32[512,128]{1,0:T(8,128)} %get-tuple-element.34), channel_id=1, source_target_pairs={{0,2},{1,3},{2,0},{3,1},{4,6},{5,7},{6,4},{7,5},{8,10},{9,11},{10,... | collective-permute-start | bytes 786440 | tf_op jit(solution)/shard_map/ppermute | solution.py:20
  129.1 7.3 %copy-start.5 = (bf16[512,128]{1,0:T(8,128)(2,1)}, bf16[512,128]{1,0:T(8,128)(2,1)S(1)}, u32[]{:S(2)}) copy-start(bf16[512,128]{1,0:T(8,128)(2,1)S(1)} %get-tuple-element.58.refs_0_) | copy-start | bytes 393220
  130.5 13.4 %collective-permute-start.21 = (bf16[512,128]{1,0:T(8,128)(2,1)S(1)}, bf16[512,128]{1,0:T(8,128)(2,1)S(1)}, u32[]{:S(2)}, u32[]{:S(2)}) collective-permute-start(bf16[512,128]{1,0:T(8,128)(2,1)S(1)} %get-tuple-element.58.refs_0_), channel_id=1, source_target_pairs={{0,3},{1,0},{2,1},{3,2},{4,7},{5,4},{6,5},{7,6},{8,11},{9,8},{10,9... | collective-permute-start | bytes 393224 | tf_op jit(solution)/shard_map/ppermute | solution.py:20
  131.5 12.5 %collective-permute-start.20 = (bf16[512,128]{1,0:T(8,128)(2,1)S(1)}, bf16[512,128]{1,0:T(8,128)(2,1)S(1)}, u32[]{:S(2)}, u32[]{:S(2)}) collective-permute-start(bf16[512,128]{1,0:T(8,128)(2,1)S(1)} %get-tuple-element.58.refs_0_), channel_id=1, source_target_pairs={{0,2},{1,3},{2,0},{3,1},{4,6},{5,7},{6,4},{7,5},{8,10},{9,11},{10,... | collective-permute-start | bytes 393224 | tf_op jit(solution)/shard_map/ppermute | solution.py:20
  132.9 11.1 %collective-permute-start.19 = (bf16[512,128]{1,0:T(8,128)(2,1)S(1)}, bf16[512,128]{1,0:T(8,128)(2,1)S(1)}, u32[]{:S(2)}, u32[]{:S(2)}) collective-permute-start(bf16[512,128]{1,0:T(8,128)(2,1)S(1)} %get-tuple-element.58.refs_0_), channel_id=1, source_target_pairs={{0,1},{1,2},{2,3},{3,0},{4,5},{5,6},{6,7},{7,4},{8,9},{9,10},{10,1... | collective-permute-start | bytes 393224 | tf_op jit(solution)/shard_map/ppermute | solution.py:20
  136.4 41.7 %all-to-all-start.4 = ((bf16[64,48,128]{2,1,0:T(8,128)(2,1)}), bf16[64,48,128]{2,1,0:T(8,128)(2,1)S(1)}, u32[]{:S(2)}, u32[]{:S(2)}) async-start(bf16[64,48,128]{2,1,0:T(8,128)(2,1)} %pad_maximum_fusion), calls=%async_computation.4 | async-start | bytes 1572864 | tf_op jit(solution)/shard_map/all_to_all | solution.py:24
  144.0 0.7 copy-start.7
  144.0 0.7 copy-start.8
  144.0 0.7 copy-start.9
  144.7 6.1 %copy-start.4 = (bf16[2,1024,512]{2,1,0:T(8,128)(2,1)S(1)}, bf16[2,1024,512]{2,1,0:T(8,128)(2,1)}, u32[]{:S(2)}) copy-start(bf16[2,1024,512]{2,1,0:T(8,128)(2,1)} %get-tuple-element.42) | copy-start | bytes 6291460
  150.8 5.1 %collective-permute-start.22 = (bf16[2048,256]{1,0:T(8,128)(2,1)}, bf16[2048,256]{1,0:T(8,128)(2,1)S(1)}, u32[]{:S(2)}, u32[]{:S(2)}) collective-permute-start(bf16[2048,256]{1,0:T(8,128)(2,1)} %get-tuple-element.44), channel_id=1, source_target_pairs={{0,128},{128,0},{1,129},{129,1},{2,130},{130,2},{3,131},{131,3},{4... | collective-permute-start | bytes 3145736 | tf_op jit(solution)/shard_map/ppermute | solution.py:20
  150.8 2.4 %copy-start.11 = (bf16[2,128,512]{2,1,0:T(8,128)(2,1)S(1)}, bf16[2,128,512]{2,1,0:T(8,128)(2,1)}, u32[]{:S(2)}) copy-start(bf16[2,128,512]{2,1,0:T(8,128)(2,1)} %get-tuple-element.46) | copy-start | bytes 786436
  150.8 5.1 %copy-start = (bf16[2,1024,512]{2,1,0:T(8,128)(2,1)S(1)}, bf16[2,1024,512]{2,1,0:T(8,128)(2,1)}, u32[]{:S(2)}) copy-start(bf16[2,1024,512]{2,1,0:T(8,128)(2,1)} %get-tuple-element.29) | copy-start | bytes 6291460
  150.8 5.1 %copy-start.1 = (bf16[512,512]{1,0:T(8,128)(2,1)S(1)}, bf16[512,512]{1,0:T(8,128)(2,1)}, u32[]{:S(2)}) copy-start(bf16[512,512]{1,0:T(8,128)(2,1)} %get-tuple-element.43.p_ref) | copy-start | bytes 1572868
  150.8 5.1 %copy-start.2 = (f32[2,128,512]{2,1,0:T(8,128)S(1)}, f32[2,128,512]{2,1,0:T(8,128)}, u32[]{:S(2)}) copy-start(f32[2,128,512]{2,1,0:T(8,128)} %get-tuple-element.45) | copy-start | bytes 1572868
  152.7 10.5 %collective-permute-start.27 = (bf16[2048,256]{1,0:T(8,128)(2,1)S(1)}, bf16[2048,256]{1,0:T(8,128)(2,1)S(1)}, u32[]{:S(2)}, u32[]{:S(2)}) collective-permute-start(bf16[2048,256]{1,0:T(8,128)(2,1)S(1)} %convolution_convert_fusion), channel_id=1, source_target_pairs={{0,128},{128,0},{1,129},{129,1},{2,130},{130,2},{3,131},{131,3},{4... | collective-permute-start | bytes 3145736 | tf_op jit(solution)/shard_map/ppermute | solution.py:20
  153.2 2.7 %collective-permute-start.23 = (bf16[2,128,512]{2,1,0:T(8,128)(2,1)S(1)}, bf16[2,128,512]{2,1,0:T(8,128)(2,1)S(1)}, u32[]{:S(2)}, u32[]{:S(2)}) collective-permute-start(bf16[2,128,512]{2,1,0:T(8,128)(2,1)S(1)} %copy-done.11), channel_id=1, source_target_pairs={{0,128},{128,0},{1,129},{129,1},{2,130},{130,2},{3,131},{131,3},{4... | collective-permute-start | bytes 786440 | tf_op jit(solution)/shard_map/ppermute | solution.py:20
  157.5 13.0 %collective-permute-start.24 = (bf16[8,72,256]{2,1,0:T(8,128)(2,1)S(1)}, bf16[8,72,256]{2,1,0:T(8,128)(2,1)S(1)}, u32[]{:S(2)}, u32[]{:S(2)}) collective-permute-start(bf16[8,72,256]{2,1,0:T(8,128)(2,1)S(1)} %get-tuple-element.48), channel_id=1, source_target_pairs={{0,4},{4,8},{8,12},{12,0},{1,5},{5,9},{9,13},{13,1},{2,6},{6,10},{... | collective-permute-start | bytes 884744 | tf_op jit(solution)/shard_map/ppermute | solution.py:20
  159.0 18.2 %collective-permute-start.25 = (bf16[8,72,256]{2,1,0:T(8,128)(2,1)S(1)}, bf16[8,72,256]{2,1,0:T(8,128)(2,1)S(1)}, u32[]{:S(2)}, u32[]{:S(2)}) collective-permute-start(bf16[8,72,256]{2,1,0:T(8,128)(2,1)S(1)} %get-tuple-element.49), channel_id=1, source_target_pairs={{0,8},{4,12},{8,0},{12,4},{1,9},{5,13},{9,1},{13,5},{2,10},{6,14},... | collective-permute-start | bytes 884744 | tf_op jit(solution)/shard_map/ppermute | solution.py:20
  161.7 15.5 %collective-permute-start.26 = (bf16[8,72,256]{2,1,0:T(8,128)(2,1)S(1)}, bf16[8,72,256]{2,1,0:T(8,128)(2,1)S(1)}, u32[]{:S(2)}, u32[]{:S(2)}) collective-permute-start(bf16[8,72,256]{2,1,0:T(8,128)(2,1)S(1)} %get-tuple-element.50), channel_id=1, source_target_pairs={{0,12},{4,0},{8,4},{12,8},{1,13},{5,1},{9,5},{13,9},{2,14},{6,2},{... | collective-permute-start | bytes 884744 | tf_op jit(solution)/shard_map/ppermute | solution.py:20
  164.7 19.5 %collective-permute-start.28 = (bf16[8,72,256]{2,1,0:T(8,128)(2,1)S(1)}, bf16[8,72,256]{2,1,0:T(8,128)(2,1)S(1)}, u32[]{:S(2)}, u32[]{:S(2)}) collective-permute-start(bf16[8,72,256]{2,1,0:T(8,128)(2,1)S(1)} %get-tuple-element.52), channel_id=1, source_target_pairs={{0,4},{4,8},{8,12},{12,0},{1,5},{5,9},{9,13},{13,1},{2,6},{6,10},{... | collective-permute-start | bytes 884744 | tf_op jit(solution)/shard_map/ppermute | solution.py:20
  165.4 24.2 %collective-permute-start.29 = (bf16[8,72,256]{2,1,0:T(8,128)(2,1)S(1)}, bf16[8,72,256]{2,1,0:T(8,128)(2,1)S(1)}, u32[]{:S(2)}, u32[]{:S(2)}) collective-permute-start(bf16[8,72,256]{2,1,0:T(8,128)(2,1)S(1)} %get-tuple-element.53), channel_id=1, source_target_pairs={{0,8},{4,12},{8,0},{12,4},{1,9},{5,13},{9,1},{13,5},{2,10},{6,14},... | collective-permute-start | bytes 884744 | tf_op jit(solution)/shard_map/ppermute | solution.py:20
  170.4 19.1 %collective-permute-start.30 = (bf16[8,72,256]{2,1,0:T(8,128)(2,1)S(1)}, bf16[8,72,256]{2,1,0:T(8,128)(2,1)S(1)}, u32[]{:S(2)}, u32[]{:S(2)}) collective-permute-start(bf16[8,72,256]{2,1,0:T(8,128)(2,1)S(1)} %get-tuple-element.54), channel_id=1, source_target_pairs={{0,12},{4,0},{8,4},{12,8},{1,13},{5,1},{9,5},{13,9},{2,14},{6,2},{... | collective-permute-start | bytes 884744 | tf_op jit(solution)/shard_map/ppermute | solution.py:20
  177.2 22.0 %copy-start.3 = (s32[1,3,8,128]{3,2,1,0:T(8,128)S(1)}, s32[1,3,8,128]{3,2,1,0:T(8,128)}, u32[]{:S(2)}) copy-start(s32[1,3,8,128]{3,2,1,0:T(8,128)} %copy.13) | copy-start | bytes 36868
  178.1 17.6 %all-to-all-start.2 = ((bf16[8,72,256]{2,1,0:T(8,128)(2,1)}), bf16[8,72,256]{2,1,0:T(8,128)(2,1)S(1)}, u32[]{:S(2)}, u32[]{:S(2)}) async-start(bf16[8,72,256]{2,1,0:T(8,128)(2,1)} %add_convert_fusion.1), calls=%async_computation.2 | async-start | bytes 589824 | tf_op jit(solution)/shard_map/all_to_all | solution.py:24
  195.7 14.2 %all-to-all-start.3 = ((bf16[8,72,256]{2,1,0:T(8,128)(2,1)}), bf16[8,72,256]{2,1,0:T(8,128)(2,1)S(1)}, u32[]{:S(2)}, u32[]{:S(2)}) async-start(bf16[8,72,256]{2,1,0:T(8,128)(2,1)} %add_convert_fusion), calls=%async_computation.3 | async-start | bytes 589824 | tf_op jit(solution)/shard_map/all_to_all | solution.py:24
